TPU v7x, 256 devices: a whole 4x4x8 slice. The times are simulated.
256 devices in a mesh: ctx: 8 (over z), head: 32 (over y, x, core).
Axes of the slice: x: 4, y: 4, z: 8, core: 2. Of those that a mesh axis runs over, the one named last changes fastest.
Arguments:
- x_stream: bfloat16 [32768, 16384], P('ctx', 'head'), may hold values from -6 to 6
- gate_z: bfloat16 [32768, 16384], P('ctx', 'head'), as said below
- state_proj: bfloat16 [32768, 2048], P('ctx', 'head'), may hold values from -5 to 5
- dt_raw: float32 [32768, 256], P('ctx', 'head'), as said below
- dt_bias: float32 [256], P('head'), may hold values from -3 to -1
- a_log: float32 [256], P('head'), as said below
- skip_d: float32 [256], P('head'), may hold values from 0.5 to 1.5
- conv_x: bfloat16 [4, 16384], P(None, 'head'), may hold values from -3 to 3
- conv_proj: bfloat16 [4, 2048], P(None, 'head'), may hold values from -3 to 3
- norm_gain: float32 [16384], P('head'), may hold values from 0.5 to 1.5
Outputs:
- mixer_out: bfloat16 [32768, 16384], P('ctx', 'head')
Inputs may be any that keep to these rules, and one draw needn't show every extreme that they name: gate_z is a bounded normal draw whose scale varies by column. dt_raw is bounded; its level varies over blocks of 4096 tokens and heads. a_log is finite.
All inputs are finite; a program needn't handle non-finite values.
Results may differ from a plain program's by a relative error of at most 0.0085.
Values may be sent and summed in bfloat16 or wider, within the bound.
No kernel may reach another device: no remote copies, remote signals or barrier semaphores. Data moves between devices by JAX's collectives and lax.ppermute only.
A program may use at most 128 MiB of HBM per device.

v0:
```python
import jax
import jax.numpy as jnp
from jax import lax
from jax.sharding import PartitionSpec as P

HEADS = 256
STATE = 128
GROUPS = 8
BLOCK_LEN = 128


def passed_along(x, axis, by):
    count = lax.axis_size(axis)
    pairs = [(i, i + by) for i in range(count) if 0 <= i + by < count]
    return lax.ppermute(x, axis, pairs)


def swapped(value, axis, bit):
    mask = 2**bit
    pairs = [(source, source ^ mask) for source in range(lax.axis_size(axis))]
    return lax.ppermute(value, axis, pairs)


def conv_silu(sequence, edge_rows, weight):
    kernel_len = weight.shape[0]
    length = sequence.shape[0]
    padded = jnp.concatenate([edge_rows, sequence], axis=0).astype(jnp.float32)
    weight_wide = weight.astype(jnp.float32)
    total = jnp.zeros(sequence.shape, jnp.float32)
    for offset in range(kernel_len):
        total = total + weight_wide[offset] * padded[offset : offset + length]
    return jax.nn.silu(total).astype(jnp.bfloat16)


def join_pair(mine, other, upper):
    return jnp.where(
        upper, jnp.concatenate([other, mine], axis=1), jnp.concatenate([mine, other], axis=1)
    )


def block_scan(x_blocks, b_blocks, c_blocks, step_size, log_decay):
    highest = lax.Precision.HIGHEST
    running = jnp.cumsum(jnp.swapaxes(log_decay, 1, 2), axis=2)
    step_heads = jnp.swapaxes(step_size, 1, 2)
    gram_matrix = jnp.einsum("ctn,csn->cts", c_blocks, b_blocks, preferred_element_type=jnp.float32)
    block_len = running.shape[2]
    row_ids = jnp.arange(block_len)[:, None]
    col_ids = jnp.arange(block_len)[None, :]
    causal_mask = row_ids >= col_ids
    log_gaps = running[:, :, :, None] - running[:, :, None, :]
    decay_matrix = jnp.where(causal_mask, jnp.exp(jnp.where(causal_mask, log_gaps, 0.0)), 0.0)
    weights = (gram_matrix[:, None] * decay_matrix * step_heads[:, :, None, :]).astype(jnp.bfloat16)
    intra_out = jnp.einsum("chts,cshp->cthp", weights, x_blocks, preferred_element_type=jnp.float32)
    block_total = running[:, :, -1]
    state_weight = jnp.exp(block_total[:, :, None] - running) * step_heads
    weighted = (x_blocks.astype(jnp.float32) * jnp.swapaxes(state_weight, 1, 2)[..., None]).astype(
        jnp.bfloat16
    )
    states = jnp.einsum("cshp,csn->chpn", weighted, b_blocks, preferred_element_type=jnp.float32)

    def advance(state_now, inputs):
        factor, addend = inputs
        return (factor[:, None, None] * state_now + addend, state_now)

    empty_state = jnp.zeros(states.shape[1:], jnp.float32)
    final_state, entering = lax.scan(advance, empty_state, (jnp.exp(block_total), states))
    c_wide = c_blocks.astype(jnp.float32)
    inter_out = jnp.exp(jnp.swapaxes(running, 1, 2))[..., None] * jnp.einsum(
        "ctn,chpn->cthp", c_wide, entering, precision=highest
    )
    return (intra_out + inter_out, final_state, block_total, running)


def on_device(
    x_stream, gate_z, state_proj, dt_raw, dt_bias, a_log, skip_d, conv_x, conv_proj, norm_gain
):
    highest = lax.Precision.HIGHEST
    kernel_len = conv_x.shape[0]
    tokens_here = x_stream.shape[0]
    heads_here = dt_raw.shape[1]
    channels = x_stream.shape[1]
    head_size = channels // heads_here
    head_pos = lax.axis_index("head")
    group_devices = lax.axis_size("head") // GROUPS
    group_levels = group_devices.bit_length() - 1
    edge_start = tokens_here - kernel_len + 1
    edge_rows = passed_along((x_stream[edge_start:], state_proj[edge_start:]), "ctx", 1)
    x_conv = conv_silu(x_stream, edge_rows[0], conv_x)
    own_cols = conv_silu(state_proj, edge_rows[1], conv_proj)
    for level in range(group_levels):
        upper = head_pos >> level & 1 == 1
        other_cols = swapped(own_cols, "head", level)
        own_cols = join_pair(own_cols, other_cols, upper)
    blocks = tokens_here // BLOCK_LEN
    b_blocks = own_cols[:, :STATE].reshape(blocks, BLOCK_LEN, STATE)
    c_blocks = own_cols[:, STATE:].reshape(blocks, BLOCK_LEN, STATE)
    step_size = jax.nn.softplus(dt_raw + dt_bias)
    log_decay = step_size * -jnp.exp(a_log)
    local_out, final_state, block_total, running = block_scan(
        x_conv.reshape(blocks, BLOCK_LEN, heads_here, head_size),
        b_blocks,
        c_blocks,
        step_size.reshape(blocks, BLOCK_LEN, heads_here),
        log_decay.reshape(blocks, BLOCK_LEN, heads_here),
    )
    block_log = jnp.sum(block_total, axis=0)
    block_logs = lax.all_gather(block_log[None], "ctx", axis=0, tiled=True)
    ctx_pos = lax.axis_index("ctx")
    count = block_logs.shape[0]
    indices = jnp.arange(count)
    between = (indices[None, :] > indices[:, None]) & (indices[None, :] < ctx_pos)
    span_logs = jnp.dot(between.astype(jnp.float32), block_logs, precision=highest)
    weight_all = jnp.where(indices[:, None] < ctx_pos, jnp.exp(span_logs), 0.0)
    entering = jnp.zeros(final_state.shape, jnp.float32) + jnp.einsum(
        "rh,rhpn->hpn",
        weight_all,
        lax.all_gather(final_state[None].astype(jnp.bfloat16), "ctx", axis=0, tiled=True).astype(
            jnp.float32
        ),
        precision=highest,
    )
    block_start = jnp.cumsum(block_total, axis=0) - block_total
    carried_out = jnp.exp(jnp.swapaxes(running + block_start[:, :, None], 1, 2))[
        ..., None
    ] * jnp.einsum("ctn,hpn->cthp", c_blocks.astype(jnp.float32), entering, precision=highest)
    mixed = (local_out + carried_out).reshape(tokens_here, heads_here, head_size)
    mixed = mixed + skip_d[None, :, None] * x_conv.astype(jnp.float32).reshape(
        tokens_here, heads_here, head_size
    )
    gated_out = mixed.reshape(tokens_here, channels) * jax.nn.silu(gate_z.astype(jnp.float32))
    group_total = jnp.sum(gated_out * gated_out, axis=1)
    for level in range(group_levels):
        group_total = group_total + swapped(group_total, "head", level)
    mean_square = group_total / (HEADS // GROUPS * head_size)
    normed = gated_out * lax.rsqrt(mean_square + 1e-05)[:, None] * norm_gain[None, :]
    return normed.astype(jnp.bfloat16)


def solution(mesh):
    return jax.shard_map(
        on_device,
        mesh=mesh,
        in_specs=(
            P("ctx", "head"),
            P("ctx", "head"),
            P("ctx", "head"),
            P("ctx", "head"),
            P("head"),
            P("head"),
            P("head"),
            P(None, "head"),
            P(None, "head"),
            P("head"),
        ),
        out_specs=P("ctx", "head"),
        check_vma=False,
    )
```

profile of v0, /device:TPU:1, one launch (start us, length us, event | category | flops | bytes accessed | tf_op | source)
XLA Modules:
  0.0 275.4 jit_solution(6585836205751092210)
XLA Ops:
  7.5 4.4 %collective-permute-start.1 = (bf16[3,64]{0,1:T(8,128)(2,1)S(1)}, bf16[3,64]{0,1:T(8,128)(2,1)S(1)}, u32[]{:S(2)}, u32[]{:S(2)}) collective-permute-start(bf16[3,64]{0,1:T(8,128)(2,1)S(1)} %slice.73), channel_id=1, source_target_pairs={{0,32},{32,64},{64,96},{96,128},{128,160},{160,192},{192,224},{1,3... | collective-permute-start | bytes 1160 | tf_op jit(solution)/shard_map/ppermute | solution.py:15
  12.7 3.6 %collective-permute-start = (bf16[3,512]{0,1:T(8,128)(2,1)S(1)}, bf16[3,512]{0,1:T(8,128)(2,1)S(1)}, u32[]{:S(2)}, u32[]{:S(2)}) collective-permute-start(bf16[3,512]{0,1:T(8,128)(2,1)S(1)} %copy.30), channel_id=1, source_target_pairs={{0,32},{32,64},{64,96},{96,128},{128,160},{160,192},{192,224},{1,3... | collective-permute-start | bytes 9224 | tf_op jit(solution)/shard_map/ppermute | solution.py:15
  16.3 6.5 %copy.31 = bf16[4096,512]{0,1:T(8,128)(2,1)} copy(bf16[4096,512]{1,0:T(8,128)(2,1)} %param.12) | data formatting | bytes 8388608 | tf_op args[0]
  23.6 9.0 %reduce_window_sum.22 = f32[32,8,128]{2,1,0:T(8,128)S(1)} reduce-window(f32[32,8,128]{2,1,0:T(8,128)S(1)} %get-tuple-element.77, f32[]{:T(128)} %constant.42.clone.1), window={size=1x1x128 pad=0_0x0_0x127_0}, to_apply=%region_0.1 | reduce-window | flops 4161536 | bytes 262148 | tf_op jit(solution)/shard_map/jit(cumsum)/reduce_window_sum | solution.py:43
  35.8 13.5 %all-reduce = f32[64]{0:T(128)S(1)} all-reduce(f32[64]{0:T(128)S(1)} %dynamic-update-slice), channel_id=2, replica_groups=mesh['ctx'=8,'head'=32] {'ctx'}, use_global_device_ids=true, to_apply=%add | all-reduce | flops 64 | bytes 512
  51.8 6.3 %copy.43 = bf16[4096,512]{0,1:T(8,128)(2,1)} copy(bf16[4096,512]{1,0:T(8,128)(2,1)} %param.13) | data formatting | bytes 8388608 | tf_op args[1]
  60.0 4.8 %collective-permute-start.2 = (bf16[4096,64]{0,1:T(8,128)(2,1)S(1)}, bf16[4096,64]{0,1:T(8,128)(2,1)S(1)}, u32[]{:S(2)}, u32[]{:S(2)}) collective-permute-start(bf16[4096,64]{0,1:T(8,128)(2,1)S(1)} %multiply_convert_fusion.5), channel_id=1, source_target_pairs={{0,1},{1,0},{2,3},{3,2},{4,5},{5,4},{6,7},{7,6},{8,9},{9,8},{10,11... | collective-permute-start | bytes 1572872 | tf_op jit(solution)/shard_map/ppermute | solution.py:21
  64.8 2.5 maximum_convert_fusion
  67.6 1.5 collective-permute-start.3
  69.1 8.7 %fusion.46 = bf16[64,8,32,128]{3,1,2,0:T(8,128)(2,1)} fusion(f32[4099,512]{0,1:T(8,128)S(1)} %maximum_convert_fusion, f32[512]{0:T(512)S(1)} %bitcast.109, f32[512]{0:T(512)S(1)} %bitcast.107, f32[512]{0:T(512)S(1)} %bitcast.105, f32[512]{0:T(512)S(1)} %bitcast.103), kind=kLoop, calls=%fused_computation.78 | loop fusion | flops 25165824 | bytes 37756928
  77.7 3.4 %copy.52 = bf16[64,8,32,128]{3,2,1,0:T(8,128)(2,1)S(1)} copy(bf16[64,8,32,128]{3,1,2,0:T(8,128)(2,1)} %fusion.46) | data formatting | bytes 8388608
  81.2 3.2 %multiply_convert_fusion.3 = bf16[32,128,8,64]{1,0,3,2:T(8,128)(2,1)} fusion(bf16[32,128,8,64]{1,0,3,2:T(8,128)(2,1)S(1)} %bitcast.95, f32[32,128,8]{1,0,2:T(8,128)S(1)} %copy.37), kind=kLoop, calls=%fused_computation.24 | loop fusion | flops 6291456 | bytes 8519680 | tf_op jit(solution)/shard_map/convert_element_type | solution.py:56
  84.4 7.2 %collective-permute-done.3 = bf16[4096,128]{0,1:T(8,128)(2,1)S(1)} collective-permute-done((bf16[4096,128]{0,1:T(8,128)(2,1)S(1)}, bf16[4096,128]{0,1:T(8,128)(2,1)S(1)}, u32[]{:S(2)}, u32[]{:S(2)}) %collective-permute-start.3) | collective-permute-done | bytes 1048608 | tf_op jit(solution)/shard_map/ppermute | solution.py:21
  92.9 7.6 %fusion.16 = f32[32,8,64,128]{3,2,1,0:T(8,128)} fusion(bf16[32,128,128,1]{2,1,3,0:T(8,128)(2,1)S(1)} %bitcast.97, bf16[32,128,8,64]{1,0,3,2:T(8,128)(2,1)} %multiply_convert_fusion.3), kind=kOutput, calls=%fused_computation.33 | convolution fusion | flops 536870912 | bytes 13631488 | tf_op jit(solution)/shard_map/cshp,csn->chpn/dot_general | solution.py:59
  100.6 79.2 %while.13 = (s32[]{:T(128)}, f32[8,64,128]{2,1,0:T(8,128)S(1)}, f32[32,8,64,128]{3,2,1,0:T(8,128)}, f32[32,8]{1,0:T(8,128)}, f32[32,8,64,128]{3,2,1,0:T(8,128)}, /*index=5*/s32[]{:T(128)}, s32[]{:T(128)}) while((s32[]{:T(128)}, f32[8,64,128]{2,1,0:T(8,128)S(1)}, f32[32,8,64,128]{3,2,1,0:T(8,128)}, f32[32,8]{1,0:T(8,128)}, ...), condition=%wide.region_2.3_spmd.clone, body=%wide.region_1.2_spmd.clone.sunk | while | flops 262147 | bytes 1311424 | solution.py:66
  102.0 1.0 bitcast_add_fusion.4
  104.4 1.0 bitcast_add_fusion.4
  114.4 1.0 bitcast_add_fusion.4
  116.8 1.0 bitcast_add_fusion.4
  119.3 1.0 bitcast_add_fusion.4
  121.8 1.0 bitcast_add_fusion.4
  131.7 1.0 bitcast_add_fusion.4
  134.2 1.0 bitcast_add_fusion.4
  136.6 1.0 bitcast_add_fusion.4
  139.1 1.0 bitcast_add_fusion.4
  141.6 1.0 bitcast_add_fusion.4
  144.1 1.0 bitcast_add_fusion.4
  151.5 1.0 bitcast_add_fusion.4
  153.9 1.0 bitcast_add_fusion.4
  156.4 1.0 bitcast_add_fusion.4
  158.9 1.0 bitcast_add_fusion.4
  161.3 1.0 bitcast_add_fusion.4
  163.8 1.0 bitcast_add_fusion.4
  166.3 1.0 bitcast_add_fusion.4
  173.7 1.0 bitcast_add_fusion.4
  176.2 1.0 bitcast_add_fusion.4
  182.0 8.4 %fusion.36 = f32[32,128,8,64]{1,3,2,0:T(8,128)} fusion(bf16[32,128,128,1]{2,1,3,0:T(8,128)(2,1)S(1)} %bitcast.93, f32[32,8,64,128]{3,2,1,0:T(8,128)} %get-tuple-element.33), kind=kOutput, calls=%fused_computation.77 | convolution fusion | flops 3221225472 | bytes 17825792 | tf_op jit(solution)/shard_map/ctn,chpn->cthp/dot_general | solution.py:68
  190.4 10.7 %fusion.1 = f32[32,8,64,128]{3,2,1,0:T(8,128)} fusion(f32[32,8,128]{2,1,0:T(8,128)S(1)} %copy-done.9, f32[32,8,128]{2,1,0:T(8,128)S(1)} %reduce_window_sum.22, f32[32,128,128]{2,1,0:T(8,128)S(1)} %fusion.35, pred[128,128]{1,0:T(8,128)(4,1)S(1)} %copy-done.11, bf16[32,128,8,64]{1,0,3,2:T(8,128)(2,1)S(1)} %bitcast.96), kind=kOutput, calls=%fused_computation.7 | convolution fusion | flops 562036736 | bytes 14958592 | tf_op jit(solution)/shard_map/chts,cshp->cthp/dot_general | solution.py:53
  201.1 15.5 %all-gather.4.cloned.1.call-done = bf16[64,64,128]{2,1,0:T(8,128)(2,1)} async-done(((bf16[8,64,128]{2,1,0:T(8,128)(2,1)}), bf16[64,64,128]{2,1,0:T(8,128)(2,1)}) %all-gather.4.cloned.1.call-update) | async-done | bytes 1048592 | tf_op jit(solution)/shard_map/all_gather | solution.py:117
  216.6 2.5 fusion.24
  219.1 8.3 %fusion.9 = f32[32,128,8,64]{1,3,2,0:T(8,128)S(1)} fusion(f32[32,8,64,128]{3,2,1,0:T(8,128)} %fusion.1, f32[32,128,8,64]{1,3,2,0:T(8,128)} %fusion.36, f32[32,128,8]{1,2,0:T(8,128)S(1)} %copy-done.7, f32[32,128,8]{1,2,0:T(8,128)S(1)} %copy-done.6, bf16[32,128,128,1]{2,1,3,0:T(8,128)(2,1)S(1)} %bitcast.94, f32[8,64,128,1]{2,1,0,3:T(8,128)S(1)} %bitcast.99), kind=kOutput, calls=%fused_computation.21 | convolution fusion | flops 3229614080 | bytes 26738688 | tf_op jit(solution)/shard_map/ctn,hpn->cthp/dot_general | solution.py:125
  227.5 8.0 %copy.42 = f32[32,128,8,64]{1,0,3,2:T(8,128)} copy(f32[32,128,8,64]{1,3,2,0:T(8,128)S(1)} %fusion.9) | data formatting | bytes 16777216 | tf_op jit(solution)/shard_map/add | solution.py:126
  235.5 13.9 %multiply_reduce_fusion = (f32[4096]{0:T(1024)S(1)}, f32[4096,512]{0,1:T(8,128)S(1)}) fusion(bf16[4096,512]{0,1:T(8,128)(2,1)S(1)} %copy-done.4, f32[512]{0:T(512)S(1)} %copy-done.13, f32[64,8,32,128]{3,2,1,0:T(8,128)} %bitcast.91, f32[4099,512]{0,1:T(8,128)S(1)} %bitcast.90, f32[512]{0:T(512)S(1)} %bitcast.110, f32[512]{0:T(512)S(1)} %bitcast.108, ...), kind=kLoop, calls=%fused_computation.23 | loop fusion | flops 48230400 | bytes 54552576 | tf_op jit(solution)/shard_map/reduce_sum | solution.py:131
  249.4 5.9 %collective-permute-start.4 = (f32[4096]{0:T(1024)S(1)}, f32[4096]{0:T(1024)S(1)}, u32[]{:S(2)}, u32[]{:S(2)}) collective-permute-start(f32[4096]{0:T(1024)S(1)} %get-tuple-element.73), channel_id=1, source_target_pairs={{0,1},{1,0},{2,3},{3,2},{4,5},{5,4},{6,7},{7,6},{8,9},{9,8},{10,11... | collective-permute-start | bytes 49160 | tf_op jit(solution)/shard_map/ppermute | solution.py:21
  256.2 1.3 collective-permute-start.5
  257.4 1.3 collective-permute-done.5
  258.8 3.3 %multiply_convert_fusion.2 = bf16[4096,512]{0,1:T(8,128)(2,1)} fusion(f32[4096,512]{0,1:T(8,128)S(1)} %get-tuple-element.74, f32[512]{0:T(512)S(1)} %copy-done.15, f32[4096]{0:T(1024)S(1)} %add_rsqrt_fusion), kind=kLoop, calls=%fused_computation.22 | loop fusion | flops 6291456 | bytes 12601344 | tf_op jit(solution)/shard_map/convert_element_type | solution.py:136
  262.1 6.4 %copy.44 = bf16[4096,512]{1,0:T(8,128)(2,1)} copy(bf16[4096,512]{0,1:T(8,128)(2,1)} %multiply_convert_fusion.2) | data formatting | bytes 8388608 | tf_op jit(solution)/shard_map/convert_element_type | solution.py:136
  (169 shorter events, 70.7 us)
Async XLA Ops:
  6.5 27.8 %copy-start.19 = (u32[256]{0:T(256)S(1)}, u32[256]{0:T(256)}, u32[]{:S(2)}) copy-start(u32[256]{0:T(256)} %constant.53) | copy-start | bytes 3076
  6.5 16.3 %copy-start.18 = (f32[8]{0:T(128)S(1)}, f32[8]{0:T(128)}, u32[]{:S(2)}) copy-start(f32[8]{0:T(128)} %param.17) | copy-start | bytes 100
  6.5 16.3 %copy-start.8 = (f32[4096,8]{0,1:T(8,128)S(1)}, f32[4096,8]{0,1:T(8,128)}, u32[]{:S(2)}) copy-start(f32[4096,8]{0,1:T(8,128)} %param.15) | copy-start | bytes 393220
  6.5 16.3 %copy-start.14 = (f32[8]{0:T(128)S(1)}, f32[8]{0:T(128)}, u32[]{:S(2)}) copy-start(f32[8]{0:T(128)} %param.16) | copy-start | bytes 100
  6.5 27.5 %copy-start.16 = (bf16[4,64]{1,0:T(4,128)(2,1)S(1)}, bf16[4,64]{1,0:T(4,128)(2,1)}, u32[]{:S(2)}) copy-start(bf16[4,64]{1,0:T(4,128)(2,1)} %param.20) | copy-start | bytes 1540
  6.5 27.5 %copy-start.12 = (bf16[4,512]{1,0:T(4,128)(2,1)S(1)}, bf16[4,512]{1,0:T(4,128)(2,1)}, u32[]{:S(2)}) copy-start(bf16[4,512]{1,0:T(4,128)(2,1)} %param.19) | copy-start | bytes 12292
  6.6 210.0 %all-gather.4.cloned.1.call-start = ((), (), s32[]{:S(2)}) async-start(), calls=%async_computation | async-start | bytes 1179648 | tf_op jit(solution)/shard_map/all_gather | solution.py:117
  7.5 51.4 %collective-permute-start.1 = (bf16[3,64]{0,1:T(8,128)(2,1)S(1)}, bf16[3,64]{0,1:T(8,128)(2,1)S(1)}, u32[]{:S(2)}, u32[]{:S(2)}) collective-permute-start(bf16[3,64]{0,1:T(8,128)(2,1)S(1)} %slice.73), channel_id=1, source_target_pairs={{0,32},{32,64},{64,96},{96,128},{128,160},{160,192},{192,224},{1,3... | collective-permute-start | bytes 1160 | tf_op jit(solution)/shard_map/ppermute | solution.py:15
  12.7 52.1 %collective-permute-start = (bf16[3,512]{0,1:T(8,128)(2,1)S(1)}, bf16[3,512]{0,1:T(8,128)(2,1)S(1)}, u32[]{:S(2)}, u32[]{:S(2)}) collective-permute-start(bf16[3,512]{0,1:T(8,128)(2,1)S(1)} %copy.30), channel_id=1, source_target_pairs={{0,32},{32,64},{64,96},{96,128},{128,160},{160,192},{192,224},{1,3... | collective-permute-start | bytes 9224 | tf_op jit(solution)/shard_map/ppermute | solution.py:15
  16.3 41.9 %copy-start.17 = (f32[8]{0:T(128)S(1)}, f32[8]{0:T(128)}, u32[]{:S(2)}) copy-start(f32[8]{0:T(128)} %param.18) | copy-start | bytes 100
  16.3 42.5 %copy-start.5 = (bf16[4096,64]{0,1:T(8,128)(2,1)S(1)}, bf16[4096,64]{0,1:T(8,128)(2,1)}, u32[]{:S(2)}) copy-start(bf16[4096,64]{0,1:T(8,128)(2,1)} %param.14) | copy-start | bytes 1572868
  58.8 6.0 %copy-start.1 = (bf16[4096,512]{0,1:T(8,128)(2,1)S(1)}, bf16[4096,512]{0,1:T(8,128)(2,1)}, u32[]{:S(2)}) copy-start(bf16[4096,512]{0,1:T(8,128)(2,1)} %copy.31) | copy-start | bytes 12582916
  60.0 7.4 %collective-permute-start.2 = (bf16[4096,64]{0,1:T(8,128)(2,1)S(1)}, bf16[4096,64]{0,1:T(8,128)(2,1)S(1)}, u32[]{:S(2)}, u32[]{:S(2)}) collective-permute-start(bf16[4096,64]{0,1:T(8,128)(2,1)S(1)} %multiply_convert_fusion.5), channel_id=1, source_target_pairs={{0,1},{1,0},{2,3},{3,2},{4,5},{5,4},{6,7},{7,6},{8,9},{9,8},{10,11... | collective-permute-start | bytes 1572872 | tf_op jit(solution)/shard_map/ppermute | solution.py:21
  67.3 10.4 %copy-start = (f32[4099,512]{0,1:T(8,128)}, f32[4099,512]{0,1:T(8,128)S(1)}, u32[]{:S(2)}) copy-start(f32[4099,512]{0,1:T(8,128)S(1)} %maximum_convert_fusion) | copy-start | bytes 25184260
  67.6 24.0 %collective-permute-start.3 = (bf16[4096,128]{0,1:T(8,128)(2,1)S(1)}, bf16[4096,128]{0,1:T(8,128)(2,1)S(1)}, u32[]{:S(2)}, u32[]{:S(2)}) collective-permute-start(bf16[4096,128]{0,1:T(8,128)(2,1)S(1)} %maximum_select_fusion.1), channel_id=1, source_target_pairs={{0,2},{1,3},{2,0},{3,1},{4,6},{5,7},{6,4},{7,5},{8,10},{9,11},{10,... | collective-permute-start | bytes 3145736 | tf_op jit(solution)/shard_map/ppermute | solution.py:21
  81.2 11.1 %copy-start.2 = (bf16[64,8,32,128]{3,2,1,0:T(8,128)(2,1)}, bf16[64,8,32,128]{3,2,1,0:T(8,128)(2,1)S(1)}, u32[]{:S(2)}) copy-start(bf16[64,8,32,128]{3,2,1,0:T(8,128)(2,1)S(1)} %copy.52) | copy-start | bytes 12582916
  181.9 8.4 %copy-start.3 = (bf16[64,8,32,128]{3,2,1,0:T(8,128)(2,1)S(1)}, bf16[64,8,32,128]{3,2,1,0:T(8,128)(2,1)}, u32[]{:S(2)}) copy-start(bf16[64,8,32,128]{3,2,1,0:T(8,128)(2,1)} %copy-done.2) | copy-start | bytes 12582916
  182.0 8.4 %copy-start.9 = (f32[32,8,128]{2,1,0:T(8,128)S(1)}, f32[32,8,128]{2,1,0:T(8,128)}, u32[]{:S(2)}) copy-start(f32[32,8,128]{2,1,0:T(8,128)} %get-tuple-element.78) | copy-start | bytes 393220
  182.0 8.4 %copy-start.11 = (pred[128,128]{1,0:T(8,128)(4,1)S(1)}, pred[128,128]{1,0:T(8,128)(4,1)}, u32[]{:S(2)}) copy-start(pred[128,128]{1,0:T(8,128)(4,1)} %iota_compare_fusion) | copy-start | bytes 49156
  190.4 26.2 %copy-start.10 = (f32[8,8,1,1]{0,2,3,1:T(1,128)S(1)}, f32[8,8,1,1]{0,2,3,1:T(1,128)}, u32[]{:S(2)}) copy-start(f32[8,8,1,1]{0,2,3,1:T(1,128)} %copy.47) | copy-start | bytes 772
  190.4 28.7 %copy-start.6 = (f32[32,128,8]{1,2,0:T(8,128)S(1)}, f32[32,128,8]{1,2,0:T(8,128)}, u32[]{:S(2)}) copy-start(f32[32,128,8]{1,2,0:T(8,128)} %get-tuple-element.81) | copy-start | bytes 393220
  190.4 28.7 %copy-start.7 = (f32[32,128,8]{1,2,0:T(8,128)S(1)}, f32[32,128,8]{1,2,0:T(8,128)}, u32[]{:S(2)}) copy-start(f32[32,128,8]{1,2,0:T(8,128)} %get-tuple-element.82) | copy-start | bytes 393220
  219.1 16.4 %slice-start = ((s8[8650752]{0:T(1024)(128)(4,1)}), s8[4194304]{0:T(1024)(128)(4,1)S(1)}, s32[]{:S(2)}) async-start(s8[8650752]{0:T(1024)(128)(4,1)} %bitcast.89), calls=%async_computation.1 | async-start | bytes 8388608
  219.1 16.4 %slice-start.1 = ((s8[8650752]{0:T(1024)(128)(4,1)}), s8[4194304]{0:T(1024)(128)(4,1)S(1)}, s32[]{:S(2)}) async-start(s8[8650752]{0:T(1024)(128)(4,1)} %bitcast.89), calls=%async_computation.2 | async-start | bytes 8388608
  227.4 8.1 %slice-start.2 = ((s8[8650752]{0:T(1024)(128)(4,1)}), s8[262144]{0:T(1024)(128)(4,1)S(1)}, s32[]{:S(2)}) async-start(s8[8650752]{0:T(1024)(128)(4,1)} %bitcast.89), calls=%async_computation.3 | async-start | bytes 524288
  227.4 8.1 %copy-start.4 = (bf16[4096,512]{0,1:T(8,128)(2,1)S(1)}, bf16[4096,512]{0,1:T(8,128)(2,1)}, u32[]{:S(2)}) copy-start(bf16[4096,512]{0,1:T(8,128)(2,1)} %copy.43) | copy-start | bytes 12582916
  227.4 8.0 %copy-start.13 = (f32[512]{0:T(512)S(1)}, f32[512]{0:T(512)}, u32[]{:S(2)}) copy-start(f32[512]{0:T(512)} %mul.228) | copy-start | bytes 6148
  235.5 23.3 %copy-start.15 = (f32[512]{0:T(512)S(1)}, f32[512]{0:T(512)}, u32[]{:S(2)}) copy-start(f32[512]{0:T(512)} %param.21) | copy-start | bytes 6148
  249.4 6.7 %collective-permute-start.4 = (f32[4096]{0:T(1024)S(1)}, f32[4096]{0:T(1024)S(1)}, u32[]{:S(2)}, u32[]{:S(2)}) collective-permute-start(f32[4096]{0:T(1024)S(1)} %get-tuple-element.73), channel_id=1, source_target_pairs={{0,1},{1,0},{2,3},{3,2},{4,5},{5,4},{6,7},{7,6},{8,9},{9,8},{10,11... | collective-permute-start | bytes 49160 | tf_op jit(solution)/shard_map/ppermute | solution.py:21
  256.2 2.6 collective-permute-start.5
Sparse Core Ops, SparseCore 0:
  181.2 35.2 all-gather.3
where the time goes:
time: 278 us; the launch traced here: 275 us
  other arithmetic  103 us (37%)
  local copies, waits for them, and re-layouts  59.4 us (21%)
  matrix products  38.5 us (14%)
  waiting for transfers between devices  24.9 us (9%)
  starting transfers between devices  21.4 us (8%)
  between operations  14.5 us (5%)
  blocking collectives  13.5 us (5%)
    add x32, other arithmetic, advance(): return (factor[:, None, None] * state_now + addend, state_now)  33.3 us
    dynamic_update_slice x32, other arithmetic, block_scan(): lax.scan(advance, empty_state, (jnp.exp(block_total), states))  23.4 us
    mul x32, local copies, waits for them, and re-layouts, advance(): return (factor[:, None, None] * state_now + addend, state_now)  21.8 us
    unnamed x53, local copies, waits for them, and re-layouts  17.8 us
    all_gather x1, waiting for transfers between devices, on_device(): lax.all_gather(final_state[None].astype(jnp.bfloat16), 'ctx', axis=0, til...  15.5 us
    reduce_sum x1, other arithmetic, on_device(): group_total = jnp.sum(gated_out * gated_out, axis=1)  13.9 us
    ppermute x4, starting transfers between devices, swapped(): return lax.ppermute(value, axis, pairs)  13.5 us
    unnamed x1, blocking collectives  13.5 us
  transfers between devices with their start and end apart: 7, of which 4 were waited for; matrix products, arithmetic and copies ran while one was open for 25% of the time, Pallas kernels for 0%

commit v1 on v0

v1 whole, which is shorter than its diff:
```python
import jax
import jax.numpy as jnp
from jax import lax
from jax.experimental import pallas as pl
from jax.experimental.pallas import tpu as pltpu
from jax.sharding import PartitionSpec as P

HEADS = 256
STATE = 128
GROUPS = 8
BLK = 128
LOG2E = 1.4426950408889634
F32 = jnp.float32
BF16 = jnp.bfloat16
HIGH = lax.Precision.HIGHEST
VMEM_CAP = 8 * 1024 * 1024
LOCAL_UNROLL = 8
CARRY_UNROLL = 8
CONV_UNROLL = (5, 8)
STATE_UNROLL = 8


def shifted(x, axis, by):
    count = lax.axis_size(axis)
    pairs = [(i, i + by) for i in range(count) if 0 <= i + by < count]
    return lax.ppermute(x, axis, pairs)


def rotated(x, axis, by):
    count = lax.axis_size(axis)
    return lax.ppermute(x, axis, [(i, (i + by) % count) for i in range(count)])


def swapped(value, axis, mask):
    return lax.ppermute(value, axis, [(i, i ^ mask) for i in range(lax.axis_size(axis))])


def after(value, *others):
    return lax.optimization_barrier((value,) + others)[0]


def params():
    return pltpu.CompilerParams(vmem_limit_bytes=VMEM_CAP)


def cost(flops, size, trans=0):
    return pl.CostEstimate(flops=flops, bytes_accessed=size, transcendentals=trans)


def specs(count, scalars=0):
    smem = pl.BlockSpec(memory_space=pltpu.SMEM)
    return [smem] * scalars + [pl.BlockSpec(memory_space=pltpu.VMEM)] * (count - scalars)


def half_silu(h):
    return h + h * jnp.tanh(h)


def iota(shape, dim):
    return lax.broadcasted_iota(jnp.int32, shape, dim)


def block_at(i):
    return pl.ds(pl.multiple_of(i * BLK, BLK), BLK)


def head_spread(heads, chans):
    return (iota((heads, chans), 1) // (chans // heads) == iota((heads, chans), 0)).astype(BF16)


def upright(row):
    count = row.shape[1]
    eye = iota((count, count), 0) == iota((count, count), 1)
    return jnp.sum(jnp.where(eye, row, 0.0), axis=1, keepdims=True)


def tails_kernel(x_ref, p_ref, w_ref, o_ref):
    half, chans = p_ref.shape[0], x_ref.shape[1]
    o_ref[0:half, :] = p_ref[...]
    for at in range(chans // BLK):
        lo = half + 16 * at
        o_ref[lo : lo + 16, :] = x_ref[:, at * BLK : (at + 1) * BLK]
    at = half + 16 * (chans // BLK)
    o_ref[at : at + 16, :] = jnp.zeros((16, BLK), BF16)
    o_ref[at : at + 4, 0:half] = w_ref[...]


def tails(x, proj_t, taps):
    tokens, chans = x.shape
    half = proj_t.shape[0]
    rows = half + 16 * (chans // BLK) + 16
    return pl.pallas_call(
        tails_kernel,
        grid=(1,),
        in_specs=[
            pl.BlockSpec((16, chans), lambda i: (tokens // 16 - 1, 0)),
            pl.BlockSpec((half, BLK), lambda i: (0, tokens // BLK - 1)),
            pl.BlockSpec(taps.shape, lambda i: (0, 0)),
        ],
        out_specs=pl.BlockSpec((rows, BLK), lambda i: (0, 0)),
        out_shape=jax.ShapeDtypeStruct((rows, BLK), BF16),
        compiler_params=pltpu.CompilerParams(vmem_limit_bytes=60 * 1024 * 1024),
        name="tails",
    )(x, proj_t, taps)


def proj_conv_kernel(flag_ref, p_ref, halo_ref, o_ref):
    rows, tokens = p_ref.shape
    group = 16
    lane = iota((group, BLK), 1)
    at = halo_ref.shape[0] - 16
    weights = jnp.transpose(0.5 * halo_ref[at : at + 16, :].astype(F32)[0:8])
    for lo in range(0, rows, group):
        span = slice(lo, lo + group)
        taps = [jnp.broadcast_to(weights[span, k : k + 1], (group, BLK)) for k in range(4)]
        halo = jnp.where(flag_ref[1] == 0, 0.0, halo_ref[span, :].astype(F32))
        prev = [pltpu.roll(halo, k, 1) for k in (1, 2, 3)]
        for i in range(tokens // BLK):
            cur = p_ref[span, i * BLK : (i + 1) * BLK].astype(F32)
            now = [pltpu.roll(cur, k, 1) for k in (1, 2, 3)]
            h = taps[3] * cur
            for k in (1, 2, 3):
                h = h + taps[3 - k] * jnp.where(lane < k, prev[k - 1], now[k - 1])
            o_ref[span, i * BLK : (i + 1) * BLK] = half_silu(h).astype(BF16)
            prev = now


def proj_conv(flag, proj_t, halo):
    rows, tokens = proj_t.shape
    return pl.pallas_call(
        proj_conv_kernel,
        in_specs=specs(3, 1),
        out_specs=specs(1)[0],
        out_shape=jax.ShapeDtypeStruct((rows, tokens), BF16),
        compiler_params=params(),
        cost_estimate=cost(rows * tokens * 4000, rows * tokens * 4, rows * tokens),
        name="proj_conv",
    )(flag, proj_t, halo)


def decay_kernel(
    dt_ref, bias_ref, alog_ref, skip_ref, run_ref, abs_ref, step_ref, tot_ref, wide_ref
):
    heads, tokens = dt_ref.shape
    blocks = tokens // BLK
    chans = tot_ref.shape[1]
    raw = dt_ref[...] + upright(bias_ref[...])
    step = jnp.maximum(raw, 0.0) + jnp.log1p(jnp.exp(-jnp.abs(raw)))
    step_ref[...] = step
    log_decay = step * (-LOG2E * jnp.exp(upright(alog_ref[...])))
    stack = jnp.concatenate(
        [log_decay[:, b * BLK : (b + 1) * BLK] for b in range(blocks)], axis=0
    )
    upper = (iota((BLK, BLK), 0) <= iota((BLK, BLK), 1)).astype(F32)
    run = jnp.dot(stack, upper, precision=HIGH, preferred_element_type=F32)
    total = run[:, BLK - 1 : BLK]
    count = blocks * heads
    r, c = iota((count, count), 0), iota((count, count), 1)
    before = ((c // heads < r // heads) & (c % heads == r % heads)).astype(F32)
    start = jnp.dot(
        before,
        jnp.broadcast_to(total, (count, BLK)),
        precision=HIGH,
        preferred_element_type=F32,
    )
    whole = run + start
    for b in range(blocks):
        run_ref[:, b * BLK : (b + 1) * BLK] = run[b * heads : (b + 1) * heads]
        abs_ref[:, b * BLK : (b + 1) * BLK] = whole[b * heads : (b + 1) * heads]
    pick = (iota((blocks, count), 1) // heads == iota((blocks, count), 0)).astype(F32)
    chan_head = iota((count, chans), 1) // (chans // heads)
    spread = jnp.where(chan_head == iota((count, chans), 0) % heads, total, 0.0)
    own = iota((heads, chans), 1) // (chans // heads) == iota((heads, chans), 0)
    wide_ref[...] = jnp.sum(
        jnp.where(own, upright(skip_ref[...]), 0.0), axis=0, keepdims=True
    )
    tot_ref[...] = jnp.dot(pick, spread, precision=HIGH, preferred_element_type=F32)


def decays(dt_t, bias, a_log, skip, chans):
    heads, tokens = dt_t.shape
    rows = jax.ShapeDtypeStruct((heads, tokens), F32)
    return pl.pallas_call(
        decay_kernel,
        in_specs=specs(4),
        out_specs=tuple(specs(5)),
        out_shape=(
            rows,
            rows,
            rows,
            jax.ShapeDtypeStruct((tokens // BLK, chans), F32),
            jax.ShapeDtypeStruct((1, chans), F32),
        ),
        compiler_params=params(),
        cost_estimate=cost(heads * tokens * 20000, heads * tokens * 16, heads * tokens * 2),
        name="decays",
    )(dt_t, bias[None, :], a_log[None, :], skip[None, :])


def chan_conv_kernel(base, flag_ref, x_ref, w_ref, run_ref, step_ref, *rest):
    o_ref, v_ref, t_ref = rest[-3:]
    halo_ref = rest[0]
    chans = x_ref.shape[1]
    heads = run_ref.shape[0]
    count = o_ref.shape[0] // BLK
    spread = head_spread(heads, chans)

    def block(i, tails):
        src, dst = block_at(base + i), block_at(i)
        run = run_ref[:, src]
        coef = (jnp.exp2(run[:, BLK - 1 : BLK] - run) * step_ref[:, src]).astype(BF16)
        wide = lax.dot_general(
            coef, spread, (((0,), (0,)), ((), ())), preferred_element_type=F32
        )
        for at in range(chans // BLK):
            lanes = slice(at * BLK, (at + 1) * BLK)
            taps = [0.5 * w_ref[k : k + 1, lanes].astype(F32) for k in range(4)]
            cur = x_ref[src, lanes].astype(F32)
            ext = jnp.concatenate([tails(at).astype(F32)[8:16], cur], axis=0)
            back = pltpu.roll(ext, 1, 0)
            older = pltpu.roll(taps[1] * ext + taps[0] * back, 2, 0)
            y = half_silu(taps[3] * cur + taps[2] * back[8:] + older[8:])
            o_ref[dst, lanes] = y.astype(BF16)
            v_ref[dst, lanes] = (y * wide[:, lanes]).astype(BF16)

    def from_halo(at):
        lo = halo_ref.shape[0] - 16 - 16 * (chans // BLK) + 16 * at
        part = halo_ref[lo : lo + 16, :]
        return jnp.where(flag_ref[1] == 0, jnp.zeros_like(part), part)

    def inner(i):
        def tail(at):
            lo = pl.multiple_of((base + i) * BLK - 16, 16)
            return x_ref[pl.ds(lo, 16), at * BLK : (at + 1) * BLK]

        block(i, tail)

    first = 1 if base == 0 else 0
    if first:
        block(0, from_halo)

    @pl.loop(first, count, unroll=CONV_UNROLL[0] if first else CONV_UNROLL[1])
    def _(i):
        inner(i)

    t_ref[...] = jnp.zeros_like(t_ref)


def chan_conv(flag, x, taps, run, step, halo, part, parts):
    tokens, chans = x.shape
    here = tokens // parts

    def kernel(*refs):
        chan_conv_kernel(part * here // BLK, *refs)

    return pl.pallas_call(
        kernel,
        in_specs=specs(5 + (part == 0), 1),
        out_specs=tuple(specs(3)),
        out_shape=(jax.ShapeDtypeStruct((here, chans), BF16),) * 2
        + (jax.ShapeDtypeStruct((8, BLK), F32),),
        compiler_params=params(),
        cost_estimate=cost(here * chans * 4000, here * chans * 6, here * chans),
        name="chan_conv",
    )(flag, x, taps, run, step, *([halo] if part == 0 else []))


def pick_quarters(flag_ref, quarter_refs, at):
    own, near, far, cross = (ref[:, at] for ref in quarter_refs)
    here = jnp.concatenate([own, near], axis=0)
    there = jnp.concatenate([far, cross], axis=0)
    return here, there, flag_ref[0] == 0


def state_kernel(flag_ref, own_ref, near_ref, far_ref, cross_ref, tot_ref, *rest):
    s_ref, msg_ref, now_ref = rest[-3:]
    v_refs = rest[:-3]
    chans = s_ref.shape[2]
    now_ref[...] = jnp.zeros_like(now_ref)
    for at, v_ref in enumerate(v_refs):
        count = v_ref.shape[0] // BLK
        base = at * count

        @pl.loop(0, count, unroll=STATE_UNROLL)
        def _(i):
            here, there, local_b = pick_quarters(
                flag_ref, (own_ref, near_ref, far_ref, cross_ref), block_at(base + i)
            )
            b = jnp.where(local_b, here, there)
            add = jnp.dot(b, v_ref[block_at(i), :], preferred_element_type=F32)
            now = now_ref[...]
            s_ref[base + i] = now.astype(BF16)
            now_ref[...] = jnp.exp2(tot_ref[pl.ds(base + i, 1), :]) * now + add

    log = jnp.sum(tot_ref[...], axis=0, keepdims=True)
    high = log.astype(BF16).astype(F32)
    mid = (log - high).astype(BF16).astype(F32)
    low = (log - high) - mid
    row = iota((16, chans), 0)
    parts = jnp.where(row == 0, high, jnp.where(row == 1, mid, jnp.where(row == 2, low, 0.0)))
    msg_ref[0:STATE, :] = now_ref[...].astype(BF16)
    msg_ref[STATE : STATE + 16, :] = parts.astype(BF16)


def states(flag, weighted, quarters, totals):
    blocks, chans = totals.shape
    return pl.pallas_call(
        state_kernel,
        in_specs=specs(6 + len(weighted), 1),
        out_specs=tuple(specs(2)),
        out_shape=(
            jax.ShapeDtypeStruct((blocks, STATE, chans), BF16),
            jax.ShapeDtypeStruct((STATE + 16, chans), BF16),
        ),
        scratch_shapes=[pltpu.VMEM((STATE, chans), F32)],
        compiler_params=params(),
        cost_estimate=cost(blocks * BLK * chans * 2000, blocks * BLK * chans * 4),
        name="states",
    )(flag, *quarters, totals, *weighted)


def local_kernel(
    base, offset, flag_ref, x_ref, own_ref, near_ref, far_ref, cross_ref, s_ref, run_ref, step_ref,
    skip_ref, o_ref
):
    tokens, chans = o_ref.shape
    heads = run_ref.shape[0]
    causal = iota((BLK, BLK), 0) >= iota((BLK, BLK), 1)
    left = iota((2 * BLK, BLK), 1) < chans // heads

    @pl.loop(0, tokens // BLK, unroll=LOCAL_UNROLL)
    def _(i):
        at = block_at(base + i)
        here, there, local_b = pick_quarters(
            flag_ref, (own_ref, near_ref, far_ref, cross_ref), at
        )
        c = jnp.transpose(jnp.where(local_b, there, here))
        b = jnp.where(local_b, here, there)
        gram = jnp.dot(c, b, preferred_element_type=F32)
        gram = jnp.where(causal, gram, 0.0).astype(BF16)
        run = run_ref[:, at]
        run_t = jnp.transpose(run)
        step = step_ref[:, at].astype(BF16)
        for pair in range(heads // 2):
            lanes = slice(pair * BLK, (pair + 1) * BLK)
            mats = []
            for h in (2 * pair, 2 * pair + 1):
                column = jnp.broadcast_to(run_t[:, h : h + 1], (BLK, BLK))
                gap = (column - run[h : h + 1, :]).astype(BF16)
                mats.append(jnp.exp2(jnp.minimum(gap, 0.0)) * gram * step[h : h + 1, :])
                mats.append(jnp.exp2(column.astype(BF16)) * c)
            lhs = jnp.concatenate(mats, axis=1)
            xs = x_ref[block_at(offset + i), lanes]
            both = jnp.concatenate([xs, s_ref[base + i, :, lanes]], axis=0)
            zero = jnp.zeros_like(both)
            rhs = jnp.concatenate(
                [jnp.where(left, both, zero), jnp.where(left, zero, both)], axis=0
            )
            out = jnp.dot(lhs, rhs, preferred_element_type=F32)
            out = out + skip_ref[:, lanes] * xs.astype(F32)
            o_ref[block_at(i), lanes] = out.astype(BF16)


def local(flag, x_conv, quarters, entering, run, step, skip, part, parts, offset):
    heads, tokens = run.shape
    chans = x_conv.shape[1]
    here = tokens // parts

    def kernel(*refs):
        local_kernel(part * here // BLK, offset, *refs)

    return pl.pallas_call(
        kernel,
        in_specs=specs(10, 1),
        out_specs=specs(1)[0],
        out_shape=jax.ShapeDtypeStruct((here, chans), BF16),
        compiler_params=params(),
        cost_estimate=cost(8000 * here * chans, here * chans * 6, here * heads * BLK * 2),
        name="local",
    )(flag, x_conv, *quarters, entering, run, step, skip)


def carry_kernel(nloc, flag_ref, own_ref, near_ref, far_ref, cross_ref, abs_ref, z_ref, *rest):
    l_refs, msgs = rest[:nloc], rest[nloc:-4]
    g_ref, q_ref, s_ref, acc_ref = rest[-4:]
    chans = g_ref.shape[1]
    heads = abs_ref.shape[0]
    gone = jnp.zeros((1, chans), F32)
    for d, msg in enumerate(msgs, 1):
        factor = jnp.where(flag_ref[1] >= d, jnp.exp2(gone), 0.0)
        term = factor * msg[0:STATE, :].astype(F32)
        acc_ref[...] = term if d == 1 else acc_ref[...] + term
        parts = msg[STATE : STATE + 16, :].astype(F32)
        gone = gone + ((parts[0:1] + parts[1:2]) + parts[2:3])
    s_ref[...] = acc_ref[...].astype(BF16)
    spread = head_spread(heads, chans)
    done = 0
    for l_ref in l_refs:
        count = l_ref.shape[0] // BLK
        first = done
        done += count

        @pl.loop(0, count, unroll=CARRY_UNROLL)
        def _(i):
            at = block_at(first + i)
            here, there, local_b = pick_quarters(
                flag_ref, (own_ref, near_ref, far_ref, cross_ref), at
            )
            c = jnp.transpose(jnp.where(local_b, there, here))
            wide = lax.dot_general(
                jnp.exp2(abs_ref[:, at]).astype(BF16),
                spread,
                (((0,), (0,)), ((), ())),
                preferred_element_type=F32,
            )
            carried = jnp.dot(c, s_ref[...], preferred_element_type=F32)
            folded = None
            for lo in range(0, chans, BLK):
                lanes = slice(lo, lo + BLK)
                gated = l_ref[block_at(i), lanes].astype(F32) + wide[:, lanes] * carried[:, lanes]
                gated = gated * half_silu(0.5 * z_ref[at, lanes].astype(F32))
                g_ref[at, lanes] = gated.astype(BF16)
                square = gated * gated
                folded = square if folded is None else folded + square
            q_ref[pl.ds(first + i, 1), :] = jnp.sum(jnp.transpose(folded), axis=0, keepdims=True)


def carry(flag, locs, gate, quarters, whole, msgs):
    heads, tokens = whole.shape
    chans = locs[0].shape[1]

    def kernel(*refs):
        carry_kernel(len(locs), *refs)

    return pl.pallas_call(
        kernel,
        in_specs=specs(7 + len(locs) + len(msgs), 1),
        out_specs=tuple(specs(2)),
        scratch_shapes=[pltpu.VMEM((STATE, chans), BF16), pltpu.VMEM((STATE, chans), F32)],
        out_shape=(
            jax.ShapeDtypeStruct((tokens, chans), BF16),
            jax.ShapeDtypeStruct((tokens // BLK, BLK), F32),
        ),
        compiler_params=params(),
        cost_estimate=cost(4000 * tokens * chans, tokens * chans * 6, tokens * chans),
        name="carry",
    )(flag, *quarters, whole, gate, *locs, *msgs)


def norm_kernel(width, g_ref, q_ref, gain_ref, o_ref):
    tokens, chans = o_ref.shape
    per = tokens // BLK
    first = pl.program_id(0) * per
    for i in range(per):
        at = slice(i * BLK, (i + 1) * BLK)
        scale = lax.rsqrt(q_ref[pl.ds(first + i, 1), :] * (1.0 / width) + 1e-05)
        column = jnp.transpose(jnp.broadcast_to(scale, (BLK, BLK)))
        for lo in range(0, chans, BLK):
            lanes = slice(lo, lo + BLK)
            g = g_ref[block_at(first + i), lanes].astype(F32)
            o_ref[at, lanes] = (g * column * gain_ref[:, lanes]).astype(BF16)


def norm(gated, squares, gain, width, rows=1024):
    tokens, chans = gated.shape

    def kernel(*refs):
        norm_kernel(width, *refs)

    return pl.pallas_call(
        kernel,
        grid=(tokens // rows,),
        in_specs=specs(3),
        out_specs=pl.BlockSpec((rows, chans), lambda i: (i, 0)),
        out_shape=jax.ShapeDtypeStruct((tokens, chans), BF16),
        compiler_params=params(),
        cost_estimate=cost(tokens * chans * 3, tokens * chans * 4),
        name="norm",
    )(gated, squares, gain)


def on_device(
    x_stream, gate_z, state_proj, dt_raw, dt_bias, a_log, skip_d, conv_x, conv_proj, norm_gain
):
    tokens, chans = x_stream.shape
    heads = dt_raw.shape[1]
    head_pos = lax.axis_index("head")
    ctx_pos = lax.axis_index("ctx")
    count = lax.axis_size("ctx")
    flag = jnp.stack([head_pos >> 1 & 1, ctx_pos]).astype(jnp.int32)

    proj_t = state_proj.T
    far_raw = swapped(proj_t, "head", 2)
    near_raw = swapped(proj_t, "head", 1)
    halo = rotated(tails(x_stream, proj_t, conv_proj), "ctx", 1)
    run, whole, step, totals, skip = decays(dt_raw.T, dt_bias, a_log, skip_d, chans)
    halves = 2
    x_two, v_two, mark = chan_conv(flag, x_stream, conv_x, run, step, None, 1, halves)
    halo = after(halo, mark)
    halo_far = swapped(halo, "head", 2)
    halo_near = swapped(halo, "head", 1)
    far_raw = after(far_raw, mark)
    cross_raw = swapped(far_raw, "head", 1)
    halo_cross = swapped(halo_far, "head", 1)
    x_one, v_one, mark = chan_conv(flag, x_stream, conv_x, run, step, halo, 0, halves)
    own = proj_conv(flag, proj_t, halo)
    near = proj_conv(flag, near_raw, halo_near)
    far = proj_conv(flag, after(far_raw, mark, own, near), halo_far)
    cross = proj_conv(flag, after(cross_raw, far), halo_cross)
    quarters = (own, near, far, cross)

    entering, message = states(flag, (v_one, v_two), quarters, totals)

    up = down = message
    ahead, behind, locs = [], [], []
    parts = count // 2
    per = parts // halves
    for at in range(parts):
        up = rotated(up, "ctx", 1)
        ahead.append(up)
        if at + 1 < count - parts:
            down = rotated(down, "ctx", -1)
            behind.append(down)
        piece = local(
            flag, (x_one, x_two)[at // per], quarters, entering, run, step, skip, at, parts,
            at % per * (tokens // parts // BLK),
        )
        if at + 1 < parts:
            up, down, piece = lax.optimization_barrier((up, down, piece))
        locs.append(piece)
    msgs = ahead + behind[::-1]

    width = HEADS // GROUPS * (chans // heads)
    gated, squares = carry(flag, locs, gate_z, quarters, whole, msgs)
    squares = (squares + swapped(squares, "head", 1)) + (
        swapped(squares, "head", 2) + swapped(squares, "head", 3)
    )
    return norm(gated, squares, norm_gain[None, :], width)


def solution(mesh):
    return jax.shard_map(
        on_device,
        mesh=mesh,
        in_specs=(
            P("ctx", "head"),
            P("ctx", "head"),
            P("ctx", "head"),
            P("ctx", "head"),
            P("head"),
            P("head"),
            P("head"),
            P(None, "head"),
            P(None, "head"),
            P("head"),
        ),
        out_specs=P("ctx", "head"),
        check_vma=False,
    )
```

time: 278 us -> 73.9 us (0.27)
  other arithmetic: 103 us -> 0.09 us
  local copies, waits for them, and re-layouts: 59.4 us -> 2.23 us
  Pallas kernels: 0 us -> 40.8 us
  matrix products: 38.5 us -> 0 us
  waiting for transfers between devices: 24.9 us -> 6.73 us
  between operations: 14.5 us -> 0.2 us
  blocking collectives: 13.5 us -> 0 us
    pallas_call x0 -> x15, Pallas kernels: none -> 40.8 us  [the longest x4 12.8 us: local(): pl.pallas_call(kernel, in_specs=specs(10, 1), out_specs=specs(1)[0], out_...]
    dot_general x7 -> x0, matrix products: 38.5 us -> none  [the longest x1 10.7 us: block_scan(): jnp.einsum('chts,cshp->cthp', weights, x_blocks, preferred_element_type=j...]
    add x33 -> x1, other arithmetic: 33.3 us -> 0.01 us  [on_device(): squares + swapped(squares, 'head', 1) + (swapped(squares, 'head', 2) + sw...]
    dynamic_update_slice x32 -> x0, other arithmetic: 23.4 us -> none  [block_scan(): lax.scan(advance, empty_state, (jnp.exp(block_total), states))]
    mul x36 -> x0, local copies, waits for them, and re-layouts: 22.5 us -> none  [the longest x32 21.8 us: advance(): return (factor[:, None, None] * state_now + addend, state_now)]
    unnamed x53 -> x18, local copies, waits for them, and re-layouts: 17.8 us -> 2.23 us
    all_gather x1 -> x0, waiting for transfers between devices: 15.5 us -> none  [on_device(): lax.all_gather(final_state[None].astype(jnp.bfloat16), 'ctx', axis=0, til...]
    reduce_sum x2 -> x0, other arithmetic: 14.1 us -> none  [the longest x1 13.9 us: on_device(): group_total = jnp.sum(gated_out * gated_out, axis=1)]
  transfers between devices with their start and end apart: 7 -> 17, of which waited for: 4 -> 4; matrix products, arithmetic and copies ran while one was open for 25% -> 0% of each run, Pallas kernels for 0% -> 39%
where the time goes in v1:
time: 73.9 us; the launch traced here: 73.7 us
  Pallas kernels  40.8 us (55%)
  starting transfers between devices  23.7 us (32%)
  waiting for transfers between devices  6.73 us (9%)
  local copies, waits for them, and re-layouts  2.23 us (3%)
    pallas_call x4, Pallas kernels, local(): pl.pallas_call(kernel, in_specs=specs(10, 1), out_specs=specs(1)[0], out_...  12.8 us
    ppermute x8, starting transfers between devices, rotated(): return lax.ppermute(x, axis, [(i, (i + by) % count) for i in range(count)])  12.7 us
    ppermute x9, starting transfers between devices, swapped(): lax.ppermute(value, axis, [(i, i ^ mask) for i in range(lax.axis_size(axi...  11 us
    pallas_call x2, Pallas kernels, chan_conv(): pl.pallas_call(kernel, in_specs=specs(5 + (part == 0), 1), out_specs=tupl...  9.28 us
    pallas_call x4, Pallas kernels, proj_conv(): pl.pallas_call(proj_conv_kernel, in_specs=specs(3, 1), out_specs=specs(1)...  5.7 us
    pallas_call x1, Pallas kernels, carry(): pl.pallas_call(kernel, in_specs=specs(7 + len(locs) + len(msgs), 1), out_...  4.96 us
    ppermute x8, waiting for transfers between devices, rotated(): return lax.ppermute(x, axis, [(i, (i + by) % count) for i in range(count)])  4.62 us
    pallas_call x1, Pallas kernels, norm(): pl.pallas_call(kernel, grid=(tokens // rows,), in_specs=specs(3), out_spe...  3.02 us
  transfers between devices with their start and end apart: 17, of which 4 were waited for; matrix products, arithmetic and copies ran while one was open for 0% of the time, Pallas kernels for 39%

profile of v1, /device:TPU:1, one launch (start us, length us, event | category | flops | bytes accessed | tf_op | source)
XLA Modules:
  0.0 73.7 jit_solution(8611196631863565171)
XLA Ops:
  0.0 2.1 %collective-permute-start.3 = (bf16[64,4096]{1,0:T(8,128)(2,1)}, bf16[64,4096]{1,0:T(8,128)(2,1)S(1)}, u32[]{:S(2)}, u32[]{:S(2)}) collective-permute-start(bf16[64,4096]{1,0:T(8,128)(2,1)} %bitcast.8), channel_id=1, source_target_pairs={{0,2},{1,3},{2,0},{3,1},{4,6},{5,7},{6,4},{7,5},{8,10},{9,11},{10,... | collective-permute-start | bytes 1572872 | tf_op jit(solution)/shard_map/ppermute | solution.py:35
  2.2 1.3 %collective-permute-start.1 = (bf16[64,4096]{1,0:T(8,128)(2,1)}, bf16[64,4096]{1,0:T(8,128)(2,1)S(1)}, u32[]{:S(2)}, u32[]{:S(2)}) collective-permute-start(bf16[64,4096]{1,0:T(8,128)(2,1)} %bitcast.9), channel_id=1, source_target_pairs={{0,1},{1,0},{2,3},{3,2},{4,5},{5,4},{6,7},{7,6},{8,9},{9,8},{10,11... | collective-permute-start | bytes 1572872 | tf_op jit(solution)/shard_map/ppermute | solution.py:35
  3.4 1.4 %tails.1 = bf16[144,128]{1,0:T(8,128)(2,1)} custom-call(bf16[4096,512]{1,0:T(8,128)(2,1)} %refs_1_.3, bf16[64,4096]{1,0:T(8,128)(2,1)} %bitcast.10, bf16[4,64]{1,0:T(4,128)(2,1)} %w_ref.1), custom_call_target="tpu_custom_call" | custom-call | tf_op jit(solution)/shard_map/tails/pallas_call | solution.py:92
  4.8 1.3 %collective-permute-start = (bf16[144,128]{1,0:T(8,128)(2,1)}, bf16[144,128]{1,0:T(8,128)(2,1)S(1)}, u32[]{:S(2)}, u32[]{:S(2)}) collective-permute-start(bf16[144,128]{1,0:T(8,128)(2,1)} %tails.1), channel_id=1, source_target_pairs={{0,32},{32,64},{64,96},{96,128},{128,160},{160,192},{192,224},{224... | collective-permute-start | bytes 110600 | tf_op jit(solution)/shard_map/ppermute | solution.py:31
  6.1 1.2 %decays.1 = (f32[8,4096]{1,0:T(8,128)S(1)}, f32[8,4096]{1,0:T(8,128)S(1)}, f32[8,4096]{1,0:T(8,128)S(1)}, f32[32,512]{1,0:T(8,128)S(1)}, f32[1,512]{1,0:T(1,128)S(1)}) custom-call(f32[8,4096]{1,0:T(8,128)S(1)} %bitcast.13, f32[1,8]{1,0:T(1,128)S(1)} %bitcast.14, f32[1,8]{1,0:T(1,128)S(1)} %bitcast.15, f32[1,8]{1,0:T(1,128)S(1)} %bitcast.16), custom_call_target="tpu_custom_call" | custom-call | flops 655360000 | bytes 524288 | tf_op jit(solution)/shard_map/decays/pallas_call | solution.py:183
  7.3 0.1 pad_add_fusion.refs_0_.flag_ref
  7.4 2.2 %copy-done = bf16[4096,512]{1,0:T(8,128)(2,1)S(1)} copy-done((bf16[4096,512]{1,0:T(8,128)(2,1)S(1)}, bf16[4096,512]{1,0:T(8,128)(2,1)}, u32[]{:S(2)}) %copy-start) | copy-done | bytes 4194328
  9.6 4.4 %chan_conv.2 = (bf16[2048,512]{1,0:T(8,128)(2,1)S(1)}, bf16[2048,512]{1,0:T(8,128)(2,1)S(1)}, f32[8,128]{1,0:T(8,128)}) custom-call(s32[2]{0:T(128)S(1)} %pad_add_fusion.refs_0_.flag_ref, bf16[4096,512]{1,0:T(8,128)(2,1)S(1)} %copy-done, bf16[4,512]{1,0:T(4,128)(2,1)S(1)} %copy-done.5, f32[8,4096]{1,0:T(8,128)S(1)} %get-tuple-element.31.refs_3_.refs_7_, ...), custom_call_target="tpu_custom_call" | custom-call | flops 4194304000 | bytes 6291456 | tf_op jit(solution)/shard_map/chan_conv/pallas_call | solution.py:256
  14.0 0.0 collective-permute-done.halo_ref.refs_5_
  14.0 0.4 collective-permute-start.4
  14.3 0.5 collective-permute-start.2
  14.8 0.0 collective-permute-done.3.p_ref
  14.8 0.4 collective-permute-start.5
  15.2 4.9 %chan_conv.3 = (bf16[2048,512]{1,0:T(8,128)(2,1)S(1)}, bf16[2048,512]{1,0:T(8,128)(2,1)S(1)}, f32[8,128]{1,0:T(8,128)}) custom-call(s32[2]{0:T(128)S(1)} %pad_add_fusion.refs_0_.flag_ref, bf16[4096,512]{1,0:T(8,128)(2,1)S(1)} %copy-done, bf16[4,512]{1,0:T(4,128)(2,1)S(1)} %copy-done.5, f32[8,4096]{1,0:T(8,128)S(1)} %get-tuple-element.31.refs_3_.refs_7_, ...), custom_call_target="tpu_custom_call" | custom-call | flops 4194304000 | bytes 6291456 | tf_op jit(solution)/shard_map/chan_conv/pallas_call | solution.py:256
  20.1 1.4 %proj_conv.4.own_ref.refs_2_.refs_1_ = bf16[64,4096]{1,0:T(8,128)(2,1)S(1)} custom-call(s32[2]{0:T(128)S(1)} %pad_add_fusion.refs_0_.flag_ref, bf16[64,4096]{1,0:T(8,128)(2,1)S(1)} %bitcast.11, bf16[144,128]{1,0:T(8,128)(2,1)S(1)} %collective-permute-done.halo_ref.refs_5_), custom_call_target="tpu_custom_call" | custom-call | flops 1048576000 | bytes 1048576 | tf_op jit(solution)/shard_map/proj_conv/pallas_call | solution.py:130
  21.6 0.0 collective-permute-done.4.halo_ref
  21.6 0.4 collective-permute-start.6
  21.9 1.4 %proj_conv.5.near_ref.refs_3_.refs_2_ = bf16[64,4096]{1,0:T(8,128)(2,1)S(1)} custom-call(s32[2]{0:T(128)S(1)} %pad_add_fusion.refs_0_.flag_ref, bf16[64,4096]{1,0:T(8,128)(2,1)S(1)} %collective-permute-done.1.p_ref, bf16[144,128]{1,0:T(8,128)(2,1)S(1)} %collective-permute-done.2.halo_ref), custom_call_target="tpu_custom_call" | custom-call | flops 1048576000 | bytes 1048576 | tf_op jit(solution)/shard_map/proj_conv/pallas_call | solution.py:130
  23.4 1.4 %proj_conv.6.far_ref.refs_4_.refs_3_ = bf16[64,4096]{1,0:T(8,128)(2,1)S(1)} custom-call(s32[2]{0:T(128)S(1)} %pad_add_fusion.refs_0_.flag_ref, bf16[64,4096]{1,0:T(8,128)(2,1)S(1)} %collective-permute-done.3.p_ref, bf16[144,128]{1,0:T(8,128)(2,1)S(1)} %collective-permute-done.4.halo_ref), custom_call_target="tpu_custom_call" | custom-call | flops 1048576000 | bytes 1048576 | tf_op jit(solution)/shard_map/proj_conv/pallas_call | solution.py:130
  24.8 0.0 collective-permute-done.6.halo_ref
  24.8 1.4 %proj_conv.7.cross_ref.refs_5_.refs_4_ = bf16[64,4096]{1,0:T(8,128)(2,1)S(1)} custom-call(s32[2]{0:T(128)S(1)} %pad_add_fusion.refs_0_.flag_ref, bf16[64,4096]{1,0:T(8,128)(2,1)S(1)} %collective-permute-done.5.p_ref, bf16[144,128]{1,0:T(8,128)(2,1)S(1)} %collective-permute-done.6.halo_ref), custom_call_target="tpu_custom_call" | custom-call | flops 1048576000 | bytes 1048576 | tf_op jit(solution)/shard_map/proj_conv/pallas_call | solution.py:130
  26.2 2.5 %states.1 = (bf16[32,128,512]{2,1,0:T(8,128)(2,1)S(1)}, bf16[144,512]{1,0:T(8,128)(2,1)S(1)}) custom-call(s32[2]{0:T(128)S(1)} %pad_add_fusion.refs_0_.flag_ref, bf16[64,4096]{1,0:T(8,128)(2,1)S(1)} %proj_conv.4.own_ref.refs_2_.refs_1_, bf16[64,4096]{1,0:T(8,128)(2,1)S(1)} %proj_conv.5.near_ref.refs_3_.refs_2_, ...), custom_call_target="tpu_custom_call" | custom-call | flops 4194304000 | bytes 8388608 | tf_op jit(solution)/shard_map/states/pallas_call | solution.py:307
  28.8 5.8 %collective-permute-start.8 = (bf16[144,512]{1,0:T(8,128)(2,1)S(1)}, bf16[144,512]{1,0:T(8,128)(2,1)S(1)}, u32[]{:S(2)}, u32[]{:S(2)}) collective-permute-start(bf16[144,512]{1,0:T(8,128)(2,1)S(1)} %get-tuple-element.42), channel_id=1, source_target_pairs={{0,224},{32,0},{64,32},{96,64},{128,96},{160,128},{192,160},{224,1... | collective-permute-start | bytes 442376 | tf_op jit(solution)/shard_map/ppermute | solution.py:31
  34.6 3.2 %local.4.refs_7_ = bf16[1024,512]{1,0:T(8,128)(2,1)S(1)} custom-call(s32[2]{0:T(128)S(1)} %pad_add_fusion.refs_0_.flag_ref, bf16[2048,512]{1,0:T(8,128)(2,1)S(1)} %get-tuple-element.43.refs_1_, bf16[64,4096]{1,0:T(8,128)(2,1)S(1)} %proj_conv.4.own_ref.refs_2_.refs_1_, bf16[64,4096]{1,0:T(8,128)(2,1)S(1)} %proj_conv.5.near_ref.refs_3_.refs_2_, ...), custom_call_target="tpu_custom_call" | custom-call | flops 4194304000 | bytes 3145728 | tf_op jit(solution)/shard_map/local/pallas_call | solution.py:372
  37.8 0.0 collective-permute-done.8.refs_17_
  37.9 2.6 %collective-permute-done.7.refs_11_ = bf16[144,512]{1,0:T(8,128)(2,1)S(1)} collective-permute-done((bf16[144,512]{1,0:T(8,128)(2,1)S(1)}, bf16[144,512]{1,0:T(8,128)(2,1)S(1)}, u32[]{:S(2)}, u32[]{:S(2)}) %collective-permute-start.7) | collective-permute-done | bytes 147488 | tf_op jit(solution)/shard_map/ppermute | solution.py:31
  40.5 0.0 collective-permute-start.9
  40.5 2.7 %collective-permute-start.10 = (bf16[144,512]{1,0:T(8,128)(2,1)S(1)}, bf16[144,512]{1,0:T(8,128)(2,1)S(1)}, u32[]{:S(2)}, u32[]{:S(2)}) collective-permute-start(bf16[144,512]{1,0:T(8,128)(2,1)S(1)} %collective-permute-done.8.refs_17_), channel_id=1, source_target_pairs={{0,224},{32,0},{64,32},{96,64},{128,96},{160,128},{192,160},{224,1... | collective-permute-start | bytes 442376 | tf_op jit(solution)/shard_map/ppermute | solution.py:31
  43.1 3.2 %local.5.refs_8_ = bf16[1024,512]{1,0:T(8,128)(2,1)S(1)} custom-call(s32[2]{0:T(128)S(1)} %pad_add_fusion.refs_0_.flag_ref, bf16[2048,512]{1,0:T(8,128)(2,1)S(1)} %get-tuple-element.43.refs_1_, bf16[64,4096]{1,0:T(8,128)(2,1)S(1)} %proj_conv.4.own_ref.refs_2_.refs_1_, bf16[64,4096]{1,0:T(8,128)(2,1)S(1)} %proj_conv.5.near_ref.refs_3_.refs_2_, ...), custom_call_target="tpu_custom_call" | custom-call | flops 4194304000 | bytes 3145728 | tf_op jit(solution)/shard_map/local/pallas_call | solution.py:372
  46.3 0.0 collective-permute-done.9.refs_12_
  46.4 0.0 collective-permute-done.10.refs_16_
  46.4 0.1 collective-permute-start.11
  46.5 2.7 %collective-permute-start.12 = (bf16[144,512]{1,0:T(8,128)(2,1)S(1)}, bf16[144,512]{1,0:T(8,128)(2,1)S(1)}, u32[]{:S(2)}, u32[]{:S(2)}) collective-permute-start(bf16[144,512]{1,0:T(8,128)(2,1)S(1)} %collective-permute-done.10.refs_16_), channel_id=1, source_target_pairs={{0,224},{32,0},{64,32},{96,64},{128,96},{160,128},{192,160},{224,1... | collective-permute-start | bytes 442376 | tf_op jit(solution)/shard_map/ppermute | solution.py:31
  49.1 3.2 %local.6.refs_9_ = bf16[1024,512]{1,0:T(8,128)(2,1)S(1)} custom-call(s32[2]{0:T(128)S(1)} %pad_add_fusion.refs_0_.flag_ref, bf16[2048,512]{1,0:T(8,128)(2,1)S(1)} %get-tuple-element.52.refs_1_, bf16[64,4096]{1,0:T(8,128)(2,1)S(1)} %proj_conv.4.own_ref.refs_2_.refs_1_, bf16[64,4096]{1,0:T(8,128)(2,1)S(1)} %proj_conv.5.near_ref.refs_3_.refs_2_, ...), custom_call_target="tpu_custom_call" | custom-call | flops 4194304000 | bytes 3145728 | tf_op jit(solution)/shard_map/local/pallas_call | solution.py:372
  52.3 0.0 copy-start.3
  52.3 0.0 collective-permute-done.11.refs_13_
  52.3 0.0 collective-permute-done.12.refs_15_
  52.4 0.1 collective-permute-start.13
  52.4 3.2 %local.7.refs_10_ = bf16[1024,512]{1,0:T(8,128)(2,1)S(1)} custom-call(s32[2]{0:T(128)S(1)} %pad_add_fusion.refs_0_.flag_ref, bf16[2048,512]{1,0:T(8,128)(2,1)S(1)} %get-tuple-element.52.refs_1_, bf16[64,4096]{1,0:T(8,128)(2,1)S(1)} %proj_conv.4.own_ref.refs_2_.refs_1_, bf16[64,4096]{1,0:T(8,128)(2,1)S(1)} %proj_conv.5.near_ref.refs_3_.refs_2_, ...), custom_call_target="tpu_custom_call" | custom-call | flops 4194304000 | bytes 3145728 | tf_op jit(solution)/shard_map/local/pallas_call | solution.py:372
  55.6 2.0 %collective-permute-done.13.refs_14_ = bf16[144,512]{1,0:T(8,128)(2,1)S(1)} collective-permute-done((bf16[144,512]{1,0:T(8,128)(2,1)S(1)}, bf16[144,512]{1,0:T(8,128)(2,1)S(1)}, u32[]{:S(2)}, u32[]{:S(2)}) %collective-permute-start.13) | collective-permute-done | bytes 147488 | tf_op jit(solution)/shard_map/ppermute | solution.py:31
  57.6 5.0 %carry.1 = (bf16[4096,512]{1,0:T(8,128)(2,1)S(1)}, f32[32,128]{1,0:T(8,128)S(1)}) custom-call(s32[2]{0:T(128)S(1)} %pad_add_fusion.refs_0_.flag_ref, bf16[64,4096]{1,0:T(8,128)(2,1)S(1)} %proj_conv.4.own_ref.refs_2_.refs_1_, bf16[64,4096]{1,0:T(8,128)(2,1)S(1)} %proj_conv.5.near_ref.refs_3_.refs_2_, bf16[64,4096]{1,0:T(8,128)(2,1)S(1)} %proj_conv.6.far_ref.refs_4_.refs_3_, ...), custom_call_target="tpu_custom_call" | custom-call | flops 8388608000 | bytes 12582912 | tf_op jit(solution)/shard_map/carry/pallas_call | solution.py:435
  62.6 5.5 %collective-permute-start.16 = (f32[32,128]{1,0:T(8,128)S(1)}, f32[32,128]{1,0:T(8,128)S(1)}, u32[]{:S(2)}, u32[]{:S(2)}) collective-permute-start(f32[32,128]{1,0:T(8,128)S(1)} %get-tuple-element.56), channel_id=1, source_target_pairs={{0,3},{1,2},{2,1},{3,0},{4,7},{5,6},{6,5},{7,4},{8,11},{9,10},{10,... | collective-permute-start | bytes 49160 | tf_op jit(solution)/shard_map/ppermute | solution.py:35
  68.1 0.0 collective-permute-start.15
  68.1 0.5 collective-permute-start.14
  68.6 0.9 %collective-permute-done.16 = f32[32,128]{1,0:T(8,128)S(1)} collective-permute-done((f32[32,128]{1,0:T(8,128)S(1)}, f32[32,128]{1,0:T(8,128)S(1)}, u32[]{:S(2)}, u32[]{:S(2)}) %collective-permute-start.16) | collective-permute-done | bytes 16416 | tf_op jit(solution)/shard_map/ppermute | solution.py:35
  69.5 1.2 %collective-permute-done.15 = f32[32,128]{1,0:T(8,128)S(1)} collective-permute-done((f32[32,128]{1,0:T(8,128)S(1)}, f32[32,128]{1,0:T(8,128)S(1)}, u32[]{:S(2)}, u32[]{:S(2)}) %collective-permute-start.15) | collective-permute-done | bytes 16416 | tf_op jit(solution)/shard_map/ppermute | solution.py:35
  70.7 0.0 collective-permute-done.14
  70.7 3.0 %norm.1 = bf16[4096,512]{1,0:T(8,128)(2,1)} custom-call(bf16[4096,512]{1,0:T(8,128)(2,1)S(1)} %get-tuple-element.55.refs_0_, f32[32,128]{1,0:T(8,128)S(1)} %add_add_fusion.refs_1_, f32[1,512]{1,0:T(1,128)S(1)} %bitcast.12), custom_call_target="tpu_custom_call" | custom-call | flops 6291456 | bytes 8388608 | tf_op jit(solution)/shard_map/norm/pallas_call | solution.py:470
  (21 shorter events, 0.0 us)
Async XLA Ops:
  0.0 6.1 %copy-start.8 = (f32[8]{0:T(128)S(1)}, f32[8]{0:T(128)}, u32[]{:S(2)}) copy-start(f32[8]{0:T(128)} %param.16) | copy-start | bytes 100
  0.0 6.1 %copy-start.7 = (f32[8]{0:T(128)S(1)}, f32[8]{0:T(128)}, u32[]{:S(2)}) copy-start(f32[8]{0:T(128)} %param.15) | copy-start | bytes 100
  0.0 6.1 %copy-start.6 = (f32[8]{0:T(128)S(1)}, f32[8]{0:T(128)}, u32[]{:S(2)}) copy-start(f32[8]{0:T(128)} %param.14) | copy-start | bytes 100
  0.0 6.1 %copy-start.4 = (f32[4096,8]{0,1:T(8,128)S(1)}, f32[4096,8]{0,1:T(8,128)}, u32[]{:S(2)}) copy-start(f32[4096,8]{0,1:T(8,128)} %param.13) | copy-start | bytes 393220
  0.0 7.4 %copy-start.5 = (bf16[4,512]{1,0:T(4,128)(2,1)S(1)}, bf16[4,512]{1,0:T(4,128)(2,1)}, u32[]{:S(2)}) copy-start(bf16[4,512]{1,0:T(4,128)(2,1)} %refs_2_.3) | copy-start | bytes 12292
  0.0 14.8 %collective-permute-start.3 = (bf16[64,4096]{1,0:T(8,128)(2,1)}, bf16[64,4096]{1,0:T(8,128)(2,1)S(1)}, u32[]{:S(2)}, u32[]{:S(2)}) collective-permute-start(bf16[64,4096]{1,0:T(8,128)(2,1)} %bitcast.8), channel_id=1, source_target_pairs={{0,2},{1,3},{2,0},{3,1},{4,6},{5,7},{6,4},{7,5},{8,10},{9,11},{10,... | collective-permute-start | bytes 1572872 | tf_op jit(solution)/shard_map/ppermute | solution.py:35
  2.2 19.8 %collective-permute-start.1 = (bf16[64,4096]{1,0:T(8,128)(2,1)}, bf16[64,4096]{1,0:T(8,128)(2,1)S(1)}, u32[]{:S(2)}, u32[]{:S(2)}) collective-permute-start(bf16[64,4096]{1,0:T(8,128)(2,1)} %bitcast.9), channel_id=1, source_target_pairs={{0,1},{1,0},{2,3},{3,2},{4,5},{5,4},{6,7},{7,6},{8,9},{9,8},{10,11... | collective-permute-start | bytes 1572872 | tf_op jit(solution)/shard_map/ppermute | solution.py:35
  4.8 9.2 %collective-permute-start = (bf16[144,128]{1,0:T(8,128)(2,1)}, bf16[144,128]{1,0:T(8,128)(2,1)S(1)}, u32[]{:S(2)}, u32[]{:S(2)}) collective-permute-start(bf16[144,128]{1,0:T(8,128)(2,1)} %tails.1), channel_id=1, source_target_pairs={{0,32},{32,64},{64,96},{96,128},{128,160},{160,192},{192,224},{224... | collective-permute-start | bytes 110600 | tf_op jit(solution)/shard_map/ppermute | solution.py:31
  7.4 2.2 %copy-start = (bf16[4096,512]{1,0:T(8,128)(2,1)S(1)}, bf16[4096,512]{1,0:T(8,128)(2,1)}, u32[]{:S(2)}) copy-start(bf16[4096,512]{1,0:T(8,128)(2,1)} %refs_1_.3) | copy-start | bytes 12582916
  14.0 6.1 %copy-start.1 = (bf16[4096,64]{0,1:T(8,128)(2,1)S(1)}, bf16[4096,64]{0,1:T(8,128)(2,1)}, u32[]{:S(2)}) copy-start(bf16[4096,64]{0,1:T(8,128)(2,1)} %param.12) | copy-start | bytes 1572868
  14.0 7.6 %collective-permute-start.4 = (bf16[144,128]{1,0:T(8,128)(2,1)S(1)}, bf16[144,128]{1,0:T(8,128)(2,1)S(1)}, u32[]{:S(2)}, u32[]{:S(2)}) collective-permute-start(bf16[144,128]{1,0:T(8,128)(2,1)S(1)} %collective-permute-done.halo_ref.refs_5_), channel_id=1, source_target_pairs={{0,2},{1,3},{2,0},{3,1},{4,6},{5,7},{6,4},{7,5},{8,10},{9,11},{10,... | collective-permute-start | bytes 110600 | tf_op jit(solution)/shard_map/ppermute | solution.py:35
  14.3 7.6 %collective-permute-start.2 = (bf16[144,128]{1,0:T(8,128)(2,1)S(1)}, bf16[144,128]{1,0:T(8,128)(2,1)S(1)}, u32[]{:S(2)}, u32[]{:S(2)}) collective-permute-start(bf16[144,128]{1,0:T(8,128)(2,1)S(1)} %collective-permute-done.halo_ref.refs_5_), channel_id=1, source_target_pairs={{0,1},{1,0},{2,3},{3,2},{4,5},{5,4},{6,7},{7,6},{8,9},{9,8},{10,11... | collective-permute-start | bytes 110600 | tf_op jit(solution)/shard_map/ppermute | solution.py:35
  14.8 10.0 %collective-permute-start.5 = (bf16[64,4096]{1,0:T(8,128)(2,1)S(1)}, bf16[64,4096]{1,0:T(8,128)(2,1)S(1)}, u32[]{:S(2)}, u32[]{:S(2)}) collective-permute-start(bf16[64,4096]{1,0:T(8,128)(2,1)S(1)} %collective-permute-done.3.p_ref), channel_id=1, source_target_pairs={{0,1},{1,0},{2,3},{3,2},{4,5},{5,4},{6,7},{7,6},{8,9},{9,8},{10,11... | collective-permute-start | bytes 1572872 | tf_op jit(solution)/shard_map/ppermute | solution.py:35
  21.6 3.2 %collective-permute-start.6 = (bf16[144,128]{1,0:T(8,128)(2,1)S(1)}, bf16[144,128]{1,0:T(8,128)(2,1)S(1)}, u32[]{:S(2)}, u32[]{:S(2)}) collective-permute-start(bf16[144,128]{1,0:T(8,128)(2,1)S(1)} %collective-permute-done.4.halo_ref), channel_id=1, source_target_pairs={{0,1},{1,0},{2,3},{3,2},{4,5},{5,4},{6,7},{7,6},{8,9},{9,8},{10,11... | collective-permute-start | bytes 110600 | tf_op jit(solution)/shard_map/ppermute | solution.py:35
  28.8 9.0 %collective-permute-start.8 = (bf16[144,512]{1,0:T(8,128)(2,1)S(1)}, bf16[144,512]{1,0:T(8,128)(2,1)S(1)}, u32[]{:S(2)}, u32[]{:S(2)}) collective-permute-start(bf16[144,512]{1,0:T(8,128)(2,1)S(1)} %get-tuple-element.42), channel_id=1, source_target_pairs={{0,224},{32,0},{64,32},{96,64},{128,96},{160,128},{192,160},{224,1... | collective-permute-start | bytes 442376 | tf_op jit(solution)/shard_map/ppermute | solution.py:31
  34.6 5.8 %collective-permute-start.7 = (bf16[144,512]{1,0:T(8,128)(2,1)S(1)}, bf16[144,512]{1,0:T(8,128)(2,1)S(1)}, u32[]{:S(2)}, u32[]{:S(2)}) collective-permute-start(bf16[144,512]{1,0:T(8,128)(2,1)S(1)} %get-tuple-element.42), channel_id=1, source_target_pairs={{0,32},{32,64},{64,96},{96,128},{128,160},{160,192},{192,224},{224... | collective-permute-start | bytes 442376 | tf_op jit(solution)/shard_map/ppermute | solution.py:31
  40.5 5.9 %collective-permute-start.9 = (bf16[144,512]{1,0:T(8,128)(2,1)S(1)}, bf16[144,512]{1,0:T(8,128)(2,1)S(1)}, u32[]{:S(2)}, u32[]{:S(2)}) collective-permute-start(bf16[144,512]{1,0:T(8,128)(2,1)S(1)} %collective-permute-done.7.refs_11_), channel_id=1, source_target_pairs={{0,32},{32,64},{64,96},{96,128},{128,160},{160,192},{192,224},{224... | collective-permute-start | bytes 442376 | tf_op jit(solution)/shard_map/ppermute | solution.py:31
  40.5 5.9 %collective-permute-start.10 = (bf16[144,512]{1,0:T(8,128)(2,1)S(1)}, bf16[144,512]{1,0:T(8,128)(2,1)S(1)}, u32[]{:S(2)}, u32[]{:S(2)}) collective-permute-start(bf16[144,512]{1,0:T(8,128)(2,1)S(1)} %collective-permute-done.8.refs_17_), channel_id=1, source_target_pairs={{0,224},{32,0},{64,32},{96,64},{128,96},{160,128},{192,160},{224,1... | collective-permute-start | bytes 442376 | tf_op jit(solution)/shard_map/ppermute | solution.py:31
  46.4 6.0 %collective-permute-start.11 = (bf16[144,512]{1,0:T(8,128)(2,1)S(1)}, bf16[144,512]{1,0:T(8,128)(2,1)S(1)}, u32[]{:S(2)}, u32[]{:S(2)}) collective-permute-start(bf16[144,512]{1,0:T(8,128)(2,1)S(1)} %collective-permute-done.9.refs_12_), channel_id=1, source_target_pairs={{0,32},{32,64},{64,96},{96,128},{128,160},{160,192},{192,224},{224... | collective-permute-start | bytes 442376 | tf_op jit(solution)/shard_map/ppermute | solution.py:31
  46.5 5.9 %collective-permute-start.12 = (bf16[144,512]{1,0:T(8,128)(2,1)S(1)}, bf16[144,512]{1,0:T(8,128)(2,1)S(1)}, u32[]{:S(2)}, u32[]{:S(2)}) collective-permute-start(bf16[144,512]{1,0:T(8,128)(2,1)S(1)} %collective-permute-done.10.refs_16_), channel_id=1, source_target_pairs={{0,224},{32,0},{64,32},{96,64},{128,96},{160,128},{192,160},{224,1... | collective-permute-start | bytes 442376 | tf_op jit(solution)/shard_map/ppermute | solution.py:31
  52.3 5.3 %copy-start.3 = (bf16[4096,512]{1,0:T(8,128)(2,1)S(1)}, bf16[4096,512]{1,0:T(8,128)(2,1)}, u32[]{:S(2)}) copy-start(bf16[4096,512]{1,0:T(8,128)(2,1)} %refs_6_.1) | copy-start | bytes 12582916
  52.4 5.3 %collective-permute-start.13 = (bf16[144,512]{1,0:T(8,128)(2,1)S(1)}, bf16[144,512]{1,0:T(8,128)(2,1)S(1)}, u32[]{:S(2)}, u32[]{:S(2)}) collective-permute-start(bf16[144,512]{1,0:T(8,128)(2,1)S(1)} %collective-permute-done.11.refs_13_), channel_id=1, source_target_pairs={{0,32},{32,64},{64,96},{96,128},{128,160},{160,192},{192,224},{224... | collective-permute-start | bytes 442376 | tf_op jit(solution)/shard_map/ppermute | solution.py:31
  57.6 13.1 %copy-start.2 = (f32[512]{0:T(512)S(1)}, f32[512]{0:T(512)}, u32[]{:S(2)}) copy-start(f32[512]{0:T(512)} %param.19) | copy-start | bytes 6148
  62.6 6.9 %collective-permute-start.16 = (f32[32,128]{1,0:T(8,128)S(1)}, f32[32,128]{1,0:T(8,128)S(1)}, u32[]{:S(2)}, u32[]{:S(2)}) collective-permute-start(f32[32,128]{1,0:T(8,128)S(1)} %get-tuple-element.56), channel_id=1, source_target_pairs={{0,3},{1,2},{2,1},{3,0},{4,7},{5,6},{6,5},{7,4},{8,11},{9,10},{10,... | collective-permute-start | bytes 49160 | tf_op jit(solution)/shard_map/ppermute | solution.py:35
  68.1 2.6 %collective-permute-start.15 = (f32[32,128]{1,0:T(8,128)S(1)}, f32[32,128]{1,0:T(8,128)S(1)}, u32[]{:S(2)}, u32[]{:S(2)}) collective-permute-start(f32[32,128]{1,0:T(8,128)S(1)} %get-tuple-element.56), channel_id=1, source_target_pairs={{0,2},{1,3},{2,0},{3,1},{4,6},{5,7},{6,4},{7,5},{8,10},{9,11},{10,... | collective-permute-start | bytes 49160 | tf_op jit(solution)/shard_map/ppermute | solution.py:35
  68.1 2.6 %collective-permute-start.14 = (f32[32,128]{1,0:T(8,128)S(1)}, f32[32,128]{1,0:T(8,128)S(1)}, u32[]{:S(2)}, u32[]{:S(2)}) collective-permute-start(f32[32,128]{1,0:T(8,128)S(1)} %get-tuple-element.56), channel_id=1, source_target_pairs={{0,1},{1,0},{2,3},{3,2},{4,5},{5,4},{6,7},{7,6},{8,9},{9,8},{10,11... | collective-permute-start | bytes 49160 | tf_op jit(solution)/shard_map/ppermute | solution.py:35

commit v2 on v1

--- a/solution.py
+++ b/solution.py
@@ -16,7 +16,7 @@
 VMEM_CAP = 8 * 1024 * 1024
 LOCAL_UNROLL = 8
 CARRY_UNROLL = 8
-CONV_UNROLL = (5, 8)
+CONV_UNROLL = (7, 8)
 STATE_UNROLL = 8
 
 
@@ -29,6 +29,16 @@
 def rotated(x, axis, by):
     count = lax.axis_size(axis)
     return lax.ppermute(x, axis, [(i, (i + by) % count) for i in range(count)])
+
+
+def opposed(x, by):
+    ctx, head = lax.axis_size("ctx"), lax.axis_size("head")
+    pairs = []
+    for i in range(ctx):
+        for j in range(head):
+            to = (i + (by if j % 2 == 0 else -by)) % ctx
+            pairs.append((i * head + j, to * head + j))
+    return lax.ppermute(x, ("ctx", "head"), pairs)
 
 
 def swapped(value, axis, mask):
@@ -104,38 +114,66 @@
     )(x, proj_t, taps)
 
 
-def proj_conv_kernel(flag_ref, p_ref, halo_ref, o_ref):
-    rows, tokens = p_ref.shape
-    group = 16
-    lane = iota((group, BLK), 1)
-    at = halo_ref.shape[0] - 16
-    weights = jnp.transpose(0.5 * halo_ref[at : at + 16, :].astype(F32)[0:8])
-    for lo in range(0, rows, group):
-        span = slice(lo, lo + group)
-        taps = [jnp.broadcast_to(weights[span, k : k + 1], (group, BLK)) for k in range(4)]
-        halo = jnp.where(flag_ref[1] == 0, 0.0, halo_ref[span, :].astype(F32))
-        prev = [pltpu.roll(halo, k, 1) for k in (1, 2, 3)]
-        for i in range(tokens // BLK):
-            cur = p_ref[span, i * BLK : (i + 1) * BLK].astype(F32)
-            now = [pltpu.roll(cur, k, 1) for k in (1, 2, 3)]
-            h = taps[3] * cur
-            for k in (1, 2, 3):
-                h = h + taps[3 - k] * jnp.where(lane < k, prev[k - 1], now[k - 1])
-            o_ref[span, i * BLK : (i + 1) * BLK] = half_silu(h).astype(BF16)
-            prev = now
-
-
-def proj_conv(flag, proj_t, halo):
-    rows, tokens = proj_t.shape
-    return pl.pallas_call(
-        proj_conv_kernel,
-        in_specs=specs(3, 1),
+def proj_conv_kernel(
+    wanted, flag_ref, own_ref, near_ref, far_ref, cross_ref, h0_ref, h1_ref, h2_ref, h3_ref, o_ref,
+    tap_ref
+):
+    half, tokens = own_ref.shape
+    here = flag_ref[0] == wanted
+
+    def raw(at):
+        return jnp.where(
+            here,
+            jnp.concatenate([own_ref[:, at], near_ref[:, at]], axis=0),
+            jnp.concatenate([far_ref[:, at], cross_ref[:, at]], axis=0),
+        )
+
+    def of_halo(rows):
+        return (
+            jnp.where(here, h0_ref[rows, :], h2_ref[rows, :]),
+            jnp.where(here, h1_ref[rows, :], h3_ref[rows, :]),
+        )
+
+    at = h0_ref.shape[0] - 16
+    for q, weights in enumerate(of_halo(slice(at, at + 16))):
+        columns = jnp.transpose(0.5 * weights.astype(F32)[0:8])
+        for k in range(4):
+            tap_ref[k, q * half : (q + 1) * half, :] = jnp.broadcast_to(
+                columns[0:half, k : k + 1], (half, BLK)
+            )
+    before = jnp.concatenate(of_halo(slice(0, half)), axis=0)
+    before = jnp.where(flag_ref[1] == 0, jnp.zeros_like(before), before)
+    src, dst = iota((2 * BLK, 4 * BLK), 0), iota((2 * BLK, 4 * BLK), 1)
+    shift = (src == BLK + dst % BLK - dst // BLK).astype(BF16)
+    for i in range(tokens // BLK):
+        cur = slice(i * BLK, (i + 1) * BLK)
+        if i == 0:
+            window = jnp.concatenate([before, raw(cur)], axis=1)
+        else:
+            window = raw(slice((i - 1) * BLK, (i + 1) * BLK))
+        moved = jnp.dot(window, shift, preferred_element_type=F32)
+        h = tap_ref[3] * moved[:, 0:BLK]
+        for k in (1, 2, 3):
+            h = h + tap_ref[3 - k] * moved[:, k * BLK : (k + 1) * BLK]
+        o_ref[:, cur] = half_silu(h).astype(BF16)
+
+
+def proj_conv(flag, raws, halos, wanted):
+    half, tokens = raws[0].shape
+
+    def kernel(*refs):
+        proj_conv_kernel(wanted, *refs)
+
+    return pl.pallas_call(
+        kernel,
+        in_specs=specs(9, 1),
         out_specs=specs(1)[0],
-        out_shape=jax.ShapeDtypeStruct((rows, tokens), BF16),
-        compiler_params=params(),
-        cost_estimate=cost(rows * tokens * 4000, rows * tokens * 4, rows * tokens),
+        out_shape=jax.ShapeDtypeStruct((2 * half, tokens), BF16),
+        scratch_shapes=[pltpu.VMEM((4, 2 * half, BLK), F32)],
+        compiler_params=params(),
+        cost_estimate=cost(half * tokens * 4000, half * tokens * 6, half * tokens * 2),
         name="proj_conv",
-    )(flag, proj_t, halo)
+    )(flag, *raws, *halos)
 
 
 def decay_kernel(
@@ -265,14 +303,55 @@
     )(flag, x, taps, run, step, *([halo] if part == 0 else []))
 
 
-def pick_quarters(flag_ref, quarter_refs, at):
-    own, near, far, cross = (ref[:, at] for ref in quarter_refs)
-    here = jnp.concatenate([own, near], axis=0)
-    there = jnp.concatenate([far, cross], axis=0)
-    return here, there, flag_ref[0] == 0
-
-
-def state_kernel(flag_ref, own_ref, near_ref, far_ref, cross_ref, tot_ref, *rest):
+def write_log(msg_ref, log):
+    high = log.astype(BF16).astype(F32)
+    mid = (log - high).astype(BF16).astype(F32)
+    low = (log - high) - mid
+    row = iota((16, log.shape[1]), 0)
+    parts = jnp.where(row == 0, high, jnp.where(row == 1, mid, jnp.where(row == 2, low, 0.0)))
+    msg_ref[STATE : STATE + 16, :] = parts.astype(BF16)
+
+
+def read_log(msg_ref):
+    parts = msg_ref[STATE : STATE + 16, :].astype(F32)
+    return (parts[0:1] + parts[1:2]) + parts[2:3]
+
+
+def merge_kernel(level, devices, flag_ref, mine_ref, got_ref, o_ref):
+    pos = flag_ref[1]
+    even = flag_ref[2] == 0
+    reach = 1 if level == 1 else 3
+    keep_even = pos >= level
+    keep_odd = pos + reach < devices
+    if level == 2:
+        keep_odd = keep_odd | (pos == devices - 1)
+    keep = jnp.where(jnp.where(even, keep_even, keep_odd), 1.0, 0.0)
+    mine_log, got_log = read_log(mine_ref), read_log(got_ref)
+    early_log = keep * jnp.where(even, got_log, mine_log)
+    late_log = jnp.where(even, mine_log, got_log)
+    factor = keep * jnp.exp2(late_log)
+    mine, got = mine_ref[0:STATE, :].astype(F32), got_ref[0:STATE, :].astype(F32)
+    state = jnp.where(even, mine, got) + factor * jnp.where(even, got, mine)
+    o_ref[0:STATE, :] = state.astype(BF16)
+    write_log(o_ref, late_log + early_log)
+
+
+def merge(flag, mine, got, level, devices):
+    def kernel(*refs):
+        merge_kernel(level, devices, *refs)
+
+    return pl.pallas_call(
+        kernel,
+        in_specs=specs(3, 1),
+        out_specs=specs(1)[0],
+        out_shape=jax.ShapeDtypeStruct(mine.shape, BF16),
+        compiler_params=params(),
+        cost_estimate=cost(mine.size * 4, mine.size * 6),
+        name="merge",
+    )(flag, mine, got)
+
+
+def state_kernel(b_ref, tot_ref, *rest):
     s_ref, msg_ref, now_ref = rest[-3:]
     v_refs = rest[:-3]
     chans = s_ref.shape[2]
@@ -283,30 +362,21 @@
 
         @pl.loop(0, count, unroll=STATE_UNROLL)
         def _(i):
-            here, there, local_b = pick_quarters(
-                flag_ref, (own_ref, near_ref, far_ref, cross_ref), block_at(base + i)
-            )
-            b = jnp.where(local_b, here, there)
+            b = b_ref[:, block_at(base + i)]
             add = jnp.dot(b, v_ref[block_at(i), :], preferred_element_type=F32)
             now = now_ref[...]
             s_ref[base + i] = now.astype(BF16)
             now_ref[...] = jnp.exp2(tot_ref[pl.ds(base + i, 1), :]) * now + add
 
-    log = jnp.sum(tot_ref[...], axis=0, keepdims=True)
-    high = log.astype(BF16).astype(F32)
-    mid = (log - high).astype(BF16).astype(F32)
-    low = (log - high) - mid
-    row = iota((16, chans), 0)
-    parts = jnp.where(row == 0, high, jnp.where(row == 1, mid, jnp.where(row == 2, low, 0.0)))
     msg_ref[0:STATE, :] = now_ref[...].astype(BF16)
-    msg_ref[STATE : STATE + 16, :] = parts.astype(BF16)
-
-
-def states(flag, weighted, quarters, totals):
+    write_log(msg_ref, jnp.sum(tot_ref[...], axis=0, keepdims=True))
+
+
+def states(weighted, b_t, totals):
     blocks, chans = totals.shape
     return pl.pallas_call(
         state_kernel,
-        in_specs=specs(6 + len(weighted), 1),
+        in_specs=specs(2 + len(weighted)),
         out_specs=tuple(specs(2)),
         out_shape=(
             jax.ShapeDtypeStruct((blocks, STATE, chans), BF16),
@@ -316,12 +386,11 @@
         compiler_params=params(),
         cost_estimate=cost(blocks * BLK * chans * 2000, blocks * BLK * chans * 4),
         name="states",
-    )(flag, *quarters, totals, *weighted)
+    )(b_t, totals, *weighted)
 
 
 def local_kernel(
-    base, offset, flag_ref, x_ref, own_ref, near_ref, far_ref, cross_ref, s_ref, run_ref, step_ref,
-    skip_ref, o_ref
+    base, offset, x_ref, b_ref, c_ref, s_ref, run_ref, step_ref, skip_ref, o_ref
 ):
     tokens, chans = o_ref.shape
     heads = run_ref.shape[0]
@@ -331,12 +400,8 @@
     @pl.loop(0, tokens // BLK, unroll=LOCAL_UNROLL)
     def _(i):
         at = block_at(base + i)
-        here, there, local_b = pick_quarters(
-            flag_ref, (own_ref, near_ref, far_ref, cross_ref), at
-        )
-        c = jnp.transpose(jnp.where(local_b, there, here))
-        b = jnp.where(local_b, here, there)
-        gram = jnp.dot(c, b, preferred_element_type=F32)
+        c = jnp.transpose(c_ref[:, at])
+        gram = jnp.dot(c, b_ref[:, at], preferred_element_type=F32)
         gram = jnp.where(causal, gram, 0.0).astype(BF16)
         run = run_ref[:, at]
         run_t = jnp.transpose(run)
@@ -361,7 +426,7 @@
             o_ref[block_at(i), lanes] = out.astype(BF16)
 
 
-def local(flag, x_conv, quarters, entering, run, step, skip, part, parts, offset):
+def local(x_conv, b_t, c_t, entering, run, step, skip, part, parts, offset):
     heads, tokens = run.shape
     chans = x_conv.shape[1]
     here = tokens // parts
@@ -371,28 +436,36 @@
 
     return pl.pallas_call(
         kernel,
-        in_specs=specs(10, 1),
+        in_specs=specs(7),
         out_specs=specs(1)[0],
         out_shape=jax.ShapeDtypeStruct((here, chans), BF16),
         compiler_params=params(),
         cost_estimate=cost(8000 * here * chans, here * chans * 6, here * heads * BLK * 2),
         name="local",
-    )(flag, x_conv, *quarters, entering, run, step, skip)
-
-
-def carry_kernel(nloc, flag_ref, own_ref, near_ref, far_ref, cross_ref, abs_ref, z_ref, *rest):
-    l_refs, msgs = rest[:nloc], rest[nloc:-4]
-    g_ref, q_ref, s_ref, acc_ref = rest[-4:]
+    )(x_conv, b_t, c_t, entering, run, step, skip)
+
+
+def carry_kernel(nloc, devices, flag_ref, c_ref, abs_ref, z_ref, *rest):
+    l_refs, msgs = rest[:nloc], rest[nloc:-3]
+    g_ref, q_ref, s_ref = rest[-3:]
     chans = g_ref.shape[1]
     heads = abs_ref.shape[0]
-    gone = jnp.zeros((1, chans), F32)
-    for d, msg in enumerate(msgs, 1):
-        factor = jnp.where(flag_ref[1] >= d, jnp.exp2(gone), 0.0)
-        term = factor * msg[0:STATE, :].astype(F32)
-        acc_ref[...] = term if d == 1 else acc_ref[...] + term
-        parts = msg[STATE : STATE + 16, :].astype(F32)
-        gone = gone + ((parts[0:1] + parts[1:2]) + parts[2:3])
-    s_ref[...] = acc_ref[...].astype(BF16)
+    pos = flag_ref[1]
+    even = flag_ref[2] == 0
+    near_ref, mid_ref, wide_ref = msgs
+    one = jnp.where(even, pos >= 1, pos + 1 >= devices)
+    two = jnp.where(even, pos >= 2, pos + 3 >= devices)
+    four = jnp.where(even, pos >= 4, pos >= 1)
+    first_ok = jnp.where(jnp.where(even, four, one), 1.0, 0.0)
+    mid_ok = jnp.where(two, 1.0, 0.0)
+    last_ok = jnp.where(jnp.where(even, one, four), 1.0, 0.0)
+    near_log, far_log = read_log(near_ref), read_log(wide_ref)
+    last_fall = jnp.exp2(last_ok * jnp.where(even, near_log, far_log))
+    mid_fall = jnp.exp2(mid_ok * read_log(mid_ref)) * last_fall * first_ok
+    last_fall = last_fall * mid_ok
+    near, wide = near_ref[0:STATE, :].astype(F32), wide_ref[0:STATE, :].astype(F32)
+    total = last_ok * jnp.where(even, near, wide) + mid_fall * jnp.where(even, wide, near)
+    s_ref[...] = (total + last_fall * mid_ref[0:STATE, :].astype(F32)).astype(BF16)
     spread = head_spread(heads, chans)
     done = 0
     for l_ref in l_refs:
@@ -403,10 +476,7 @@
         @pl.loop(0, count, unroll=CARRY_UNROLL)
         def _(i):
             at = block_at(first + i)
-            here, there, local_b = pick_quarters(
-                flag_ref, (own_ref, near_ref, far_ref, cross_ref), at
-            )
-            c = jnp.transpose(jnp.where(local_b, there, here))
+            c = jnp.transpose(c_ref[:, at])
             wide = lax.dot_general(
                 jnp.exp2(abs_ref[:, at]).astype(BF16),
                 spread,
@@ -425,18 +495,18 @@
             q_ref[pl.ds(first + i, 1), :] = jnp.sum(jnp.transpose(folded), axis=0, keepdims=True)
 
 
-def carry(flag, locs, gate, quarters, whole, msgs):
+def carry(flag, locs, gate, c_t, whole, msgs, devices):
     heads, tokens = whole.shape
     chans = locs[0].shape[1]
 
     def kernel(*refs):
-        carry_kernel(len(locs), *refs)
+        carry_kernel(len(locs), devices, *refs)
 
     return pl.pallas_call(
         kernel,
-        in_specs=specs(7 + len(locs) + len(msgs), 1),
+        in_specs=specs(4 + len(locs) + len(msgs), 1),
         out_specs=tuple(specs(2)),
-        scratch_shapes=[pltpu.VMEM((STATE, chans), BF16), pltpu.VMEM((STATE, chans), F32)],
+        scratch_shapes=[pltpu.VMEM((STATE, chans), BF16)],
         out_shape=(
             jax.ShapeDtypeStruct((tokens, chans), BF16),
             jax.ShapeDtypeStruct((tokens // BLK, BLK), F32),
@@ -444,7 +514,7 @@
         compiler_params=params(),
         cost_estimate=cost(4000 * tokens * chans, tokens * chans * 6, tokens * chans),
         name="carry",
-    )(flag, *quarters, whole, gate, *locs, *msgs)
+    )(flag, c_t, whole, gate, *locs, *msgs)
 
 
 def norm_kernel(width, g_ref, q_ref, gain_ref, o_ref):
@@ -461,7 +531,7 @@
             o_ref[at, lanes] = (g * column * gain_ref[:, lanes]).astype(BF16)
 
 
-def norm(gated, squares, gain, width, rows=1024):
+def norm(gated, squares, gain, width, rows=2048):
     tokens, chans = gated.shape
 
     def kernel(*refs):
@@ -487,51 +557,56 @@
     head_pos = lax.axis_index("head")
     ctx_pos = lax.axis_index("ctx")
     count = lax.axis_size("ctx")
-    flag = jnp.stack([head_pos >> 1 & 1, ctx_pos]).astype(jnp.int32)
+    flag = jnp.stack([head_pos >> 1 & 1, ctx_pos, head_pos & 1]).astype(jnp.int32)
 
     proj_t = state_proj.T
     far_raw = swapped(proj_t, "head", 2)
     near_raw = swapped(proj_t, "head", 1)
-    halo = rotated(tails(x_stream, proj_t, conv_proj), "ctx", 1)
-    run, whole, step, totals, skip = decays(dt_raw.T, dt_bias, a_log, skip_d, chans)
-    halves = 2
-    x_two, v_two, mark = chan_conv(flag, x_stream, conv_x, run, step, None, 1, halves)
+    ends = tails(x_stream, proj_t, conv_proj)
+    halo = rotated(ends, "ctx", 1)
+    run, whole, step, totals, skip = decays(after(dt_raw.T, ends), dt_bias, a_log, skip_d, chans)
+
+    def conv(part, *needs):
+        return chan_conv(after(flag, *needs), x_stream, conv_x, run, step, halo, part, 4)
+
+    x3, v3, mark = conv(3)
     halo = after(halo, mark)
     halo_far = swapped(halo, "head", 2)
     halo_near = swapped(halo, "head", 1)
-    far_raw = after(far_raw, mark)
+    x2, v2, mark = conv(2, halo, mark)
+    far_raw, halo_far = lax.optimization_barrier((far_raw, halo_far, mark))[:2]
     cross_raw = swapped(far_raw, "head", 1)
     halo_cross = swapped(halo_far, "head", 1)
-    x_one, v_one, mark = chan_conv(flag, x_stream, conv_x, run, step, halo, 0, halves)
-    own = proj_conv(flag, proj_t, halo)
-    near = proj_conv(flag, near_raw, halo_near)
-    far = proj_conv(flag, after(far_raw, mark, own, near), halo_far)
-    cross = proj_conv(flag, after(cross_raw, far), halo_cross)
-    quarters = (own, near, far, cross)
-
-    entering, message = states(flag, (v_one, v_two), quarters, totals)
-
-    up = down = message
-    ahead, behind, locs = [], [], []
-    parts = count // 2
-    per = parts // halves
-    for at in range(parts):
-        up = rotated(up, "ctx", 1)
-        ahead.append(up)
-        if at + 1 < count - parts:
-            down = rotated(down, "ctx", -1)
-            behind.append(down)
-        piece = local(
-            flag, (x_one, x_two)[at // per], quarters, entering, run, step, skip, at, parts,
-            at % per * (tokens // parts // BLK),
+    x1, v1, mark = conv(1, far_raw, halo_far)
+    x0, v0, mark = conv(0, mark)
+    raws = (proj_t, near_raw, far_raw, after(cross_raw, mark))
+    halos = (halo, halo_near, halo_far, halo_cross)
+    b_t = proj_conv(flag, raws, halos, 0)
+    entering, message = states((v0, v1, v2, v3), b_t, totals)
+    c_t = proj_conv(after(flag, message), raws, halos, 1)
+
+    locs = []
+
+    def piece(at, *needs):
+        x_conv = (x0, x1, x2, x3)[at]
+        locs.append(
+            local(x_conv, b_t, c_t, entering, after(run, *needs), step, skip, at, 4, 0)
         )
-        if at + 1 < parts:
-            up, down, piece = lax.optimization_barrier((up, down, piece))
-        locs.append(piece)
-    msgs = ahead + behind[::-1]
+        return locs[-1]
+
+    one = opposed(message, 1)
+    pair = merge(flag, message, after(one, c_t), 1, count)
+    two = opposed(pair, 2)
+    piece(0, pair)
+    last = piece(1, pair)
+    quad = merge(flag, pair, after(two, last), 2, count)
+    four = opposed(quad, 4)
+    piece(2, quad)
+    last = piece(3, quad)
+    msgs = (one, two, after(four, last))
 
     width = HEADS // GROUPS * (chans // heads)
-    gated, squares = carry(flag, locs, gate_z, quarters, whole, msgs)
+    gated, squares = carry(flag, locs, gate_z, c_t, whole, msgs, count)
     squares = (squares + swapped(squares, "head", 1)) + (
         swapped(squares, "head", 2) + swapped(squares, "head", 3)
     )

time: 73.9 us -> 68.7 us (0.930)
  Pallas kernels: 40.8 us -> 36.1 us
  starting transfers between devices: 23.7 us -> 22.1 us
  waiting for transfers between devices: 6.73 us -> 7.72 us
    ppermute x8 -> x1, starting transfers between devices: 12.7 us -> 1.64 us  [rotated(): return lax.ppermute(x, axis, [(i, (i + by) % count) for i in range(count)])]
    ppermute x0 -> x3, starting transfers between devices: none -> 10.2 us  [opposed(): return lax.ppermute(x, ('ctx', 'head'), pairs)]
    ppermute x8 -> x1, waiting for transfers between devices: 4.62 us -> 0.01 us  [rotated(): return lax.ppermute(x, axis, [(i, (i + by) % count) for i in range(count)])]
    ppermute x0 -> x3, waiting for transfers between devices: none -> 4.13 us  [opposed(): return lax.ppermute(x, ('ctx', 'head'), pairs)]
    pallas_call x10, Pallas kernels: 26 us -> 22.2 us  [the longest x4 10.7 us: local(): pl.pallas_call(kernel, in_specs=specs(7), out_specs=specs(1)[0], out_shap...]
    ppermute x9, waiting for transfers between devices: 2.11 us -> 3.58 us  [swapped(): lax.ppermute(value, axis, [(i, i ^ mask) for i in range(lax.axis_size(axi...]
    ppermute x9, starting transfers between devices: 11 us -> 10.3 us  [swapped(): lax.ppermute(value, axis, [(i, i ^ mask) for i in range(lax.axis_size(axi...]
    pallas_call x2 -> x4, Pallas kernels: 9.28 us -> 8.75 us  [chan_conv(): pl.pallas_call(kernel, in_specs=specs(5 + (part == 0), 1), out_specs=tupl...]
  transfers between devices with their start and end apart: 17 -> 13, of which waited for: 4 -> 4; matrix products, arithmetic and copies ran while one was open for 0% -> 0% of each run, Pallas kernels for 39% -> 35%
where the time goes in v2:
time: 68.7 us; the launch traced here: 68.5 us
  Pallas kernels  36.1 us (53%)
  starting transfers between devices  22.1 us (32%)
  waiting for transfers between devices  7.72 us (11%)
  local copies, waits for them, and re-layouts  2.23 us (3%)
    pallas_call x4, Pallas kernels, local(): pl.pallas_call(kernel, in_specs=specs(7), out_specs=specs(1)[0], out_shap...  10.7 us
    ppermute x9, starting transfers between devices, swapped(): lax.ppermute(value, axis, [(i, i ^ mask) for i in range(lax.axis_size(axi...  10.3 us
    ppermute x3, starting transfers between devices, opposed(): return lax.ppermute(x, ('ctx', 'head'), pairs)  10.2 us
    pallas_call x4, Pallas kernels, chan_conv(): pl.pallas_call(kernel, in_specs=specs(5 + (part == 0), 1), out_specs=tupl...  8.75 us
    pallas_call x1, Pallas kernels, carry(): pl.pallas_call(kernel, in_specs=specs(4 + len(locs) + len(msgs), 1), out_...  4.63 us
    pallas_call x2, Pallas kernels, proj_conv(): pl.pallas_call(kernel, in_specs=specs(9, 1), out_specs=specs(1)[0], out_s...  4.26 us
    ppermute x3, waiting for transfers between devices, opposed(): return lax.ppermute(x, ('ctx', 'head'), pairs)  4.13 us
    ppermute x9, waiting for transfers between devices, swapped(): lax.ppermute(value, axis, [(i, i ^ mask) for i in range(lax.axis_size(axi...  3.58 us
  transfers between devices with their start and end apart: 13, of which 4 were waited for; matrix products, arithmetic and copies ran while one was open for 0% of the time, Pallas kernels for 35%

profile of v2, /device:TPU:1, one launch (start us, length us, event | category | flops | bytes accessed | tf_op | source)
XLA Modules:
  0.0 68.5 jit_solution(9578073381282969795)
XLA Ops:
  0.0 2.1 %collective-permute-start.1 = (bf16[64,4096]{1,0:T(8,128)(2,1)}, bf16[64,4096]{1,0:T(8,128)(2,1)S(1)}, u32[]{:S(2)}, u32[]{:S(2)}) collective-permute-start(bf16[64,4096]{1,0:T(8,128)(2,1)} %bitcast.9), channel_id=1, source_target_pairs={{0,2},{1,3},{2,0},{3,1},{4,6},{5,7},{6,4},{7,5},{8,10},{9,11},{10,... | collective-permute-start | bytes 1572872 | tf_op jit(solution)/shard_map/ppermute | solution.py:45
  2.2 1.4 %tails.1 = bf16[144,128]{1,0:T(8,128)(2,1)} custom-call(bf16[4096,512]{1,0:T(8,128)(2,1)} %refs_1_.7, bf16[64,4096]{1,0:T(8,128)(2,1)} %bitcast.10, bf16[4,64]{1,0:T(4,128)(2,1)} %w_ref.1), custom_call_target="tpu_custom_call" | custom-call | tf_op jit(solution)/shard_map/tails/pallas_call | solution.py:102
  3.5 1.6 %collective-permute-start.2 = (bf16[144,128]{1,0:T(8,128)(2,1)}, bf16[144,128]{1,0:T(8,128)(2,1)S(1)}, u32[]{:S(2)}, u32[]{:S(2)}) collective-permute-start(bf16[144,128]{1,0:T(8,128)(2,1)} %tails.1), channel_id=1, source_target_pairs={{0,32},{32,64},{64,96},{96,128},{128,160},{160,192},{192,224},{224... | collective-permute-start | bytes 110600 | tf_op jit(solution)/shard_map/ppermute | solution.py:31
  5.2 0.1 pad_add_fusion.refs_0_
  5.3 0.0 copy-start.1
  5.3 1.2 %decays.1 = (f32[8,4096]{1,0:T(8,128)S(1)}, f32[8,4096]{1,0:T(8,128)S(1)}, f32[8,4096]{1,0:T(8,128)S(1)}, f32[32,512]{1,0:T(8,128)S(1)}, f32[1,512]{1,0:T(1,128)S(1)}) custom-call(f32[8,4096]{1,0:T(8,128)S(1)} %bitcast.15, f32[1,8]{1,0:T(1,128)S(1)} %bitcast.16, f32[1,8]{1,0:T(1,128)S(1)} %bitcast.17, f32[1,8]{1,0:T(1,128)S(1)} %bitcast.18), custom_call_target="tpu_custom_call" | custom-call | flops 655360000 | bytes 524288 | tf_op jit(solution)/shard_map/decays/pallas_call | solution.py:221
  6.4 0.0 copy-start
  6.5 2.2 %copy-done = bf16[4096,512]{1,0:T(8,128)(2,1)S(1)} copy-done((bf16[4096,512]{1,0:T(8,128)(2,1)S(1)}, bf16[4096,512]{1,0:T(8,128)(2,1)}, u32[]{:S(2)}) %copy-start) | copy-done | bytes 4194328
  8.6 2.2 %chan_conv.4 = (bf16[1024,512]{1,0:T(8,128)(2,1)S(1)}, bf16[1024,512]{1,0:T(8,128)(2,1)S(1)}, f32[8,128]{1,0:T(8,128)}) custom-call(s32[3]{0:T(128)S(1)} %pad_add_fusion.refs_0_, bf16[4096,512]{1,0:T(8,128)(2,1)S(1)} %copy-done, bf16[4,512]{1,0:T(4,128)(2,1)S(1)} %copy-done.5, f32[8,4096]{1,0:T(8,128)S(1)} %get-tuple-element.60.refs_3_.refs_4_, ...), custom_call_target="tpu_custom_call" | custom-call | flops 2097152000 | bytes 3145728 | tf_op jit(solution)/shard_map/chan_conv/pallas_call | solution.py:294
  10.8 0.0 collective-permute-done.2.refs_5_
  10.9 0.3 collective-permute-start.3
  11.2 1.8 %collective-permute-start = (bf16[64,4096]{1,0:T(8,128)(2,1)S(1)}, bf16[64,4096]{1,0:T(8,128)(2,1)S(1)}, u32[]{:S(2)}, u32[]{:S(2)}) collective-permute-start(bf16[64,4096]{1,0:T(8,128)(2,1)S(1)} %bitcast.11), channel_id=1, source_target_pairs={{0,1},{1,0},{2,3},{3,2},{4,5},{5,4},{6,7},{7,6},{8,9},{9,8},{10,11... | collective-permute-start | bytes 1572872 | tf_op jit(solution)/shard_map/ppermute | solution.py:45
  13.0 0.0 collective-permute-start.5
  13.0 1.5 %collective-permute-done.3.refs_7_ = bf16[144,128]{1,0:T(8,128)(2,1)S(1)} collective-permute-done((bf16[144,128]{1,0:T(8,128)(2,1)S(1)}, bf16[144,128]{1,0:T(8,128)(2,1)S(1)}, u32[]{:S(2)}, u32[]{:S(2)}) %collective-permute-start.3) | collective-permute-done | bytes 36896 | tf_op jit(solution)/shard_map/ppermute | solution.py:45
  14.5 0.0 collective-permute-done.1.refs_3_
  14.5 1.9 %collective-permute-start.4 = (bf16[64,4096]{1,0:T(8,128)(2,1)S(1)}, bf16[64,4096]{1,0:T(8,128)(2,1)S(1)}, u32[]{:S(2)}, u32[]{:S(2)}) collective-permute-start(bf16[64,4096]{1,0:T(8,128)(2,1)S(1)} %collective-permute-done.1.refs_3_), channel_id=1, source_target_pairs={{0,1},{1,0},{2,3},{3,2},{4,5},{5,4},{6,7},{7,6},{8,9},{9,8},{10,11... | collective-permute-start | bytes 1572872 | tf_op jit(solution)/shard_map/ppermute | solution.py:45
  16.4 2.2 %chan_conv.5 = (bf16[1024,512]{1,0:T(8,128)(2,1)S(1)}, bf16[1024,512]{1,0:T(8,128)(2,1)S(1)}, f32[8,128]{1,0:T(8,128)}) custom-call(s32[3]{0:T(128)S(1)} %pad_add_fusion.refs_0_, bf16[4096,512]{1,0:T(8,128)(2,1)S(1)} %copy-done, bf16[4,512]{1,0:T(4,128)(2,1)S(1)} %copy-done.5, f32[8,4096]{1,0:T(8,128)S(1)} %get-tuple-element.60.refs_3_.refs_4_, ...), custom_call_target="tpu_custom_call" | custom-call | flops 2097152000 | bytes 3145728 | tf_op jit(solution)/shard_map/chan_conv/pallas_call | solution.py:294
  18.6 2.2 %chan_conv.7 = (bf16[1024,512]{1,0:T(8,128)(2,1)S(1)}, bf16[1024,512]{1,0:T(8,128)(2,1)S(1)}, f32[8,128]{1,0:T(8,128)}) custom-call(s32[3]{0:T(128)S(1)} %pad_add_fusion.refs_0_, bf16[4096,512]{1,0:T(8,128)(2,1)S(1)} %copy-done, bf16[4,512]{1,0:T(4,128)(2,1)S(1)} %copy-done.5, f32[8,4096]{1,0:T(8,128)S(1)} %get-tuple-element.60.refs_3_.refs_4_, ...), custom_call_target="tpu_custom_call" | custom-call | flops 2097152000 | bytes 3145728 | tf_op jit(solution)/shard_map/chan_conv/pallas_call | solution.py:294
  20.8 0.3 collective-permute-start.6
  21.1 2.2 %chan_conv.6 = (bf16[1024,512]{1,0:T(8,128)(2,1)S(1)}, bf16[1024,512]{1,0:T(8,128)(2,1)S(1)}, f32[8,128]{1,0:T(8,128)}) custom-call(s32[3]{0:T(128)S(1)} %pad_add_fusion.refs_0_, bf16[4096,512]{1,0:T(8,128)(2,1)S(1)} %copy-done, bf16[4,512]{1,0:T(4,128)(2,1)S(1)} %copy-done.5, f32[8,4096]{1,0:T(8,128)S(1)} %get-tuple-element.60.refs_3_.refs_4_, ...), custom_call_target="tpu_custom_call" | custom-call | flops 2097152000 | bytes 3145728 | tf_op jit(solution)/shard_map/chan_conv/pallas_call | solution.py:294
  23.3 0.0 collective-permute-done.4.refs_4_
  23.3 0.0 collective-permute-done.5.refs_6_
  23.3 0.0 collective-permute-done.refs_2_
  23.3 0.0 collective-permute-done.6.refs_8_
  23.4 2.1 %proj_conv.2.b_ref.refs_1_ = bf16[128,4096]{1,0:T(8,128)(2,1)S(1)} custom-call(s32[3]{0:T(128)S(1)} %pad_add_fusion.refs_0_, bf16[64,4096]{1,0:T(8,128)(2,1)S(1)} %bitcast.12, bf16[64,4096]{1,0:T(8,128)(2,1)S(1)} %collective-permute-done.refs_2_, bf16[64,4096]{1,0:T(8,128)(2,1)S(1)} %collective-permute-done.1.refs_3_, ...), custom_call_target="tpu_custom_call" | custom-call | flops 1048576000 | bytes 1572864 | tf_op jit(solution)/shard_map/proj_conv/pallas_call | solution.py:167
  25.5 1.3 %states.1 = (bf16[32,128,512]{2,1,0:T(8,128)(2,1)S(1)}, bf16[144,512]{1,0:T(8,128)(2,1)S(1)}) custom-call(bf16[128,4096]{1,0:T(8,128)(2,1)S(1)} %proj_conv.2.b_ref.refs_1_, f32[32,512]{1,0:T(8,128)S(1)} %get-tuple-element.42.tot_ref, bf16[1024,512]{1,0:T(8,128)(2,1)S(1)} %get-tuple-element.43.rest_0_, bf16[1024,512]{1,0:T(8,128)(2,1)S(1)} %get-tuple-element.45.rest_1_, ...), custom_call_target="tpu_custom_call" | custom-call | flops 4194304000 | bytes 8388608 | tf_op jit(solution)/shard_map/states/pallas_call | solution.py:377
  26.8 5.5 %collective-permute-start.7 = (bf16[144,512]{1,0:T(8,128)(2,1)S(1)}, bf16[144,512]{1,0:T(8,128)(2,1)S(1)}, u32[]{:S(2)}, u32[]{:S(2)}) collective-permute-start(bf16[144,512]{1,0:T(8,128)(2,1)S(1)} %get-tuple-element.49.refs_1_), channel_id=1, source_target_pairs={{0,32},{1,225},{2,34},{3,227},{4,36},{5,229},{6,38},{7,231},{8,40}... | collective-permute-start | bytes 442376 | tf_op jit(solution)/shard_map/ppermute | solution.py:41
  32.3 2.1 %proj_conv.3.refs_2_.refs_1_ = bf16[128,4096]{1,0:T(8,128)(2,1)S(1)} custom-call(s32[3]{0:T(128)S(1)} %pad_add_fusion.refs_0_, bf16[64,4096]{1,0:T(8,128)(2,1)S(1)} %bitcast.13, bf16[64,4096]{1,0:T(8,128)(2,1)S(1)} %collective-permute-done.refs_2_, bf16[64,4096]{1,0:T(8,128)(2,1)S(1)} %collective-permute-done.1.refs_3_, ...), custom_call_target="tpu_custom_call" | custom-call | flops 1048576000 | bytes 1572864 | tf_op jit(solution)/shard_map/proj_conv/pallas_call | solution.py:167
  34.5 0.0 collective-permute-done.7.refs_2_.refs_8_
  34.5 0.6 merge.2.refs_1_
  35.1 2.7 %collective-permute-start.8 = (bf16[144,512]{1,0:T(8,128)(2,1)S(1)}, bf16[144,512]{1,0:T(8,128)(2,1)S(1)}, u32[]{:S(2)}, u32[]{:S(2)}) collective-permute-start(bf16[144,512]{1,0:T(8,128)(2,1)S(1)} %merge.2.refs_1_), channel_id=1, source_target_pairs={{0,64},{1,193},{2,66},{3,195},{4,68},{5,197},{6,70},{7,199},{8,72}... | collective-permute-start | bytes 442376 | tf_op jit(solution)/shard_map/ppermute | solution.py:41
  37.8 2.7 %local.5.refs_5_ = bf16[1024,512]{1,0:T(8,128)(2,1)S(1)} custom-call(bf16[1024,512]{1,0:T(8,128)(2,1)S(1)} %get-tuple-element.57.refs_0_, bf16[128,4096]{1,0:T(8,128)(2,1)S(1)} %proj_conv.2.b_ref.refs_1_, bf16[128,4096]{1,0:T(8,128)(2,1)S(1)} %proj_conv.3.refs_2_.refs_1_, bf16[32,128,512]{2,1,0:T(8,128)(2,1)S(1)} %get-tuple-element.53.refs_3_, ...), custom_call_target="tpu_custom_call" | custom-call | flops 4194304000 | bytes 3145728 | tf_op jit(solution)/shard_map/local/pallas_call | solution.py:437
  40.4 2.7 %local.4.refs_4_ = bf16[1024,512]{1,0:T(8,128)(2,1)S(1)} custom-call(bf16[1024,512]{1,0:T(8,128)(2,1)S(1)} %get-tuple-element.52.refs_0_, bf16[128,4096]{1,0:T(8,128)(2,1)S(1)} %proj_conv.2.b_ref.refs_1_, bf16[128,4096]{1,0:T(8,128)(2,1)S(1)} %proj_conv.3.refs_2_.refs_1_, bf16[32,128,512]{2,1,0:T(8,128)(2,1)S(1)} %get-tuple-element.53.refs_3_, ...), custom_call_target="tpu_custom_call" | custom-call | flops 4194304000 | bytes 3145728 | tf_op jit(solution)/shard_map/local/pallas_call | solution.py:437
  43.1 0.0 collective-permute-done.8.refs_2_.refs_9_
  43.1 0.6 merge.3
  43.8 2.1 %collective-permute-start.9 = (bf16[144,512]{1,0:T(8,128)(2,1)S(1)}, bf16[144,512]{1,0:T(8,128)(2,1)S(1)}, u32[]{:S(2)}, u32[]{:S(2)}) collective-permute-start(bf16[144,512]{1,0:T(8,128)(2,1)S(1)} %merge.3), channel_id=1, source_target_pairs={{0,128},{1,129},{2,130},{3,131},{4,132},{5,133},{6,134},{7,135},{8... | collective-permute-start | bytes 442376 | tf_op jit(solution)/shard_map/ppermute | solution.py:41
  45.8 2.7 %local.7.refs_7_ = bf16[1024,512]{1,0:T(8,128)(2,1)S(1)} custom-call(bf16[1024,512]{1,0:T(8,128)(2,1)S(1)} %get-tuple-element.61.refs_0_, bf16[128,4096]{1,0:T(8,128)(2,1)S(1)} %proj_conv.2.b_ref.refs_1_, bf16[128,4096]{1,0:T(8,128)(2,1)S(1)} %proj_conv.3.refs_2_.refs_1_, bf16[32,128,512]{2,1,0:T(8,128)(2,1)S(1)} %get-tuple-element.53.refs_3_, ...), custom_call_target="tpu_custom_call" | custom-call | flops 4194304000 | bytes 3145728 | tf_op jit(solution)/shard_map/local/pallas_call | solution.py:437
  48.5 0.0 copy-start.3
  48.5 2.7 %local.6.refs_6_ = bf16[1024,512]{1,0:T(8,128)(2,1)S(1)} custom-call(bf16[1024,512]{1,0:T(8,128)(2,1)S(1)} %get-tuple-element.58.refs_0_, bf16[128,4096]{1,0:T(8,128)(2,1)S(1)} %proj_conv.2.b_ref.refs_1_, bf16[128,4096]{1,0:T(8,128)(2,1)S(1)} %proj_conv.3.refs_2_.refs_1_, bf16[32,128,512]{2,1,0:T(8,128)(2,1)S(1)} %get-tuple-element.53.refs_3_, ...), custom_call_target="tpu_custom_call" | custom-call | flops 4194304000 | bytes 3145728 | tf_op jit(solution)/shard_map/local/pallas_call | solution.py:437
  51.2 4.1 %collective-permute-done.9.refs_10_ = bf16[144,512]{1,0:T(8,128)(2,1)S(1)} collective-permute-done((bf16[144,512]{1,0:T(8,128)(2,1)S(1)}, bf16[144,512]{1,0:T(8,128)(2,1)S(1)}, u32[]{:S(2)}, u32[]{:S(2)}) %collective-permute-start.9) | collective-permute-done | bytes 147488 | tf_op jit(solution)/shard_map/ppermute | solution.py:41
  55.4 4.6 %carry.1 = (bf16[4096,512]{1,0:T(8,128)(2,1)S(1)}, f32[32,128]{1,0:T(8,128)S(1)}) custom-call(s32[3]{0:T(128)S(1)} %pad_add_fusion.refs_0_, bf16[128,4096]{1,0:T(8,128)(2,1)S(1)} %proj_conv.3.refs_2_.refs_1_, f32[8,4096]{1,0:T(8,128)S(1)} %get-tuple-element.51.refs_2_, bf16[4096,512]{1,0:T(8,128)(2,1)S(1)} %copy-done.3, bf16[1024,512]{1,0:T(8,128)(2,1)S(1)} %local.4.refs_4_, ...), custom_call_target="tpu_custom_call" | custom-call | flops 8388608000 | bytes 12582912 | tf_op jit(solution)/shard_map/carry/pallas_call | solution.py:505
  60.0 3.2 %collective-permute-start.12 = (f32[32,128]{1,0:T(8,128)S(1)}, f32[32,128]{1,0:T(8,128)S(1)}, u32[]{:S(2)}, u32[]{:S(2)}) collective-permute-start(f32[32,128]{1,0:T(8,128)S(1)} %get-tuple-element.64), channel_id=1, source_target_pairs={{0,3},{1,2},{2,1},{3,0},{4,7},{5,6},{6,5},{7,4},{8,11},{9,10},{10,... | collective-permute-start | bytes 49160 | tf_op jit(solution)/shard_map/ppermute | solution.py:45
  63.2 0.3 collective-permute-start.11
  63.5 0.2 collective-permute-start.10
  63.7 1.3 %collective-permute-done.12 = f32[32,128]{1,0:T(8,128)S(1)} collective-permute-done((f32[32,128]{1,0:T(8,128)S(1)}, f32[32,128]{1,0:T(8,128)S(1)}, u32[]{:S(2)}, u32[]{:S(2)}) %collective-permute-start.12) | collective-permute-done | bytes 16416 | tf_op jit(solution)/shard_map/ppermute | solution.py:45
  65.0 0.8 %collective-permute-done.11 = f32[32,128]{1,0:T(8,128)S(1)} collective-permute-done((f32[32,128]{1,0:T(8,128)S(1)}, f32[32,128]{1,0:T(8,128)S(1)}, u32[]{:S(2)}, u32[]{:S(2)}) %collective-permute-start.11) | collective-permute-done | bytes 16416 | tf_op jit(solution)/shard_map/ppermute | solution.py:45
  65.8 0.0 collective-permute-done.10
  65.8 2.7 %norm.1 = bf16[4096,512]{1,0:T(8,128)(2,1)} custom-call(bf16[4096,512]{1,0:T(8,128)(2,1)S(1)} %get-tuple-element.63.refs_0_, f32[32,128]{1,0:T(8,128)S(1)} %add_add_fusion.refs_1_, f32[1,512]{1,0:T(1,128)S(1)} %bitcast.14), custom_call_target="tpu_custom_call" | custom-call | flops 6291456 | bytes 8388608 | tf_op jit(solution)/shard_map/norm/pallas_call | solution.py:540
  (15 shorter events, 0.0 us)
Async XLA Ops:
  0.0 5.2 %copy-start.4 = (f32[4096,8]{0,1:T(8,128)S(1)}, f32[4096,8]{0,1:T(8,128)}, u32[]{:S(2)}) copy-start(f32[4096,8]{0,1:T(8,128)} %param.13) | copy-start | bytes 393220
  0.0 5.2 %copy-start.8 = (f32[8]{0:T(128)S(1)}, f32[8]{0:T(128)}, u32[]{:S(2)}) copy-start(f32[8]{0:T(128)} %param.16) | copy-start | bytes 100
  0.0 5.2 %copy-start.7 = (f32[8]{0:T(128)S(1)}, f32[8]{0:T(128)}, u32[]{:S(2)}) copy-start(f32[8]{0:T(128)} %param.15) | copy-start | bytes 100
  0.0 5.2 %copy-start.6 = (f32[8]{0:T(128)S(1)}, f32[8]{0:T(128)}, u32[]{:S(2)}) copy-start(f32[8]{0:T(128)} %param.14) | copy-start | bytes 100
  0.0 6.4 %copy-start.5 = (bf16[4,512]{1,0:T(4,128)(2,1)S(1)}, bf16[4,512]{1,0:T(4,128)(2,1)}, u32[]{:S(2)}) copy-start(bf16[4,512]{1,0:T(4,128)(2,1)} %refs_2_.7) | copy-start | bytes 12292
  0.0 14.5 %collective-permute-start.1 = (bf16[64,4096]{1,0:T(8,128)(2,1)}, bf16[64,4096]{1,0:T(8,128)(2,1)S(1)}, u32[]{:S(2)}, u32[]{:S(2)}) collective-permute-start(bf16[64,4096]{1,0:T(8,128)(2,1)} %bitcast.9), channel_id=1, source_target_pairs={{0,2},{1,3},{2,0},{3,1},{4,6},{5,7},{6,4},{7,5},{8,10},{9,11},{10,... | collective-permute-start | bytes 1572872 | tf_op jit(solution)/shard_map/ppermute | solution.py:45
  3.5 7.3 %collective-permute-start.2 = (bf16[144,128]{1,0:T(8,128)(2,1)}, bf16[144,128]{1,0:T(8,128)(2,1)S(1)}, u32[]{:S(2)}, u32[]{:S(2)}) collective-permute-start(bf16[144,128]{1,0:T(8,128)(2,1)} %tails.1), channel_id=1, source_target_pairs={{0,32},{32,64},{64,96},{96,128},{128,160},{160,192},{192,224},{224... | collective-permute-start | bytes 110600 | tf_op jit(solution)/shard_map/ppermute | solution.py:31
  5.3 5.9 %copy-start.1 = (bf16[4096,64]{0,1:T(8,128)(2,1)S(1)}, bf16[4096,64]{0,1:T(8,128)(2,1)}, u32[]{:S(2)}) copy-start(bf16[4096,64]{0,1:T(8,128)(2,1)} %param.12) | copy-start | bytes 1572868
  6.4 2.2 %copy-start = (bf16[4096,512]{1,0:T(8,128)(2,1)S(1)}, bf16[4096,512]{1,0:T(8,128)(2,1)}, u32[]{:S(2)}) copy-start(bf16[4096,512]{1,0:T(8,128)(2,1)} %refs_1_.7) | copy-start | bytes 12582916
  10.9 3.7 %collective-permute-start.3 = (bf16[144,128]{1,0:T(8,128)(2,1)S(1)}, bf16[144,128]{1,0:T(8,128)(2,1)S(1)}, u32[]{:S(2)}, u32[]{:S(2)}) collective-permute-start(bf16[144,128]{1,0:T(8,128)(2,1)S(1)} %collective-permute-done.2.refs_5_), channel_id=1, source_target_pairs={{0,2},{1,3},{2,0},{3,1},{4,6},{5,7},{6,4},{7,5},{8,10},{9,11},{10,... | collective-permute-start | bytes 110600 | tf_op jit(solution)/shard_map/ppermute | solution.py:45
  11.2 12.1 %collective-permute-start = (bf16[64,4096]{1,0:T(8,128)(2,1)S(1)}, bf16[64,4096]{1,0:T(8,128)(2,1)S(1)}, u32[]{:S(2)}, u32[]{:S(2)}) collective-permute-start(bf16[64,4096]{1,0:T(8,128)(2,1)S(1)} %bitcast.11), channel_id=1, source_target_pairs={{0,1},{1,0},{2,3},{3,2},{4,5},{5,4},{6,7},{7,6},{8,9},{9,8},{10,11... | collective-permute-start | bytes 1572872 | tf_op jit(solution)/shard_map/ppermute | solution.py:45
  13.0 10.3 %collective-permute-start.5 = (bf16[144,128]{1,0:T(8,128)(2,1)S(1)}, bf16[144,128]{1,0:T(8,128)(2,1)S(1)}, u32[]{:S(2)}, u32[]{:S(2)}) collective-permute-start(bf16[144,128]{1,0:T(8,128)(2,1)S(1)} %collective-permute-done.2.refs_5_), channel_id=1, source_target_pairs={{0,1},{1,0},{2,3},{3,2},{4,5},{5,4},{6,7},{7,6},{8,9},{9,8},{10,11... | collective-permute-start | bytes 110600 | tf_op jit(solution)/shard_map/ppermute | solution.py:45
  14.5 8.8 %collective-permute-start.4 = (bf16[64,4096]{1,0:T(8,128)(2,1)S(1)}, bf16[64,4096]{1,0:T(8,128)(2,1)S(1)}, u32[]{:S(2)}, u32[]{:S(2)}) collective-permute-start(bf16[64,4096]{1,0:T(8,128)(2,1)S(1)} %collective-permute-done.1.refs_3_), channel_id=1, source_target_pairs={{0,1},{1,0},{2,3},{3,2},{4,5},{5,4},{6,7},{7,6},{8,9},{9,8},{10,11... | collective-permute-start | bytes 1572872 | tf_op jit(solution)/shard_map/ppermute | solution.py:45
  20.8 2.5 %collective-permute-start.6 = (bf16[144,128]{1,0:T(8,128)(2,1)S(1)}, bf16[144,128]{1,0:T(8,128)(2,1)S(1)}, u32[]{:S(2)}, u32[]{:S(2)}) collective-permute-start(bf16[144,128]{1,0:T(8,128)(2,1)S(1)} %collective-permute-done.3.refs_7_), channel_id=1, source_target_pairs={{0,1},{1,0},{2,3},{3,2},{4,5},{5,4},{6,7},{7,6},{8,9},{9,8},{10,11... | collective-permute-start | bytes 110600 | tf_op jit(solution)/shard_map/ppermute | solution.py:45
  26.8 7.6 %collective-permute-start.7 = (bf16[144,512]{1,0:T(8,128)(2,1)S(1)}, bf16[144,512]{1,0:T(8,128)(2,1)S(1)}, u32[]{:S(2)}, u32[]{:S(2)}) collective-permute-start(bf16[144,512]{1,0:T(8,128)(2,1)S(1)} %get-tuple-element.49.refs_1_), channel_id=1, source_target_pairs={{0,32},{1,225},{2,34},{3,227},{4,36},{5,229},{6,38},{7,231},{8,40}... | collective-permute-start | bytes 442376 | tf_op jit(solution)/shard_map/ppermute | solution.py:41
  35.1 8.0 %collective-permute-start.8 = (bf16[144,512]{1,0:T(8,128)(2,1)S(1)}, bf16[144,512]{1,0:T(8,128)(2,1)S(1)}, u32[]{:S(2)}, u32[]{:S(2)}) collective-permute-start(bf16[144,512]{1,0:T(8,128)(2,1)S(1)} %merge.2.refs_1_), channel_id=1, source_target_pairs={{0,64},{1,193},{2,66},{3,195},{4,68},{5,197},{6,70},{7,199},{8,72}... | collective-permute-start | bytes 442376 | tf_op jit(solution)/shard_map/ppermute | solution.py:41
  43.8 11.6 %collective-permute-start.9 = (bf16[144,512]{1,0:T(8,128)(2,1)S(1)}, bf16[144,512]{1,0:T(8,128)(2,1)S(1)}, u32[]{:S(2)}, u32[]{:S(2)}) collective-permute-start(bf16[144,512]{1,0:T(8,128)(2,1)S(1)} %merge.3), channel_id=1, source_target_pairs={{0,128},{1,129},{2,130},{3,131},{4,132},{5,133},{6,134},{7,135},{8... | collective-permute-start | bytes 442376 | tf_op jit(solution)/shard_map/ppermute | solution.py:41
  48.5 6.8 %copy-start.3 = (bf16[4096,512]{1,0:T(8,128)(2,1)S(1)}, bf16[4096,512]{1,0:T(8,128)(2,1)}, u32[]{:S(2)}) copy-start(bf16[4096,512]{1,0:T(8,128)(2,1)} %refs_3_.1) | copy-start | bytes 12582916
  55.4 10.5 %copy-start.2 = (f32[512]{0:T(512)S(1)}, f32[512]{0:T(512)}, u32[]{:S(2)}) copy-start(f32[512]{0:T(512)} %param.19) | copy-start | bytes 6148
  60.0 5.1 %collective-permute-start.12 = (f32[32,128]{1,0:T(8,128)S(1)}, f32[32,128]{1,0:T(8,128)S(1)}, u32[]{:S(2)}, u32[]{:S(2)}) collective-permute-start(f32[32,128]{1,0:T(8,128)S(1)} %get-tuple-element.64), channel_id=1, source_target_pairs={{0,3},{1,2},{2,1},{3,0},{4,7},{5,6},{6,5},{7,4},{8,11},{9,10},{10,... | collective-permute-start | bytes 49160 | tf_op jit(solution)/shard_map/ppermute | solution.py:45
  63.2 2.6 %collective-permute-start.11 = (f32[32,128]{1,0:T(8,128)S(1)}, f32[32,128]{1,0:T(8,128)S(1)}, u32[]{:S(2)}, u32[]{:S(2)}) collective-permute-start(f32[32,128]{1,0:T(8,128)S(1)} %get-tuple-element.64), channel_id=1, source_target_pairs={{0,2},{1,3},{2,0},{3,1},{4,6},{5,7},{6,4},{7,5},{8,10},{9,11},{10,... | collective-permute-start | bytes 49160 | tf_op jit(solution)/shard_map/ppermute | solution.py:45
  63.5 2.3 %collective-permute-start.10 = (f32[32,128]{1,0:T(8,128)S(1)}, f32[32,128]{1,0:T(8,128)S(1)}, u32[]{:S(2)}, u32[]{:S(2)}) collective-permute-start(f32[32,128]{1,0:T(8,128)S(1)} %get-tuple-element.64), channel_id=1, source_target_pairs={{0,1},{1,0},{2,3},{3,2},{4,5},{5,4},{6,7},{7,6},{8,9},{9,8},{10,11... | collective-permute-start | bytes 49160 | tf_op jit(solution)/shard_map/ppermute | solution.py:45

commit v3 on v2

--- a/solution.py
+++ b/solution.py
@@ -45,10 +45,6 @@
     return lax.ppermute(value, axis, [(i, i ^ mask) for i in range(lax.axis_size(axis))])
 
 
-def after(value, *others):
-    return lax.optimization_barrier((value,) + others)[0]
-
-
 def params():
     return pltpu.CompilerParams(vmem_limit_bytes=VMEM_CAP)
 
@@ -60,6 +56,17 @@
 def specs(count, scalars=0):
     smem = pl.BlockSpec(memory_space=pltpu.SMEM)
     return [smem] * scalars + [pl.BlockSpec(memory_space=pltpu.VMEM)] * (count - scalars)
+
+
+def ordered(kernel, skip, extra):
+    def call(*refs):
+        return kernel(*refs[:skip], *refs[skip + extra :])
+
+    return call
+
+
+def unread(needs):
+    return [pl.BlockSpec(memory_space=pl.ANY)] * len(needs)
 
 
 def half_silu(h):
@@ -110,6 +117,7 @@
         out_specs=pl.BlockSpec((rows, BLK), lambda i: (0, 0)),
         out_shape=jax.ShapeDtypeStruct((rows, BLK), BF16),
         compiler_params=pltpu.CompilerParams(vmem_limit_bytes=60 * 1024 * 1024),
+        cost_estimate=cost(2 << 30, 1 << 20),
         name="tails",
     )(x, proj_t, taps)
 
@@ -158,22 +166,22 @@
         o_ref[:, cur] = half_silu(h).astype(BF16)
 
 
-def proj_conv(flag, raws, halos, wanted):
+def proj_conv(flag, raws, halos, wanted, needs=()):
     half, tokens = raws[0].shape
 
     def kernel(*refs):
         proj_conv_kernel(wanted, *refs)
 
     return pl.pallas_call(
-        kernel,
-        in_specs=specs(9, 1),
+        ordered(kernel, 9, len(needs)),
+        in_specs=specs(9, 1) + unread(needs),
         out_specs=specs(1)[0],
         out_shape=jax.ShapeDtypeStruct((2 * half, tokens), BF16),
         scratch_shapes=[pltpu.VMEM((4, 2 * half, BLK), F32)],
         compiler_params=params(),
         cost_estimate=cost(half * tokens * 4000, half * tokens * 6, half * tokens * 2),
         name="proj_conv",
-    )(flag, *raws, *halos)
+    )(flag, *raws, *halos, *needs)
 
 
 def decay_kernel(
@@ -215,12 +223,12 @@
     tot_ref[...] = jnp.dot(pick, spread, precision=HIGH, preferred_element_type=F32)
 
 
-def decays(dt_t, bias, a_log, skip, chans):
+def decays(dt_t, bias, a_log, skip, chans, needs=()):
     heads, tokens = dt_t.shape
     rows = jax.ShapeDtypeStruct((heads, tokens), F32)
     return pl.pallas_call(
-        decay_kernel,
-        in_specs=specs(4),
+        ordered(decay_kernel, 4, len(needs)),
+        in_specs=specs(4) + unread(needs),
         out_specs=tuple(specs(5)),
         out_shape=(
             rows,
@@ -230,9 +238,9 @@
             jax.ShapeDtypeStruct((1, chans), F32),
         ),
         compiler_params=params(),
-        cost_estimate=cost(heads * tokens * 20000, heads * tokens * 16, heads * tokens * 2),
+        cost_estimate=cost(heads * tokens * 80000, heads * tokens * 16, heads * tokens * 2),
         name="decays",
-    )(dt_t, bias[None, :], a_log[None, :], skip[None, :])
+    )(dt_t, bias[None, :], a_log[None, :], skip[None, :], *needs)
 
 
 def chan_conv_kernel(base, flag_ref, x_ref, w_ref, run_ref, step_ref, *rest):
@@ -284,7 +292,7 @@
     t_ref[...] = jnp.zeros_like(t_ref)
 
 
-def chan_conv(flag, x, taps, run, step, halo, part, parts):
+def chan_conv(flag, x, taps, run, step, halo, part, parts, needs=()):
     tokens, chans = x.shape
     here = tokens // parts
 
@@ -292,15 +300,15 @@
         chan_conv_kernel(part * here // BLK, *refs)
 
     return pl.pallas_call(
-        kernel,
-        in_specs=specs(5 + (part == 0), 1),
+        ordered(kernel, 5 + (part == 0), len(needs)),
+        in_specs=specs(5 + (part == 0), 1) + unread(needs),
         out_specs=tuple(specs(3)),
         out_shape=(jax.ShapeDtypeStruct((here, chans), BF16),) * 2
         + (jax.ShapeDtypeStruct((8, BLK), F32),),
         compiler_params=params(),
         cost_estimate=cost(here * chans * 4000, here * chans * 6, here * chans),
         name="chan_conv",
-    )(flag, x, taps, run, step, *([halo] if part == 0 else []))
+    )(flag, x, taps, run, step, *([halo] if part == 0 else []), *needs)
 
 
 def write_log(msg_ref, log):
@@ -336,19 +344,19 @@
     write_log(o_ref, late_log + early_log)
 
 
-def merge(flag, mine, got, level, devices):
+def merge(flag, mine, got, level, devices, needs=()):
     def kernel(*refs):
         merge_kernel(level, devices, *refs)
 
     return pl.pallas_call(
-        kernel,
-        in_specs=specs(3, 1),
+        ordered(kernel, 3, len(needs)),
+        in_specs=specs(3, 1) + unread(needs),
         out_specs=specs(1)[0],
         out_shape=jax.ShapeDtypeStruct(mine.shape, BF16),
         compiler_params=params(),
         cost_estimate=cost(mine.size * 4, mine.size * 6),
         name="merge",
-    )(flag, mine, got)
+    )(flag, mine, got, *needs)
 
 
 def state_kernel(b_ref, tot_ref, *rest):
@@ -426,7 +434,7 @@
             o_ref[block_at(i), lanes] = out.astype(BF16)
 
 
-def local(x_conv, b_t, c_t, entering, run, step, skip, part, parts, offset):
+def local(x_conv, b_t, c_t, entering, run, step, skip, part, parts, offset, needs=()):
     heads, tokens = run.shape
     chans = x_conv.shape[1]
     here = tokens // parts
@@ -435,14 +443,14 @@
         local_kernel(part * here // BLK, offset, *refs)
 
     return pl.pallas_call(
-        kernel,
-        in_specs=specs(7),
+        ordered(kernel, 7, len(needs)),
+        in_specs=specs(7) + unread(needs),
         out_specs=specs(1)[0],
         out_shape=jax.ShapeDtypeStruct((here, chans), BF16),
         compiler_params=params(),
         cost_estimate=cost(8000 * here * chans, here * chans * 6, here * heads * BLK * 2),
         name="local",
-    )(x_conv, b_t, c_t, entering, run, step, skip)
+    )(x_conv, b_t, c_t, entering, run, step, skip, *needs)
 
 
 def carry_kernel(nloc, devices, flag_ref, c_ref, abs_ref, z_ref, *rest):
@@ -564,46 +572,46 @@
     near_raw = swapped(proj_t, "head", 1)
     ends = tails(x_stream, proj_t, conv_proj)
     halo = rotated(ends, "ctx", 1)
-    run, whole, step, totals, skip = decays(after(dt_raw.T, ends), dt_bias, a_log, skip_d, chans)
+    run, whole, step, totals, skip = decays(dt_raw.T, dt_bias, a_log, skip_d, chans, (ends,))
 
     def conv(part, *needs):
-        return chan_conv(after(flag, *needs), x_stream, conv_x, run, step, halo, part, 4)
+        return chan_conv(flag, x_stream, conv_x, run, step, halo, part, 4, needs)
 
     x3, v3, mark = conv(3)
-    halo = after(halo, mark)
     halo_far = swapped(halo, "head", 2)
     halo_near = swapped(halo, "head", 1)
     x2, v2, mark = conv(2, halo, mark)
-    far_raw, halo_far = lax.optimization_barrier((far_raw, halo_far, mark))[:2]
+    x1, v1, mark = conv(1, mark)
+    far_raw, halo_far, mark = lax.optimization_barrier((far_raw, halo_far, mark))
     cross_raw = swapped(far_raw, "head", 1)
     halo_cross = swapped(halo_far, "head", 1)
-    x1, v1, mark = conv(1, far_raw, halo_far)
-    x0, v0, mark = conv(0, mark)
-    raws = (proj_t, near_raw, far_raw, after(cross_raw, mark))
+    x0, v0, mark = conv(0, far_raw, halo_far, mark)
+    cross_raw, mark = lax.optimization_barrier((cross_raw, mark))
+    raws = (proj_t, near_raw, far_raw, cross_raw)
     halos = (halo, halo_near, halo_far, halo_cross)
     b_t = proj_conv(flag, raws, halos, 0)
     entering, message = states((v0, v1, v2, v3), b_t, totals)
-    c_t = proj_conv(after(flag, message), raws, halos, 1)
+    c_t = proj_conv(flag, raws, halos, 1, (message,))
 
     locs = []
 
     def piece(at, *needs):
         x_conv = (x0, x1, x2, x3)[at]
         locs.append(
-            local(x_conv, b_t, c_t, entering, after(run, *needs), step, skip, at, 4, 0)
+            local(x_conv, b_t, c_t, entering, run, step, skip, at, 4, 0, needs)
         )
         return locs[-1]
 
     one = opposed(message, 1)
-    pair = merge(flag, message, after(one, c_t), 1, count)
+    pair = merge(flag, message, one, 1, count, (c_t,))
     two = opposed(pair, 2)
     piece(0, pair)
-    last = piece(1, pair)
-    quad = merge(flag, pair, after(two, last), 2, count)
+    last = piece(1, pair, locs[0])
+    quad = merge(flag, pair, two, 2, count, (last,))
     four = opposed(quad, 4)
     piece(2, quad)
-    last = piece(3, quad)
-    msgs = (one, two, after(four, last))
+    piece(3, quad)
+    msgs = (one, two, four)
 
     width = HEADS // GROUPS * (chans // heads)
     gated, squares = carry(flag, locs, gate_z, c_t, whole, msgs, count)

time: 68.7 us -> 64.7 us (0.942)
  waiting for transfers between devices: 7.72 us -> 4.35 us
    ppermute x3, waiting for transfers between devices: 4.13 us -> 1.99 us  [opposed(): return lax.ppermute(x, ('ctx', 'head'), pairs)]
    ppermute x9, waiting for transfers between devices: 3.58 us -> 2.11 us  [swapped(): lax.ppermute(value, axis, [(i, i ^ mask) for i in range(lax.axis_size(axi...]
    ppermute x3, starting transfers between devices: 10.2 us -> 9.24 us  [opposed(): return lax.ppermute(x, ('ctx', 'head'), pairs)]
    unnamed x18 -> x20, local copies, waits for them, and re-layouts: 2.23 us -> 1.82 us
  transfers between devices with their start and end apart: 13 -> 13, of which waited for: 4 -> 4; matrix products, arithmetic and copies ran while one was open for 0% -> 0% of each run, Pallas kernels for 35% -> 38%
where the time goes in v3:
time: 64.7 us; the launch traced here: 64.5 us
  Pallas kernels  36.3 us (56%)
  starting transfers between devices  21.8 us (34%)
  waiting for transfers between devices  4.35 us (7%)
  local copies, waits for them, and re-layouts  1.82 us (3%)
    ppermute x9, starting transfers between devices, swapped(): lax.ppermute(value, axis, [(i, i ^ mask) for i in range(lax.axis_size(axi...  10.9 us
    pallas_call x4, Pallas kernels, local(): pl.pallas_call(ordered(kernel, 7, len(needs)), in_specs=specs(7) + unread...  10.8 us
    ppermute x3, starting transfers between devices, opposed(): return lax.ppermute(x, ('ctx', 'head'), pairs)  9.24 us
    pallas_call x4, Pallas kernels, chan_conv(): pl.pallas_call(ordered(kernel, 5 + (part == 0), len(needs)), in_specs=spe...  8.75 us
    pallas_call x1, Pallas kernels, carry(): pl.pallas_call(kernel, in_specs=specs(4 + len(locs) + len(msgs), 1), out_...  4.74 us
    pallas_call x2, Pallas kernels, proj_conv(): pl.pallas_call(ordered(kernel, 9, len(needs)), in_specs=specs(9, 1) + unr...  4.28 us
    pallas_call x1, Pallas kernels, norm(): pl.pallas_call(kernel, grid=(tokens // rows,), in_specs=specs(3), out_spe...  2.66 us
    ppermute x9, waiting for transfers between devices, swapped(): lax.ppermute(value, axis, [(i, i ^ mask) for i in range(lax.axis_size(axi...  2.11 us
  transfers between devices with their start and end apart: 13, of which 4 were waited for; matrix products, arithmetic and copies ran while one was open for 0% of the time, Pallas kernels for 38%

profile of v3, /device:TPU:1, one launch (start us, length us, event | category | flops | bytes accessed | tf_op | source)
XLA Modules:
  0.0 64.5 jit_solution(7996298662669163133)
XLA Ops:
  0.0 2.1 %collective-permute-start.1 = (bf16[64,4096]{1,0:T(8,128)(2,1)}, bf16[64,4096]{1,0:T(8,128)(2,1)S(1)}, u32[]{:S(2)}, u32[]{:S(2)}) collective-permute-start(bf16[64,4096]{1,0:T(8,128)(2,1)} %bitcast.10), channel_id=1, source_target_pairs={{0,2},{1,3},{2,0},{3,1},{4,6},{5,7},{6,4},{7,5},{8,10},{9,11},{10,... | collective-permute-start | bytes 1572872 | tf_op jit(solution)/shard_map/ppermute | solution.py:45
  2.1 1.4 %tails.1.refs_4_ = bf16[144,128]{1,0:T(8,128)(2,1)} custom-call(bf16[4096,512]{1,0:T(8,128)(2,1)} %refs_1_.7, bf16[64,4096]{1,0:T(8,128)(2,1)} %bitcast.11, bf16[4,64]{1,0:T(4,128)(2,1)} %w_ref.1), custom_call_target="tpu_custom_call" | custom-call | flops 2147483648 | bytes 1048576 | tf_op jit(solution)/shard_map/tails/pallas_call | solution.py:109
  3.5 1.6 %collective-permute-start.2 = (bf16[144,128]{1,0:T(8,128)(2,1)}, bf16[144,128]{1,0:T(8,128)(2,1)S(1)}, u32[]{:S(2)}, u32[]{:S(2)}) collective-permute-start(bf16[144,128]{1,0:T(8,128)(2,1)} %tails.1.refs_4_), channel_id=1, source_target_pairs={{0,32},{32,64},{64,96},{96,128},{128,160},{160,192},{192,224},{224... | collective-permute-start | bytes 110600 | tf_op jit(solution)/shard_map/ppermute | solution.py:31
  5.2 0.1 pad_add_fusion.refs_0_
  5.3 0.0 copy-start.5
  5.3 0.8 %copy-done.5 = bf16[144,128]{1,0:T(8,128)(2,1)S(1)} copy-done((bf16[144,128]{1,0:T(8,128)(2,1)S(1)}, bf16[144,128]{1,0:T(8,128)(2,1)}, u32[]{:S(2)}) %copy-start.5) | copy-done | bytes 36888
  6.0 1.2 %decays.1 = (f32[8,4096]{1,0:T(8,128)S(1)}, f32[8,4096]{1,0:T(8,128)S(1)}, f32[8,4096]{1,0:T(8,128)S(1)}, f32[32,512]{1,0:T(8,128)S(1)}, f32[1,512]{1,0:T(1,128)S(1)}) custom-call(f32[8,4096]{1,0:T(8,128)S(1)} %bitcast.15, f32[1,8]{1,0:T(1,128)S(1)} %bitcast.16, f32[1,8]{1,0:T(1,128)S(1)} %bitcast.17, f32[1,8]{1,0:T(1,128)S(1)} %bitcast.18, ...), custom_call_target="tpu_custom_call" | custom-call | flops 2621440000 | bytes 524288 | tf_op jit(solution)/shard_map/decays/pallas_call | solution.py:229
  7.2 1.0 %copy-done.1 = bf16[4096,512]{1,0:T(8,128)(2,1)S(1)} copy-done((bf16[4096,512]{1,0:T(8,128)(2,1)S(1)}, bf16[4096,512]{1,0:T(8,128)(2,1)}, u32[]{:S(2)}) %copy-start.1) | copy-done | bytes 4194328
  8.2 2.2 %chan_conv.4 = (bf16[1024,512]{1,0:T(8,128)(2,1)S(1)}, bf16[1024,512]{1,0:T(8,128)(2,1)S(1)}, f32[8,128]{1,0:T(8,128)S(1)}) custom-call(s32[3]{0:T(128)S(1)} %pad_add_fusion.refs_0_, bf16[4096,512]{1,0:T(8,128)(2,1)S(1)} %copy-done.1, bf16[4,512]{1,0:T(4,128)(2,1)S(1)} %copy-done.6, f32[8,4096]{1,0:T(8,128)S(1)} %get-tuple-element.28.refs_3_.refs_4_, ...), custom_call_target="tpu_custom_call" | custom-call | flops 2097152000 | bytes 3145728 | tf_op jit(solution)/shard_map/chan_conv/pallas_call | solution.py:302
  10.4 0.2 collective-permute-done.2.refs_5_
  10.7 0.3 collective-permute-start.3
  10.9 2.2 %chan_conv.5 = (bf16[1024,512]{1,0:T(8,128)(2,1)S(1)}, bf16[1024,512]{1,0:T(8,128)(2,1)S(1)}, f32[8,128]{1,0:T(8,128)S(1)}) custom-call(s32[3]{0:T(128)S(1)} %pad_add_fusion.refs_0_, bf16[4096,512]{1,0:T(8,128)(2,1)S(1)} %copy-done.1, bf16[4,512]{1,0:T(4,128)(2,1)S(1)} %copy-done.6, f32[8,4096]{1,0:T(8,128)S(1)} %get-tuple-element.28.refs_3_.refs_4_, ...), custom_call_target="tpu_custom_call" | custom-call | flops 2097152000 | bytes 3145728 | tf_op jit(solution)/shard_map/chan_conv/pallas_call | solution.py:302
  13.1 0.0 copy-start.3
  13.1 2.2 %chan_conv.6 = (bf16[1024,512]{1,0:T(8,128)(2,1)S(1)}, bf16[1024,512]{1,0:T(8,128)(2,1)S(1)}, f32[8,128]{1,0:T(8,128)S(1)}) custom-call(s32[3]{0:T(128)S(1)} %pad_add_fusion.refs_0_, bf16[4096,512]{1,0:T(8,128)(2,1)S(1)} %copy-done.1, bf16[4,512]{1,0:T(4,128)(2,1)S(1)} %copy-done.6, f32[8,4096]{1,0:T(8,128)S(1)} %get-tuple-element.28.refs_3_.refs_4_, ...), custom_call_target="tpu_custom_call" | custom-call | flops 2097152000 | bytes 3145728 | tf_op jit(solution)/shard_map/chan_conv/pallas_call | solution.py:302
  15.3 0.0 collective-permute-done.3.refs_7_
  15.3 0.0 collective-permute-done.1.refs_3_.refs_6_
  15.3 2.2 %collective-permute-start.4 = (bf16[64,4096]{1,0:T(8,128)(2,1)S(1)}, bf16[64,4096]{1,0:T(8,128)(2,1)S(1)}, u32[]{:S(2)}, u32[]{:S(2)}) collective-permute-start(bf16[64,4096]{1,0:T(8,128)(2,1)S(1)} %collective-permute-done.1.refs_3_.refs_6_), channel_id=1, source_target_pairs={{0,1},{1,0},{2,3},{3,2},{4,5},{5,4},{6,7},{7,6},{8,9},{9,8},{10,11... | collective-permute-start | bytes 1572872 | tf_op jit(solution)/shard_map/ppermute | solution.py:45
  17.5 0.1 collective-permute-start
  17.6 0.4 collective-permute-start.5
  18.0 0.1 collective-permute-start.6
  18.2 2.2 %chan_conv.7 = (bf16[1024,512]{1,0:T(8,128)(2,1)S(1)}, bf16[1024,512]{1,0:T(8,128)(2,1)S(1)}, f32[8,128]{1,0:T(8,128)}) custom-call(s32[3]{0:T(128)S(1)} %pad_add_fusion.refs_0_, bf16[4096,512]{1,0:T(8,128)(2,1)S(1)} %copy-done.1, bf16[4,512]{1,0:T(4,128)(2,1)S(1)} %copy-done.6, f32[8,4096]{1,0:T(8,128)S(1)} %get-tuple-element.28.refs_3_.refs_4_, ...), custom_call_target="tpu_custom_call" | custom-call | flops 2097152000 | bytes 3145728 | tf_op jit(solution)/shard_map/chan_conv/pallas_call | solution.py:302
  20.4 0.0 collective-permute-done.4.refs_4_
  20.4 0.0 collective-permute-done.5.refs_6_
  20.4 0.0 collective-permute-done.refs_2_
  20.4 0.0 collective-permute-done.6.refs_8_
  20.4 2.1 %proj_conv.2.b_ref.refs_1_ = bf16[128,4096]{1,0:T(8,128)(2,1)S(1)} custom-call(s32[3]{0:T(128)S(1)} %pad_add_fusion.refs_0_, bf16[64,4096]{1,0:T(8,128)(2,1)S(1)} %bitcast.13, bf16[64,4096]{1,0:T(8,128)(2,1)S(1)} %collective-permute-done.refs_2_, bf16[64,4096]{1,0:T(8,128)(2,1)S(1)} %collective-permute-done.1.refs_3_.refs_6_, ...), custom_call_target="tpu_custom_call" | custom-call | flops 1048576000 | bytes 1572864 | tf_op jit(solution)/shard_map/proj_conv/pallas_call | solution.py:175
  22.5 1.3 %states.1 = (bf16[32,128,512]{2,1,0:T(8,128)(2,1)S(1)}, bf16[144,512]{1,0:T(8,128)(2,1)S(1)}) custom-call(bf16[128,4096]{1,0:T(8,128)(2,1)S(1)} %proj_conv.2.b_ref.refs_1_, f32[32,512]{1,0:T(8,128)S(1)} %get-tuple-element.35.tot_ref, bf16[1024,512]{1,0:T(8,128)(2,1)S(1)} %get-tuple-element.37.rest_0_, bf16[1024,512]{1,0:T(8,128)(2,1)S(1)} %get-tuple-element.38.rest_1_, ...), custom_call_target="tpu_custom_call" | custom-call | flops 4194304000 | bytes 8388608 | tf_op jit(solution)/shard_map/states/pallas_call | solution.py:385
  23.8 4.4 %collective-permute-start.7 = (bf16[144,512]{1,0:T(8,128)(2,1)S(1)}, bf16[144,512]{1,0:T(8,128)(2,1)S(1)}, u32[]{:S(2)}, u32[]{:S(2)}) collective-permute-start(bf16[144,512]{1,0:T(8,128)(2,1)S(1)} %get-tuple-element.41.refs_9_.refs_1_), channel_id=1, source_target_pairs={{0,32},{1,225},{2,34},{3,227},{4,36},{5,229},{6,38},{7,231},{8,40}... | collective-permute-start | bytes 442376 | tf_op jit(solution)/shard_map/ppermute | solution.py:41
  28.2 2.1 %proj_conv.3.refs_3_.refs_2_.refs_1_ = bf16[128,4096]{1,0:T(8,128)(2,1)S(1)} custom-call(s32[3]{0:T(128)S(1)} %pad_add_fusion.refs_0_, bf16[64,4096]{1,0:T(8,128)(2,1)S(1)} %bitcast.14, bf16[64,4096]{1,0:T(8,128)(2,1)S(1)} %collective-permute-done.refs_2_, bf16[64,4096]{1,0:T(8,128)(2,1)S(1)} %collective-permute-done.1.refs_3_.refs_6_, ...), custom_call_target="tpu_custom_call" | custom-call | flops 1048576000 | bytes 1572864 | tf_op jit(solution)/shard_map/proj_conv/pallas_call | solution.py:175
  30.4 0.0 collective-permute-done.7.refs_2_.refs_8_
  30.4 0.6 merge.2.refs_7_.refs_1_
  31.0 2.7 %collective-permute-start.8 = (bf16[144,512]{1,0:T(8,128)(2,1)S(1)}, bf16[144,512]{1,0:T(8,128)(2,1)S(1)}, u32[]{:S(2)}, u32[]{:S(2)}) collective-permute-start(bf16[144,512]{1,0:T(8,128)(2,1)S(1)} %merge.2.refs_7_.refs_1_), channel_id=1, source_target_pairs={{0,64},{1,193},{2,66},{3,195},{4,68},{5,197},{6,70},{7,199},{8,72}... | collective-permute-start | bytes 442376 | tf_op jit(solution)/shard_map/ppermute | solution.py:41
  33.7 2.7 %local.4.refs_8_.refs_4_ = bf16[1024,512]{1,0:T(8,128)(2,1)S(1)} custom-call(bf16[1024,512]{1,0:T(8,128)(2,1)S(1)} %get-tuple-element.43.refs_0_, bf16[128,4096]{1,0:T(8,128)(2,1)S(1)} %proj_conv.2.b_ref.refs_1_, bf16[128,4096]{1,0:T(8,128)(2,1)S(1)} %proj_conv.3.refs_3_.refs_2_.refs_1_, bf16[32,128,512]{2,1,0:T(8,128)(2,1)S(1)} %get-tuple-element.44.refs_3_, ...), custom_call_target="tpu_custom_call" | custom-call | flops 4194304000 | bytes 3145728 | tf_op jit(solution)/shard_map/local/pallas_call | solution.py:445
  36.4 2.7 %local.5.refs_3_.refs_5_ = bf16[1024,512]{1,0:T(8,128)(2,1)S(1)} custom-call(bf16[1024,512]{1,0:T(8,128)(2,1)S(1)} %get-tuple-element.46.refs_0_, bf16[128,4096]{1,0:T(8,128)(2,1)S(1)} %proj_conv.2.b_ref.refs_1_, bf16[128,4096]{1,0:T(8,128)(2,1)S(1)} %proj_conv.3.refs_3_.refs_2_.refs_1_, bf16[32,128,512]{2,1,0:T(8,128)(2,1)S(1)} %get-tuple-element.44.refs_3_, ...), custom_call_target="tpu_custom_call" | custom-call | flops 4194304000 | bytes 3145728 | tf_op jit(solution)/shard_map/local/pallas_call | solution.py:445
  39.1 0.0 collective-permute-done.8.refs_2_.refs_9_
  39.1 0.6 merge.3.refs_7_
  39.7 2.2 %collective-permute-start.9 = (bf16[144,512]{1,0:T(8,128)(2,1)S(1)}, bf16[144,512]{1,0:T(8,128)(2,1)S(1)}, u32[]{:S(2)}, u32[]{:S(2)}) collective-permute-start(bf16[144,512]{1,0:T(8,128)(2,1)S(1)} %merge.3.refs_7_), channel_id=1, source_target_pairs={{0,128},{1,129},{2,130},{3,131},{4,132},{5,133},{6,134},{7,135},{8... | collective-permute-start | bytes 442376 | tf_op jit(solution)/shard_map/ppermute | solution.py:41
  41.9 2.7 %local.7.refs_7_ = bf16[1024,512]{1,0:T(8,128)(2,1)S(1)} custom-call(bf16[1024,512]{1,0:T(8,128)(2,1)S(1)} %get-tuple-element.48.refs_0_, bf16[128,4096]{1,0:T(8,128)(2,1)S(1)} %proj_conv.2.b_ref.refs_1_, bf16[128,4096]{1,0:T(8,128)(2,1)S(1)} %proj_conv.3.refs_3_.refs_2_.refs_1_, bf16[32,128,512]{2,1,0:T(8,128)(2,1)S(1)} %get-tuple-element.44.refs_3_, ...), custom_call_target="tpu_custom_call" | custom-call | flops 4194304000 | bytes 3145728 | tf_op jit(solution)/shard_map/local/pallas_call | solution.py:445
  44.6 0.0 copy-start.2
  44.6 2.7 %local.6.refs_6_ = bf16[1024,512]{1,0:T(8,128)(2,1)S(1)} custom-call(bf16[1024,512]{1,0:T(8,128)(2,1)S(1)} %get-tuple-element.47.refs_0_, bf16[128,4096]{1,0:T(8,128)(2,1)S(1)} %proj_conv.2.b_ref.refs_1_, bf16[128,4096]{1,0:T(8,128)(2,1)S(1)} %proj_conv.3.refs_3_.refs_2_.refs_1_, bf16[32,128,512]{2,1,0:T(8,128)(2,1)S(1)} %get-tuple-element.44.refs_3_, ...), custom_call_target="tpu_custom_call" | custom-call | flops 4194304000 | bytes 3145728 | tf_op jit(solution)/shard_map/local/pallas_call | solution.py:445
  47.3 2.0 %collective-permute-done.9.refs_10_ = bf16[144,512]{1,0:T(8,128)(2,1)S(1)} collective-permute-done((bf16[144,512]{1,0:T(8,128)(2,1)S(1)}, bf16[144,512]{1,0:T(8,128)(2,1)S(1)}, u32[]{:S(2)}, u32[]{:S(2)}) %collective-permute-start.9) | collective-permute-done | bytes 147488 | tf_op jit(solution)/shard_map/ppermute | solution.py:41
  49.3 4.7 %carry.1 = (bf16[4096,512]{1,0:T(8,128)(2,1)S(1)}, f32[32,128]{1,0:T(8,128)S(1)}) custom-call(s32[3]{0:T(128)S(1)} %pad_add_fusion.refs_0_, bf16[128,4096]{1,0:T(8,128)(2,1)S(1)} %proj_conv.3.refs_3_.refs_2_.refs_1_, f32[8,4096]{1,0:T(8,128)S(1)} %get-tuple-element.42.refs_2_, bf16[4096,512]{1,0:T(8,128)(2,1)S(1)} %copy-done.2, ...), custom_call_target="tpu_custom_call" | custom-call | flops 8388608000 | bytes 12582912 | tf_op jit(solution)/shard_map/carry/pallas_call | solution.py:513
  54.1 5.2 %collective-permute-start.12 = (f32[32,128]{1,0:T(8,128)S(1)}, f32[32,128]{1,0:T(8,128)S(1)}, u32[]{:S(2)}, u32[]{:S(2)}) collective-permute-start(f32[32,128]{1,0:T(8,128)S(1)} %get-tuple-element.50), channel_id=1, source_target_pairs={{0,3},{1,2},{2,1},{3,0},{4,7},{5,6},{6,5},{7,4},{8,11},{9,10},{10,... | collective-permute-start | bytes 49160 | tf_op jit(solution)/shard_map/ppermute | solution.py:45
  59.3 0.3 collective-permute-start.11
  59.5 0.2 collective-permute-start.10
  59.8 1.3 %collective-permute-done.12 = f32[32,128]{1,0:T(8,128)S(1)} collective-permute-done((f32[32,128]{1,0:T(8,128)S(1)}, f32[32,128]{1,0:T(8,128)S(1)}, u32[]{:S(2)}, u32[]{:S(2)}) %collective-permute-start.12) | collective-permute-done | bytes 16416 | tf_op jit(solution)/shard_map/ppermute | solution.py:45
  61.1 0.8 %collective-permute-done.11 = f32[32,128]{1,0:T(8,128)S(1)} collective-permute-done((f32[32,128]{1,0:T(8,128)S(1)}, f32[32,128]{1,0:T(8,128)S(1)}, u32[]{:S(2)}, u32[]{:S(2)}) %collective-permute-start.11) | collective-permute-done | bytes 16416 | tf_op jit(solution)/shard_map/ppermute | solution.py:45
  61.9 2.7 %norm.1 = bf16[4096,512]{1,0:T(8,128)(2,1)} custom-call(bf16[4096,512]{1,0:T(8,128)(2,1)S(1)} %get-tuple-element.49.refs_0_, f32[32,128]{1,0:T(8,128)S(1)} %add_add_fusion.refs_1_, f32[1,512]{1,0:T(1,128)S(1)} %bitcast.9), custom_call_target="tpu_custom_call" | custom-call | flops 6291456 | bytes 8388608 | tf_op jit(solution)/shard_map/norm/pallas_call | solution.py:548
  (17 shorter events, 0.0 us)
Async XLA Ops:
  0.0 5.2 %copy-start.9 = (f32[8]{0:T(128)S(1)}, f32[8]{0:T(128)}, u32[]{:S(2)}) copy-start(f32[8]{0:T(128)} %param.16) | copy-start | bytes 100
  0.0 5.2 %copy-start.8 = (f32[8]{0:T(128)S(1)}, f32[8]{0:T(128)}, u32[]{:S(2)}) copy-start(f32[8]{0:T(128)} %param.15) | copy-start | bytes 100
  0.0 5.2 %copy-start.7 = (f32[8]{0:T(128)S(1)}, f32[8]{0:T(128)}, u32[]{:S(2)}) copy-start(f32[8]{0:T(128)} %param.14) | copy-start | bytes 100
  0.0 5.2 %copy-start.4 = (f32[4096,8]{0,1:T(8,128)S(1)}, f32[4096,8]{0,1:T(8,128)}, u32[]{:S(2)}) copy-start(f32[4096,8]{0,1:T(8,128)} %param.13) | copy-start | bytes 393220
  0.0 15.3 %collective-permute-start.1 = (bf16[64,4096]{1,0:T(8,128)(2,1)}, bf16[64,4096]{1,0:T(8,128)(2,1)S(1)}, u32[]{:S(2)}, u32[]{:S(2)}) collective-permute-start(bf16[64,4096]{1,0:T(8,128)(2,1)} %bitcast.10), channel_id=1, source_target_pairs={{0,2},{1,3},{2,0},{3,1},{4,6},{5,7},{6,4},{7,5},{8,10},{9,11},{10,... | collective-permute-start | bytes 1572872 | tf_op jit(solution)/shard_map/ppermute | solution.py:45
  3.5 7.1 %collective-permute-start.2 = (bf16[144,128]{1,0:T(8,128)(2,1)}, bf16[144,128]{1,0:T(8,128)(2,1)S(1)}, u32[]{:S(2)}, u32[]{:S(2)}) collective-permute-start(bf16[144,128]{1,0:T(8,128)(2,1)} %tails.1.refs_4_), channel_id=1, source_target_pairs={{0,32},{32,64},{64,96},{96,128},{128,160},{160,192},{192,224},{224... | collective-permute-start | bytes 110600 | tf_op jit(solution)/shard_map/ppermute | solution.py:31
  5.3 0.8 %copy-start.5 = (bf16[144,128]{1,0:T(8,128)(2,1)S(1)}, bf16[144,128]{1,0:T(8,128)(2,1)}, u32[]{:S(2)}) copy-start(bf16[144,128]{1,0:T(8,128)(2,1)} %tails.1.refs_4_) | copy-start | bytes 110596
  6.0 2.2 %copy-start.1 = (bf16[4096,512]{1,0:T(8,128)(2,1)S(1)}, bf16[4096,512]{1,0:T(8,128)(2,1)}, u32[]{:S(2)}) copy-start(bf16[4096,512]{1,0:T(8,128)(2,1)} %refs_1_.7) | copy-start | bytes 12582916
  6.0 2.2 %copy-start.6 = (bf16[4,512]{1,0:T(4,128)(2,1)S(1)}, bf16[4,512]{1,0:T(4,128)(2,1)}, u32[]{:S(2)}) copy-start(bf16[4,512]{1,0:T(4,128)(2,1)} %refs_2_.7) | copy-start | bytes 12292
  10.7 4.7 %collective-permute-start.3 = (bf16[144,128]{1,0:T(8,128)(2,1)S(1)}, bf16[144,128]{1,0:T(8,128)(2,1)S(1)}, u32[]{:S(2)}, u32[]{:S(2)}) collective-permute-start(bf16[144,128]{1,0:T(8,128)(2,1)S(1)} %collective-permute-done.2.refs_5_), channel_id=1, source_target_pairs={{0,2},{1,3},{2,0},{3,1},{4,6},{5,7},{6,4},{7,5},{8,10},{9,11},{10,... | collective-permute-start | bytes 110600 | tf_op jit(solution)/shard_map/ppermute | solution.py:45
  13.1 4.4 %copy-start.3 = (bf16[4096,64]{0,1:T(8,128)(2,1)S(1)}, bf16[4096,64]{0,1:T(8,128)(2,1)}, u32[]{:S(2)}) copy-start(bf16[4096,64]{0,1:T(8,128)(2,1)} %param.12) | copy-start | bytes 1572868
  15.3 5.0 %collective-permute-start.4 = (bf16[64,4096]{1,0:T(8,128)(2,1)S(1)}, bf16[64,4096]{1,0:T(8,128)(2,1)S(1)}, u32[]{:S(2)}, u32[]{:S(2)}) collective-permute-start(bf16[64,4096]{1,0:T(8,128)(2,1)S(1)} %collective-permute-done.1.refs_3_.refs_6_), channel_id=1, source_target_pairs={{0,1},{1,0},{2,3},{3,2},{4,5},{5,4},{6,7},{7,6},{8,9},{9,8},{10,11... | collective-permute-start | bytes 1572872 | tf_op jit(solution)/shard_map/ppermute | solution.py:45
  17.5 2.8 %collective-permute-start = (bf16[64,4096]{1,0:T(8,128)(2,1)S(1)}, bf16[64,4096]{1,0:T(8,128)(2,1)S(1)}, u32[]{:S(2)}, u32[]{:S(2)}) collective-permute-start(bf16[64,4096]{1,0:T(8,128)(2,1)S(1)} %bitcast.12), channel_id=1, source_target_pairs={{0,1},{1,0},{2,3},{3,2},{4,5},{5,4},{6,7},{7,6},{8,9},{9,8},{10,11... | collective-permute-start | bytes 1572872 | tf_op jit(solution)/shard_map/ppermute | solution.py:45
  17.6 2.7 %collective-permute-start.5 = (bf16[144,128]{1,0:T(8,128)(2,1)S(1)}, bf16[144,128]{1,0:T(8,128)(2,1)S(1)}, u32[]{:S(2)}, u32[]{:S(2)}) collective-permute-start(bf16[144,128]{1,0:T(8,128)(2,1)S(1)} %collective-permute-done.2.refs_5_), channel_id=1, source_target_pairs={{0,1},{1,0},{2,3},{3,2},{4,5},{5,4},{6,7},{7,6},{8,9},{9,8},{10,11... | collective-permute-start | bytes 110600 | tf_op jit(solution)/shard_map/ppermute | solution.py:45
  18.0 2.3 %collective-permute-start.6 = (bf16[144,128]{1,0:T(8,128)(2,1)S(1)}, bf16[144,128]{1,0:T(8,128)(2,1)S(1)}, u32[]{:S(2)}, u32[]{:S(2)}) collective-permute-start(bf16[144,128]{1,0:T(8,128)(2,1)S(1)} %collective-permute-done.3.refs_7_), channel_id=1, source_target_pairs={{0,1},{1,0},{2,3},{3,2},{4,5},{5,4},{6,7},{7,6},{8,9},{9,8},{10,11... | collective-permute-start | bytes 110600 | tf_op jit(solution)/shard_map/ppermute | solution.py:45
  23.8 6.5 %collective-permute-start.7 = (bf16[144,512]{1,0:T(8,128)(2,1)S(1)}, bf16[144,512]{1,0:T(8,128)(2,1)S(1)}, u32[]{:S(2)}, u32[]{:S(2)}) collective-permute-start(bf16[144,512]{1,0:T(8,128)(2,1)S(1)} %get-tuple-element.41.refs_9_.refs_1_), channel_id=1, source_target_pairs={{0,32},{1,225},{2,34},{3,227},{4,36},{5,229},{6,38},{7,231},{8,40}... | collective-permute-start | bytes 442376 | tf_op jit(solution)/shard_map/ppermute | solution.py:41
  31.0 8.1 %collective-permute-start.8 = (bf16[144,512]{1,0:T(8,128)(2,1)S(1)}, bf16[144,512]{1,0:T(8,128)(2,1)S(1)}, u32[]{:S(2)}, u32[]{:S(2)}) collective-permute-start(bf16[144,512]{1,0:T(8,128)(2,1)S(1)} %merge.2.refs_7_.refs_1_), channel_id=1, source_target_pairs={{0,64},{1,193},{2,66},{3,195},{4,68},{5,197},{6,70},{7,199},{8,72}... | collective-permute-start | bytes 442376 | tf_op jit(solution)/shard_map/ppermute | solution.py:41
  39.7 9.6 %collective-permute-start.9 = (bf16[144,512]{1,0:T(8,128)(2,1)S(1)}, bf16[144,512]{1,0:T(8,128)(2,1)S(1)}, u32[]{:S(2)}, u32[]{:S(2)}) collective-permute-start(bf16[144,512]{1,0:T(8,128)(2,1)S(1)} %merge.3.refs_7_), channel_id=1, source_target_pairs={{0,128},{1,129},{2,130},{3,131},{4,132},{5,133},{6,134},{7,135},{8... | collective-permute-start | bytes 442376 | tf_op jit(solution)/shard_map/ppermute | solution.py:41
  44.6 4.7 %copy-start.2 = (bf16[4096,512]{1,0:T(8,128)(2,1)S(1)}, bf16[4096,512]{1,0:T(8,128)(2,1)}, u32[]{:S(2)}) copy-start(bf16[4096,512]{1,0:T(8,128)(2,1)} %refs_3_.1) | copy-start | bytes 12582916
  49.3 12.6 %copy-start = (f32[512]{0:T(512)S(1)}, f32[512]{0:T(512)}, u32[]{:S(2)}) copy-start(f32[512]{0:T(512)} %param.19) | copy-start | bytes 6148
  54.1 7.0 %collective-permute-start.12 = (f32[32,128]{1,0:T(8,128)S(1)}, f32[32,128]{1,0:T(8,128)S(1)}, u32[]{:S(2)}, u32[]{:S(2)}) collective-permute-start(f32[32,128]{1,0:T(8,128)S(1)} %get-tuple-element.50), channel_id=1, source_target_pairs={{0,3},{1,2},{2,1},{3,0},{4,7},{5,6},{6,5},{7,4},{8,11},{9,10},{10,... | collective-permute-start | bytes 49160 | tf_op jit(solution)/shard_map/ppermute | solution.py:45
  59.3 2.6 %collective-permute-start.11 = (f32[32,128]{1,0:T(8,128)S(1)}, f32[32,128]{1,0:T(8,128)S(1)}, u32[]{:S(2)}, u32[]{:S(2)}) collective-permute-start(f32[32,128]{1,0:T(8,128)S(1)} %get-tuple-element.50), channel_id=1, source_target_pairs={{0,2},{1,3},{2,0},{3,1},{4,6},{5,7},{6,4},{7,5},{8,10},{9,11},{10,... | collective-permute-start | bytes 49160 | tf_op jit(solution)/shard_map/ppermute | solution.py:45
  59.5 2.3 %collective-permute-start.10 = (f32[32,128]{1,0:T(8,128)S(1)}, f32[32,128]{1,0:T(8,128)S(1)}, u32[]{:S(2)}, u32[]{:S(2)}) collective-permute-start(f32[32,128]{1,0:T(8,128)S(1)} %get-tuple-element.50), channel_id=1, source_target_pairs={{0,1},{1,0},{2,3},{3,2},{4,5},{5,4},{6,7},{7,6},{8,9},{9,8},{10,11... | collective-permute-start | bytes 49160 | tf_op jit(solution)/shard_map/ppermute | solution.py:45

commit v4 on v3

--- a/solution.py
+++ b/solution.py
@@ -453,11 +453,43 @@
     )(x_conv, b_t, c_t, entering, run, step, skip, *needs)
 
 
-def carry_kernel(nloc, devices, flag_ref, c_ref, abs_ref, z_ref, *rest):
+def gate_kernel(z_ref, abs_ref, g_ref, w_ref):
+    tokens, chans = z_ref.shape
+    spread = head_spread(abs_ref.shape[0], chans)
+
+    @pl.loop(0, tokens // BLK, unroll=4)
+    def _(i):
+        at = block_at(i)
+        wide = lax.dot_general(
+            jnp.exp2(abs_ref[:, at]).astype(BF16),
+            spread,
+            (((0,), (0,)), ((), ())),
+            preferred_element_type=F32,
+        )
+        for lo in range(0, chans, BLK):
+            lanes = slice(lo, lo + BLK)
+            gate = half_silu(0.5 * z_ref[at, lanes].astype(F32))
+            g_ref[at, lanes] = gate.astype(BF16)
+            w_ref[at, lanes] = (gate * wide[:, lanes]).astype(BF16)
+
+
+def gates(z, whole, needs):
+    tokens, chans = z.shape
+    return pl.pallas_call(
+        ordered(gate_kernel, 2, len(needs)),
+        in_specs=specs(2) + unread(needs),
+        out_specs=tuple(specs(2)),
+        out_shape=(jax.ShapeDtypeStruct((tokens, chans), BF16),) * 2,
+        compiler_params=params(),
+        cost_estimate=cost(tokens * chans * 1500, tokens * chans * 6, tokens * chans),
+        name="gates",
+    )(z, whole, *needs)
+
+
+def carry_kernel(nloc, devices, flag_ref, c_ref, gate_ref, fall_ref, *rest):
     l_refs, msgs = rest[:nloc], rest[nloc:-3]
     g_ref, q_ref, s_ref = rest[-3:]
     chans = g_ref.shape[1]
-    heads = abs_ref.shape[0]
     pos = flag_ref[1]
     even = flag_ref[2] == 0
     near_ref, mid_ref, wide_ref = msgs
@@ -474,7 +506,6 @@
     near, wide = near_ref[0:STATE, :].astype(F32), wide_ref[0:STATE, :].astype(F32)
     total = last_ok * jnp.where(even, near, wide) + mid_fall * jnp.where(even, wide, near)
     s_ref[...] = (total + last_fall * mid_ref[0:STATE, :].astype(F32)).astype(BF16)
-    spread = head_spread(heads, chans)
     done = 0
     for l_ref in l_refs:
         count = l_ref.shape[0] // BLK
@@ -485,27 +516,20 @@
         def _(i):
             at = block_at(first + i)
             c = jnp.transpose(c_ref[:, at])
-            wide = lax.dot_general(
-                jnp.exp2(abs_ref[:, at]).astype(BF16),
-                spread,
-                (((0,), (0,)), ((), ())),
-                preferred_element_type=F32,
-            )
             carried = jnp.dot(c, s_ref[...], preferred_element_type=F32)
             folded = None
             for lo in range(0, chans, BLK):
                 lanes = slice(lo, lo + BLK)
-                gated = l_ref[block_at(i), lanes].astype(F32) + wide[:, lanes] * carried[:, lanes]
-                gated = gated * half_silu(0.5 * z_ref[at, lanes].astype(F32))
+                gated = l_ref[block_at(i), lanes].astype(F32) * gate_ref[at, lanes].astype(F32)
+                gated = gated + fall_ref[at, lanes].astype(F32) * carried[:, lanes]
                 g_ref[at, lanes] = gated.astype(BF16)
                 square = gated * gated
                 folded = square if folded is None else folded + square
             q_ref[pl.ds(first + i, 1), :] = jnp.sum(jnp.transpose(folded), axis=0, keepdims=True)
 
 
-def carry(flag, locs, gate, c_t, whole, msgs, devices):
-    heads, tokens = whole.shape
-    chans = locs[0].shape[1]
+def carry(flag, locs, gate, fall, c_t, msgs, devices):
+    tokens, chans = gate.shape
 
     def kernel(*refs):
         carry_kernel(len(locs), devices, *refs)
@@ -522,7 +546,7 @@
         compiler_params=params(),
         cost_estimate=cost(4000 * tokens * chans, tokens * chans * 6, tokens * chans),
         name="carry",
-    )(flag, c_t, whole, gate, *locs, *msgs)
+    )(flag, c_t, gate, fall, *locs, *msgs)
 
 
 def norm_kernel(width, g_ref, q_ref, gain_ref, o_ref):
@@ -572,7 +596,7 @@
     near_raw = swapped(proj_t, "head", 1)
     ends = tails(x_stream, proj_t, conv_proj)
     halo = rotated(ends, "ctx", 1)
-    run, whole, step, totals, skip = decays(dt_raw.T, dt_bias, a_log, skip_d, chans, (ends,))
+    run, whole, step, totals, skip = decays(dt_raw.T, dt_bias, a_log, skip_d, chans)
 
     def conv(part, *needs):
         return chan_conv(flag, x_stream, conv_x, run, step, halo, part, 4, needs)
@@ -603,7 +627,8 @@
         return locs[-1]
 
     one = opposed(message, 1)
-    pair = merge(flag, message, one, 1, count, (c_t,))
+    gate, fall = gates(gate_z, whole, (message, c_t))
+    pair = merge(flag, message, one, 1, count, (fall,))
     two = opposed(pair, 2)
     piece(0, pair)
     last = piece(1, pair, locs[0])
@@ -614,7 +639,7 @@
     msgs = (one, two, four)
 
     width = HEADS // GROUPS * (chans // heads)
-    gated, squares = carry(flag, locs, gate_z, c_t, whole, msgs, count)
+    gated, squares = carry(flag, locs, gate, fall, c_t, msgs, count)
     squares = (squares + swapped(squares, "head", 1)) + (
         swapped(squares, "head", 2) + swapped(squares, "head", 3)
     )

time: 64.7 us -> 64.9 us (level)
  Pallas kernels: 36.3 us -> 38.5 us
  starting transfers between devices: 21.8 us -> 19.6 us
  waiting for transfers between devices: 4.35 us -> 5.33 us
  local copies, waits for them, and re-layouts: 1.82 us -> 1.04 us
    pallas_call x0 -> x1, Pallas kernels: none -> 3.24 us  [gates(): pl.pallas_call(ordered(gate_kernel, 2, len(needs)), in_specs=specs(2) + u...]
    ppermute x9, starting transfers between devices: 10.9 us -> 9.73 us  [swapped(): lax.ppermute(value, axis, [(i, i ^ mask) for i in range(lax.axis_size(axi...]
    pallas_call x1, Pallas kernels: 4.74 us -> 3.6 us  [carry(): pl.pallas_call(kernel, in_specs=specs(4 + len(locs) + len(msgs), 1), out_...]
    ppermute x3, starting transfers between devices: 9.24 us -> 8.21 us  [opposed(): return lax.ppermute(x, ('ctx', 'head'), pairs)]
    unnamed x20 -> x18, local copies, waits for them, and re-layouts: 1.82 us -> 1.04 us
    ppermute x1, waiting for transfers between devices: 0.25 us -> 1.01 us  [rotated(): return lax.ppermute(x, axis, [(i, (i + by) % count) for i in range(count)])]
  transfers between devices with their start and end apart: 13 -> 13, of which waited for: 4 -> 4; matrix products, arithmetic and copies ran while one was open for 0% -> 0% of each run, Pallas kernels for 38% -> 42%
where the time goes in v4:
time: 64.9 us; the launch traced here: 64.8 us
  Pallas kernels  38.5 us (59%)
  starting transfers between devices  19.6 us (30%)
  waiting for transfers between devices  5.33 us (8%)
  local copies, waits for them, and re-layouts  1.04 us (2%)
    pallas_call x4, Pallas kernels, local(): pl.pallas_call(ordered(kernel, 7, len(needs)), in_specs=specs(7) + unread...  10.8 us
    ppermute x9, starting transfers between devices, swapped(): lax.ppermute(value, axis, [(i, i ^ mask) for i in range(lax.axis_size(axi...  9.73 us
    pallas_call x4, Pallas kernels, chan_conv(): pl.pallas_call(ordered(kernel, 5 + (part == 0), len(needs)), in_specs=spe...  8.77 us
    ppermute x3, starting transfers between devices, opposed(): return lax.ppermute(x, ('ctx', 'head'), pairs)  8.21 us
    pallas_call x2, Pallas kernels, proj_conv(): pl.pallas_call(ordered(kernel, 9, len(needs)), in_specs=specs(9, 1) + unr...  4.29 us
    pallas_call x1, Pallas kernels, carry(): pl.pallas_call(kernel, in_specs=specs(4 + len(locs) + len(msgs), 1), out_...  3.6 us
    pallas_call x1, Pallas kernels, gates(): pl.pallas_call(ordered(gate_kernel, 2, len(needs)), in_specs=specs(2) + u...  3.24 us
    pallas_call x1, Pallas kernels, norm(): pl.pallas_call(kernel, grid=(tokens // rows,), in_specs=specs(3), out_spe...  2.66 us
  transfers between devices with their start and end apart: 13, of which 4 were waited for; matrix products, arithmetic and copies ran while one was open for 0% of the time, Pallas kernels for 42%

profile of v4, /device:TPU:1, one launch (start us, length us, event | category | flops | bytes accessed | tf_op | source)
XLA Modules:
  0.0 64.8 jit_solution(7825306623286153492)
XLA Ops:
  0.0 2.1 %collective-permute-start.1 = (bf16[64,4096]{1,0:T(8,128)(2,1)}, bf16[64,4096]{1,0:T(8,128)(2,1)S(1)}, u32[]{:S(2)}, u32[]{:S(2)}) collective-permute-start(bf16[64,4096]{1,0:T(8,128)(2,1)} %bitcast.10), channel_id=1, source_target_pairs={{0,2},{1,3},{2,0},{3,1},{4,6},{5,7},{6,4},{7,5},{8,10},{9,11},{10,... | collective-permute-start | bytes 1572872 | tf_op jit(solution)/shard_map/ppermute | solution.py:45
  2.1 1.4 %tails.1 = bf16[144,128]{1,0:T(8,128)(2,1)} custom-call(bf16[4096,512]{1,0:T(8,128)(2,1)} %refs_1_.7, bf16[64,4096]{1,0:T(8,128)(2,1)} %bitcast.11, bf16[4,64]{1,0:T(4,128)(2,1)} %w_ref.1), custom_call_target="tpu_custom_call" | custom-call | flops 2147483648 | bytes 1048576 | tf_op jit(solution)/shard_map/tails/pallas_call | solution.py:109
  3.5 1.6 %collective-permute-start.2 = (bf16[144,128]{1,0:T(8,128)(2,1)}, bf16[144,128]{1,0:T(8,128)(2,1)S(1)}, u32[]{:S(2)}, u32[]{:S(2)}) collective-permute-start(bf16[144,128]{1,0:T(8,128)(2,1)} %tails.1), channel_id=1, source_target_pairs={{0,32},{32,64},{64,96},{96,128},{128,160},{160,192},{192,224},{224... | collective-permute-start | bytes 110600 | tf_op jit(solution)/shard_map/ppermute | solution.py:31
  5.2 0.1 pad_add_fusion.refs_0_
  5.3 0.0 copy-start.1
  5.3 0.0 copy-start.5
  5.3 1.2 %decays.1 = (f32[8,4096]{1,0:T(8,128)S(1)}, f32[8,4096]{1,0:T(8,128)S(1)}, f32[8,4096]{1,0:T(8,128)S(1)}, f32[32,512]{1,0:T(8,128)S(1)}, f32[1,512]{1,0:T(1,128)S(1)}) custom-call(f32[8,4096]{1,0:T(8,128)S(1)} %bitcast.15, f32[1,8]{1,0:T(1,128)S(1)} %bitcast.16, f32[1,8]{1,0:T(1,128)S(1)} %bitcast.17, f32[1,8]{1,0:T(1,128)S(1)} %bitcast.18), custom_call_target="tpu_custom_call" | custom-call | flops 2621440000 | bytes 524288 | tf_op jit(solution)/shard_map/decays/pallas_call | solution.py:229
  6.4 1.0 %copy-done.1 = bf16[4096,512]{1,0:T(8,128)(2,1)S(1)} copy-done((bf16[4096,512]{1,0:T(8,128)(2,1)S(1)}, bf16[4096,512]{1,0:T(8,128)(2,1)}, u32[]{:S(2)}) %copy-start.1) | copy-done | bytes 4194328
  7.4 2.2 %chan_conv.4 = (bf16[1024,512]{1,0:T(8,128)(2,1)S(1)}, bf16[1024,512]{1,0:T(8,128)(2,1)S(1)}, f32[8,128]{1,0:T(8,128)S(1)}) custom-call(s32[3]{0:T(128)S(1)} %pad_add_fusion.refs_0_, bf16[4096,512]{1,0:T(8,128)(2,1)S(1)} %copy-done.1, bf16[4,512]{1,0:T(4,128)(2,1)S(1)} %copy-done.5, f32[8,4096]{1,0:T(8,128)S(1)} %get-tuple-element.30.refs_3_.refs_4_, ...), custom_call_target="tpu_custom_call" | custom-call | flops 2097152000 | bytes 3145728 | tf_op jit(solution)/shard_map/chan_conv/pallas_call | solution.py:302
  9.6 1.0 %collective-permute-done.2.refs_5_ = bf16[144,128]{1,0:T(8,128)(2,1)S(1)} collective-permute-done((bf16[144,128]{1,0:T(8,128)(2,1)}, bf16[144,128]{1,0:T(8,128)(2,1)S(1)}, u32[]{:S(2)}, u32[]{:S(2)}) %collective-permute-start.2) | collective-permute-done | bytes 36896 | tf_op jit(solution)/shard_map/ppermute | solution.py:31
  10.7 0.3 collective-permute-start.3
  10.9 2.2 %chan_conv.5 = (bf16[1024,512]{1,0:T(8,128)(2,1)S(1)}, bf16[1024,512]{1,0:T(8,128)(2,1)S(1)}, f32[8,128]{1,0:T(8,128)S(1)}) custom-call(s32[3]{0:T(128)S(1)} %pad_add_fusion.refs_0_, bf16[4096,512]{1,0:T(8,128)(2,1)S(1)} %copy-done.1, bf16[4,512]{1,0:T(4,128)(2,1)S(1)} %copy-done.5, f32[8,4096]{1,0:T(8,128)S(1)} %get-tuple-element.30.refs_3_.refs_4_, ...), custom_call_target="tpu_custom_call" | custom-call | flops 2097152000 | bytes 3145728 | tf_op jit(solution)/shard_map/chan_conv/pallas_call | solution.py:302
  13.1 0.0 copy-start.3
  13.1 2.2 %chan_conv.6 = (bf16[1024,512]{1,0:T(8,128)(2,1)S(1)}, bf16[1024,512]{1,0:T(8,128)(2,1)S(1)}, f32[8,128]{1,0:T(8,128)S(1)}) custom-call(s32[3]{0:T(128)S(1)} %pad_add_fusion.refs_0_, bf16[4096,512]{1,0:T(8,128)(2,1)S(1)} %copy-done.1, bf16[4,512]{1,0:T(4,128)(2,1)S(1)} %copy-done.5, f32[8,4096]{1,0:T(8,128)S(1)} %get-tuple-element.30.refs_3_.refs_4_, ...), custom_call_target="tpu_custom_call" | custom-call | flops 2097152000 | bytes 3145728 | tf_op jit(solution)/shard_map/chan_conv/pallas_call | solution.py:302
  15.3 0.0 collective-permute-done.3.refs_7_
  15.3 0.0 collective-permute-done.1.refs_3_.refs_6_
  15.3 2.2 %collective-permute-start.4 = (bf16[64,4096]{1,0:T(8,128)(2,1)S(1)}, bf16[64,4096]{1,0:T(8,128)(2,1)S(1)}, u32[]{:S(2)}, u32[]{:S(2)}) collective-permute-start(bf16[64,4096]{1,0:T(8,128)(2,1)S(1)} %collective-permute-done.1.refs_3_.refs_6_), channel_id=1, source_target_pairs={{0,1},{1,0},{2,3},{3,2},{4,5},{5,4},{6,7},{7,6},{8,9},{9,8},{10,11... | collective-permute-start | bytes 1572872 | tf_op jit(solution)/shard_map/ppermute | solution.py:45
  17.5 0.1 collective-permute-start
  17.6 0.4 collective-permute-start.5
  18.0 0.1 collective-permute-start.6
  18.2 2.2 %chan_conv.7 = (bf16[1024,512]{1,0:T(8,128)(2,1)S(1)}, bf16[1024,512]{1,0:T(8,128)(2,1)S(1)}, f32[8,128]{1,0:T(8,128)}) custom-call(s32[3]{0:T(128)S(1)} %pad_add_fusion.refs_0_, bf16[4096,512]{1,0:T(8,128)(2,1)S(1)} %copy-done.1, bf16[4,512]{1,0:T(4,128)(2,1)S(1)} %copy-done.5, f32[8,4096]{1,0:T(8,128)S(1)} %get-tuple-element.30.refs_3_.refs_4_, ...), custom_call_target="tpu_custom_call" | custom-call | flops 2097152000 | bytes 3145728 | tf_op jit(solution)/shard_map/chan_conv/pallas_call | solution.py:302
  20.4 0.0 collective-permute-done.4.refs_4_
  20.4 0.0 collective-permute-done.5.refs_6_
  20.4 0.0 collective-permute-done.refs_2_
  20.4 0.0 collective-permute-done.6.refs_8_
  20.4 2.1 %proj_conv.2.b_ref.refs_1_ = bf16[128,4096]{1,0:T(8,128)(2,1)S(1)} custom-call(s32[3]{0:T(128)S(1)} %pad_add_fusion.refs_0_, bf16[64,4096]{1,0:T(8,128)(2,1)S(1)} %bitcast.13, bf16[64,4096]{1,0:T(8,128)(2,1)S(1)} %collective-permute-done.refs_2_, bf16[64,4096]{1,0:T(8,128)(2,1)S(1)} %collective-permute-done.1.refs_3_.refs_6_, ...), custom_call_target="tpu_custom_call" | custom-call | flops 1048576000 | bytes 1572864 | tf_op jit(solution)/shard_map/proj_conv/pallas_call | solution.py:175
  22.6 0.0 copy-start.2
  22.6 1.3 %states.1 = (bf16[32,128,512]{2,1,0:T(8,128)(2,1)S(1)}, bf16[144,512]{1,0:T(8,128)(2,1)S(1)}) custom-call(bf16[128,4096]{1,0:T(8,128)(2,1)S(1)} %proj_conv.2.b_ref.refs_1_, f32[32,512]{1,0:T(8,128)S(1)} %get-tuple-element.37.tot_ref, bf16[1024,512]{1,0:T(8,128)(2,1)S(1)} %get-tuple-element.39.rest_0_, bf16[1024,512]{1,0:T(8,128)(2,1)S(1)} %get-tuple-element.40.rest_1_, ...), custom_call_target="tpu_custom_call" | custom-call | flops 4194304000 | bytes 8388608 | tf_op jit(solution)/shard_map/states/pallas_call | solution.py:385
  23.9 4.4 %collective-permute-start.7 = (bf16[144,512]{1,0:T(8,128)(2,1)S(1)}, bf16[144,512]{1,0:T(8,128)(2,1)S(1)}, u32[]{:S(2)}, u32[]{:S(2)}) collective-permute-start(bf16[144,512]{1,0:T(8,128)(2,1)S(1)} %get-tuple-element.43.refs_9_.refs_2_.refs_1_), channel_id=1, source_target_pairs={{0,32},{1,225},{2,34},{3,227},{4,36},{5,229},{6,38},{7,231},{8,40}... | collective-permute-start | bytes 442376 | tf_op jit(solution)/shard_map/ppermute | solution.py:41
  28.3 2.1 %proj_conv.3.refs_3_.refs_2_.refs_1_ = bf16[128,4096]{1,0:T(8,128)(2,1)S(1)} custom-call(s32[3]{0:T(128)S(1)} %pad_add_fusion.refs_0_, bf16[64,4096]{1,0:T(8,128)(2,1)S(1)} %bitcast.14, bf16[64,4096]{1,0:T(8,128)(2,1)S(1)} %collective-permute-done.refs_2_, bf16[64,4096]{1,0:T(8,128)(2,1)S(1)} %collective-permute-done.1.refs_3_.refs_6_, ...), custom_call_target="tpu_custom_call" | custom-call | flops 1048576000 | bytes 1572864 | tf_op jit(solution)/shard_map/proj_conv/pallas_call | solution.py:175
  30.4 3.2 %gates.1 = (bf16[4096,512]{1,0:T(8,128)(2,1)S(1)}, bf16[4096,512]{1,0:T(8,128)(2,1)S(1)}) custom-call(bf16[4096,512]{1,0:T(8,128)(2,1)S(1)} %copy-done.2, f32[8,4096]{1,0:T(8,128)S(1)} %get-tuple-element.44.refs_1_, bf16[144,512]{1,0:T(8,128)(2,1)S(1)} %get-tuple-element.43.refs_9_.refs_2_.refs_1_, bf16[128,4096]{1,0:T(8,128)(2,1)S(1)} %proj_conv.3.refs_3_.refs_2_.refs_1_), custom_call_target="tpu_custom_call" | custom-call | flops 3145728000 | bytes 12582912 | tf_op jit(solution)/shard_map/gates/pallas_call | solution.py:478
  33.7 0.6 merge.2.refs_7_.refs_1_
  34.3 1.2 %collective-permute-start.8 = (bf16[144,512]{1,0:T(8,128)(2,1)S(1)}, bf16[144,512]{1,0:T(8,128)(2,1)S(1)}, u32[]{:S(2)}, u32[]{:S(2)}) collective-permute-start(bf16[144,512]{1,0:T(8,128)(2,1)S(1)} %merge.2.refs_7_.refs_1_), channel_id=1, source_target_pairs={{0,64},{1,193},{2,66},{3,195},{4,68},{5,197},{6,70},{7,199},{8,72}... | collective-permute-start | bytes 442376 | tf_op jit(solution)/shard_map/ppermute | solution.py:41
  35.6 2.7 %local.4.refs_8_.refs_4_ = bf16[1024,512]{1,0:T(8,128)(2,1)S(1)} custom-call(bf16[1024,512]{1,0:T(8,128)(2,1)S(1)} %get-tuple-element.47.refs_0_, bf16[128,4096]{1,0:T(8,128)(2,1)S(1)} %proj_conv.2.b_ref.refs_1_, bf16[128,4096]{1,0:T(8,128)(2,1)S(1)} %proj_conv.3.refs_3_.refs_2_.refs_1_, bf16[32,128,512]{2,1,0:T(8,128)(2,1)S(1)} %get-tuple-element.48.refs_3_, ...), custom_call_target="tpu_custom_call" | custom-call | flops 4194304000 | bytes 3145728 | tf_op jit(solution)/shard_map/local/pallas_call | solution.py:445
  38.3 2.7 %local.5.refs_3_.refs_5_ = bf16[1024,512]{1,0:T(8,128)(2,1)S(1)} custom-call(bf16[1024,512]{1,0:T(8,128)(2,1)S(1)} %get-tuple-element.50.refs_0_, bf16[128,4096]{1,0:T(8,128)(2,1)S(1)} %proj_conv.2.b_ref.refs_1_, bf16[128,4096]{1,0:T(8,128)(2,1)S(1)} %proj_conv.3.refs_3_.refs_2_.refs_1_, bf16[32,128,512]{2,1,0:T(8,128)(2,1)S(1)} %get-tuple-element.48.refs_3_, ...), custom_call_target="tpu_custom_call" | custom-call | flops 4194304000 | bytes 3145728 | tf_op jit(solution)/shard_map/local/pallas_call | solution.py:445
  41.0 0.0 collective-permute-done.8.refs_2_.refs_9_
  41.0 0.6 merge.3.refs_7_
  41.6 2.6 %collective-permute-start.9 = (bf16[144,512]{1,0:T(8,128)(2,1)S(1)}, bf16[144,512]{1,0:T(8,128)(2,1)S(1)}, u32[]{:S(2)}, u32[]{:S(2)}) collective-permute-start(bf16[144,512]{1,0:T(8,128)(2,1)S(1)} %merge.3.refs_7_), channel_id=1, source_target_pairs={{0,128},{1,129},{2,130},{3,131},{4,132},{5,133},{6,134},{7,135},{8... | collective-permute-start | bytes 442376 | tf_op jit(solution)/shard_map/ppermute | solution.py:41
  44.2 2.7 %local.7.refs_7_ = bf16[1024,512]{1,0:T(8,128)(2,1)S(1)} custom-call(bf16[1024,512]{1,0:T(8,128)(2,1)S(1)} %get-tuple-element.52.refs_0_, bf16[128,4096]{1,0:T(8,128)(2,1)S(1)} %proj_conv.2.b_ref.refs_1_, bf16[128,4096]{1,0:T(8,128)(2,1)S(1)} %proj_conv.3.refs_3_.refs_2_.refs_1_, bf16[32,128,512]{2,1,0:T(8,128)(2,1)S(1)} %get-tuple-element.48.refs_3_, ...), custom_call_target="tpu_custom_call" | custom-call | flops 4194304000 | bytes 3145728 | tf_op jit(solution)/shard_map/local/pallas_call | solution.py:445
  46.9 2.7 %local.6.refs_6_ = bf16[1024,512]{1,0:T(8,128)(2,1)S(1)} custom-call(bf16[1024,512]{1,0:T(8,128)(2,1)S(1)} %get-tuple-element.51.refs_0_, bf16[128,4096]{1,0:T(8,128)(2,1)S(1)} %proj_conv.2.b_ref.refs_1_, bf16[128,4096]{1,0:T(8,128)(2,1)S(1)} %proj_conv.3.refs_3_.refs_2_.refs_1_, bf16[32,128,512]{2,1,0:T(8,128)(2,1)S(1)} %get-tuple-element.48.refs_3_, ...), custom_call_target="tpu_custom_call" | custom-call | flops 4194304000 | bytes 3145728 | tf_op jit(solution)/shard_map/local/pallas_call | solution.py:445
  49.7 2.2 %collective-permute-done.9.refs_10_ = bf16[144,512]{1,0:T(8,128)(2,1)S(1)} collective-permute-done((bf16[144,512]{1,0:T(8,128)(2,1)S(1)}, bf16[144,512]{1,0:T(8,128)(2,1)S(1)}, u32[]{:S(2)}, u32[]{:S(2)}) %collective-permute-start.9) | collective-permute-done | bytes 147488 | tf_op jit(solution)/shard_map/ppermute | solution.py:41
  51.9 3.6 %carry.1 = (bf16[4096,512]{1,0:T(8,128)(2,1)S(1)}, f32[32,128]{1,0:T(8,128)S(1)}) custom-call(s32[3]{0:T(128)S(1)} %pad_add_fusion.refs_0_, bf16[128,4096]{1,0:T(8,128)(2,1)S(1)} %proj_conv.3.refs_3_.refs_2_.refs_1_, bf16[4096,512]{1,0:T(8,128)(2,1)S(1)} %get-tuple-element.45.refs_2_, bf16[4096,512]{1,0:T(8,128)(2,1)S(1)} %get-tuple-element.46.refs_3_, ...), custom_call_target="tpu_custom_call" | custom-call | flops 8388608000 | bytes 12582912 | tf_op jit(solution)/shard_map/carry/pallas_call | solution.py:537
  55.5 4.0 %collective-permute-start.12 = (f32[32,128]{1,0:T(8,128)S(1)}, f32[32,128]{1,0:T(8,128)S(1)}, u32[]{:S(2)}, u32[]{:S(2)}) collective-permute-start(f32[32,128]{1,0:T(8,128)S(1)} %get-tuple-element.54), channel_id=1, source_target_pairs={{0,3},{1,2},{2,1},{3,0},{4,7},{5,6},{6,5},{7,4},{8,11},{9,10},{10,... | collective-permute-start | bytes 49160 | tf_op jit(solution)/shard_map/ppermute | solution.py:45
  59.5 0.2 collective-permute-start.11
  59.7 0.3 collective-permute-start.10
  60.0 1.2 %collective-permute-done.12 = f32[32,128]{1,0:T(8,128)S(1)} collective-permute-done((f32[32,128]{1,0:T(8,128)S(1)}, f32[32,128]{1,0:T(8,128)S(1)}, u32[]{:S(2)}, u32[]{:S(2)}) %collective-permute-start.12) | collective-permute-done | bytes 16416 | tf_op jit(solution)/shard_map/ppermute | solution.py:45
  61.2 0.9 %collective-permute-done.11 = f32[32,128]{1,0:T(8,128)S(1)} collective-permute-done((f32[32,128]{1,0:T(8,128)S(1)}, f32[32,128]{1,0:T(8,128)S(1)}, u32[]{:S(2)}, u32[]{:S(2)}) %collective-permute-start.11) | collective-permute-done | bytes 16416 | tf_op jit(solution)/shard_map/ppermute | solution.py:45
  62.1 2.7 %norm.1 = bf16[4096,512]{1,0:T(8,128)(2,1)} custom-call(bf16[4096,512]{1,0:T(8,128)(2,1)S(1)} %get-tuple-element.53.refs_0_, f32[32,128]{1,0:T(8,128)S(1)} %add_add_fusion.refs_1_, f32[1,512]{1,0:T(1,128)S(1)} %bitcast.9), custom_call_target="tpu_custom_call" | custom-call | flops 6291456 | bytes 8388608 | tf_op jit(solution)/shard_map/norm/pallas_call | solution.py:572
  (16 shorter events, 0.0 us)
Async XLA Ops:
  0.0 5.2 %copy-start.8 = (f32[8]{0:T(128)S(1)}, f32[8]{0:T(128)}, u32[]{:S(2)}) copy-start(f32[8]{0:T(128)} %param.16) | copy-start | bytes 100
  0.0 5.2 %copy-start.7 = (f32[8]{0:T(128)S(1)}, f32[8]{0:T(128)}, u32[]{:S(2)}) copy-start(f32[8]{0:T(128)} %param.15) | copy-start | bytes 100
  0.0 5.2 %copy-start.6 = (f32[8]{0:T(128)S(1)}, f32[8]{0:T(128)}, u32[]{:S(2)}) copy-start(f32[8]{0:T(128)} %param.14) | copy-start | bytes 100
  0.0 5.2 %copy-start.4 = (f32[4096,8]{0,1:T(8,128)S(1)}, f32[4096,8]{0,1:T(8,128)}, u32[]{:S(2)}) copy-start(f32[4096,8]{0,1:T(8,128)} %param.13) | copy-start | bytes 393220
  0.0 15.3 %collective-permute-start.1 = (bf16[64,4096]{1,0:T(8,128)(2,1)}, bf16[64,4096]{1,0:T(8,128)(2,1)S(1)}, u32[]{:S(2)}, u32[]{:S(2)}) collective-permute-start(bf16[64,4096]{1,0:T(8,128)(2,1)} %bitcast.10), channel_id=1, source_target_pairs={{0,2},{1,3},{2,0},{3,1},{4,6},{5,7},{6,4},{7,5},{8,10},{9,11},{10,... | collective-permute-start | bytes 1572872 | tf_op jit(solution)/shard_map/ppermute | solution.py:45
  3.5 7.1 %collective-permute-start.2 = (bf16[144,128]{1,0:T(8,128)(2,1)}, bf16[144,128]{1,0:T(8,128)(2,1)S(1)}, u32[]{:S(2)}, u32[]{:S(2)}) collective-permute-start(bf16[144,128]{1,0:T(8,128)(2,1)} %tails.1), channel_id=1, source_target_pairs={{0,32},{32,64},{64,96},{96,128},{128,160},{160,192},{192,224},{224... | collective-permute-start | bytes 110600 | tf_op jit(solution)/shard_map/ppermute | solution.py:31
  5.3 2.2 %copy-start.1 = (bf16[4096,512]{1,0:T(8,128)(2,1)S(1)}, bf16[4096,512]{1,0:T(8,128)(2,1)}, u32[]{:S(2)}) copy-start(bf16[4096,512]{1,0:T(8,128)(2,1)} %refs_1_.7) | copy-start | bytes 12582916
  5.3 2.2 %copy-start.5 = (bf16[4,512]{1,0:T(4,128)(2,1)S(1)}, bf16[4,512]{1,0:T(4,128)(2,1)}, u32[]{:S(2)}) copy-start(bf16[4,512]{1,0:T(4,128)(2,1)} %refs_2_.7) | copy-start | bytes 12292
  10.7 4.7 %collective-permute-start.3 = (bf16[144,128]{1,0:T(8,128)(2,1)S(1)}, bf16[144,128]{1,0:T(8,128)(2,1)S(1)}, u32[]{:S(2)}, u32[]{:S(2)}) collective-permute-start(bf16[144,128]{1,0:T(8,128)(2,1)S(1)} %collective-permute-done.2.refs_5_), channel_id=1, source_target_pairs={{0,2},{1,3},{2,0},{3,1},{4,6},{5,7},{6,4},{7,5},{8,10},{9,11},{10,... | collective-permute-start | bytes 110600 | tf_op jit(solution)/shard_map/ppermute | solution.py:45
  13.1 4.4 %copy-start.3 = (bf16[4096,64]{0,1:T(8,128)(2,1)S(1)}, bf16[4096,64]{0,1:T(8,128)(2,1)}, u32[]{:S(2)}) copy-start(bf16[4096,64]{0,1:T(8,128)(2,1)} %param.12) | copy-start | bytes 1572868
  15.3 5.0 %collective-permute-start.4 = (bf16[64,4096]{1,0:T(8,128)(2,1)S(1)}, bf16[64,4096]{1,0:T(8,128)(2,1)S(1)}, u32[]{:S(2)}, u32[]{:S(2)}) collective-permute-start(bf16[64,4096]{1,0:T(8,128)(2,1)S(1)} %collective-permute-done.1.refs_3_.refs_6_), channel_id=1, source_target_pairs={{0,1},{1,0},{2,3},{3,2},{4,5},{5,4},{6,7},{7,6},{8,9},{9,8},{10,11... | collective-permute-start | bytes 1572872 | tf_op jit(solution)/shard_map/ppermute | solution.py:45
  17.5 2.9 %collective-permute-start = (bf16[64,4096]{1,0:T(8,128)(2,1)S(1)}, bf16[64,4096]{1,0:T(8,128)(2,1)S(1)}, u32[]{:S(2)}, u32[]{:S(2)}) collective-permute-start(bf16[64,4096]{1,0:T(8,128)(2,1)S(1)} %bitcast.12), channel_id=1, source_target_pairs={{0,1},{1,0},{2,3},{3,2},{4,5},{5,4},{6,7},{7,6},{8,9},{9,8},{10,11... | collective-permute-start | bytes 1572872 | tf_op jit(solution)/shard_map/ppermute | solution.py:45
  17.6 2.7 %collective-permute-start.5 = (bf16[144,128]{1,0:T(8,128)(2,1)S(1)}, bf16[144,128]{1,0:T(8,128)(2,1)S(1)}, u32[]{:S(2)}, u32[]{:S(2)}) collective-permute-start(bf16[144,128]{1,0:T(8,128)(2,1)S(1)} %collective-permute-done.2.refs_5_), channel_id=1, source_target_pairs={{0,1},{1,0},{2,3},{3,2},{4,5},{5,4},{6,7},{7,6},{8,9},{9,8},{10,11... | collective-permute-start | bytes 110600 | tf_op jit(solution)/shard_map/ppermute | solution.py:45
  18.0 2.4 %collective-permute-start.6 = (bf16[144,128]{1,0:T(8,128)(2,1)S(1)}, bf16[144,128]{1,0:T(8,128)(2,1)S(1)}, u32[]{:S(2)}, u32[]{:S(2)}) collective-permute-start(bf16[144,128]{1,0:T(8,128)(2,1)S(1)} %collective-permute-done.3.refs_7_), channel_id=1, source_target_pairs={{0,1},{1,0},{2,3},{3,2},{4,5},{5,4},{6,7},{7,6},{8,9},{9,8},{10,11... | collective-permute-start | bytes 110600 | tf_op jit(solution)/shard_map/ppermute | solution.py:45
  22.6 7.9 %copy-start.2 = (bf16[4096,512]{1,0:T(8,128)(2,1)S(1)}, bf16[4096,512]{1,0:T(8,128)(2,1)}, u32[]{:S(2)}) copy-start(bf16[4096,512]{1,0:T(8,128)(2,1)} %refs_0_.1) | copy-start | bytes 12582916
  23.9 9.8 %collective-permute-start.7 = (bf16[144,512]{1,0:T(8,128)(2,1)S(1)}, bf16[144,512]{1,0:T(8,128)(2,1)S(1)}, u32[]{:S(2)}, u32[]{:S(2)}) collective-permute-start(bf16[144,512]{1,0:T(8,128)(2,1)S(1)} %get-tuple-element.43.refs_9_.refs_2_.refs_1_), channel_id=1, source_target_pairs={{0,32},{1,225},{2,34},{3,227},{4,36},{5,229},{6,38},{7,231},{8,40}... | collective-permute-start | bytes 442376 | tf_op jit(solution)/shard_map/ppermute | solution.py:41
  34.3 6.7 %collective-permute-start.8 = (bf16[144,512]{1,0:T(8,128)(2,1)S(1)}, bf16[144,512]{1,0:T(8,128)(2,1)S(1)}, u32[]{:S(2)}, u32[]{:S(2)}) collective-permute-start(bf16[144,512]{1,0:T(8,128)(2,1)S(1)} %merge.2.refs_7_.refs_1_), channel_id=1, source_target_pairs={{0,64},{1,193},{2,66},{3,195},{4,68},{5,197},{6,70},{7,199},{8,72}... | collective-permute-start | bytes 442376 | tf_op jit(solution)/shard_map/ppermute | solution.py:41
  41.6 10.2 %collective-permute-start.9 = (bf16[144,512]{1,0:T(8,128)(2,1)S(1)}, bf16[144,512]{1,0:T(8,128)(2,1)S(1)}, u32[]{:S(2)}, u32[]{:S(2)}) collective-permute-start(bf16[144,512]{1,0:T(8,128)(2,1)S(1)} %merge.3.refs_7_), channel_id=1, source_target_pairs={{0,128},{1,129},{2,130},{3,131},{4,132},{5,133},{6,134},{7,135},{8... | collective-permute-start | bytes 442376 | tf_op jit(solution)/shard_map/ppermute | solution.py:41
  51.9 10.2 %copy-start = (f32[512]{0:T(512)S(1)}, f32[512]{0:T(512)}, u32[]{:S(2)}) copy-start(f32[512]{0:T(512)} %param.19) | copy-start | bytes 6148
  55.5 5.7 %collective-permute-start.12 = (f32[32,128]{1,0:T(8,128)S(1)}, f32[32,128]{1,0:T(8,128)S(1)}, u32[]{:S(2)}, u32[]{:S(2)}) collective-permute-start(f32[32,128]{1,0:T(8,128)S(1)} %get-tuple-element.54), channel_id=1, source_target_pairs={{0,3},{1,2},{2,1},{3,0},{4,7},{5,6},{6,5},{7,4},{8,11},{9,10},{10,... | collective-permute-start | bytes 49160 | tf_op jit(solution)/shard_map/ppermute | solution.py:45
  59.5 2.6 %collective-permute-start.11 = (f32[32,128]{1,0:T(8,128)S(1)}, f32[32,128]{1,0:T(8,128)S(1)}, u32[]{:S(2)}, u32[]{:S(2)}) collective-permute-start(f32[32,128]{1,0:T(8,128)S(1)} %get-tuple-element.54), channel_id=1, source_target_pairs={{0,2},{1,3},{2,0},{3,1},{4,6},{5,7},{6,4},{7,5},{8,10},{9,11},{10,... | collective-permute-start | bytes 49160 | tf_op jit(solution)/shard_map/ppermute | solution.py:45
  59.7 2.4 %collective-permute-start.10 = (f32[32,128]{1,0:T(8,128)S(1)}, f32[32,128]{1,0:T(8,128)S(1)}, u32[]{:S(2)}, u32[]{:S(2)}) collective-permute-start(f32[32,128]{1,0:T(8,128)S(1)} %get-tuple-element.54), channel_id=1, source_target_pairs={{0,1},{1,0},{2,3},{3,2},{4,5},{5,4},{6,7},{7,6},{8,9},{9,8},{10,11... | collective-permute-start | bytes 49160 | tf_op jit(solution)/shard_map/ppermute | solution.py:45
